TPU v7x, 32 devices: a whole 2x2x4 slice. The times are simulated.
32 devices in a mesh: section: 2 (over core), group: 4 (over y, x), dp: 4 (over z).
Axes of the slice: x: 2, y: 2, z: 4, core: 2. Of those that a mesh axis runs over, the one named last changes fastest.
Arguments:
- tokens: bfloat16 [2, 4096, 768], P(None, ('group', 'dp')), may hold values from -6 to 6
- cotangent: bfloat16 [2, 4096, 768], P(None, ('group', 'dp')), may hold values from -6 to 6
- lengths: int32 [2, 16, 3], P(None, ('group', 'dp')), may hold values from 1 to 128, 256 in all within a row
- attend_gain: bfloat16 [2, 768], P('section', 'dp'), may hold values from 0.5 to 1.5
- attend_bias: bfloat16 [2, 768], P('section', 'dp'), may hold values from -1.5 to 1.5
- qkv_weight: bfloat16 [2, 768, 2304], P('section', 'dp'), may hold values from -0.21875 to 0.21875
- out_weight: bfloat16 [2, 768, 768], P('section', 'dp'), may hold values from -0.875 to 0.875
- feed_gain: bfloat16 [2, 768], P('section', 'dp'), may hold values from 0.5 to 1.5
- feed_bias: bfloat16 [2, 768], P('section', 'dp'), may hold values from -1.5 to 1.5
- up_weight: bfloat16 [2, 768, 3072], P('section', 'dp'), may hold values from -0.21875 to 0.21875
- down_weight: bfloat16 [2, 3072, 768], P('section', 'dp'), may hold values from -0.109375 to 0.109375
Outputs:
- layer_out: bfloat16 [2, 2, 4096, 768], P('section', None, ('group', 'dp'))
- input_grad: bfloat16 [2, 2, 4096, 768], P('section', None, ('group', 'dp'))
- attend_gain_grad: float32 [2, 768], P('section', 'dp')
- attend_bias_grad: float32 [2, 768], P('section', 'dp')
- qkv_grad: float32 [2, 768, 2304], P('section', 'dp')
- out_grad: float32 [2, 768, 768], P('section', 'dp')
- feed_gain_grad: float32 [2, 768], P('section', 'dp')
- feed_bias_grad: float32 [2, 768], P('section', 'dp')
- up_grad: float32 [2, 768, 3072], P('section', 'dp')
- down_grad: float32 [2, 3072, 768], P('section', 'dp')
Inputs may be any that keep to these rules, and one draw needn't show every extreme that they name: The 3 lengths of one device's block of a micro-batch add up to 256; the longest sequence of every block has 128 tokens.
All inputs are finite; a program needn't handle non-finite values.
Results may differ from a plain program's by a relative error of at most 0.02.
Values may be sent and summed in bfloat16 or wider, within the bound.
No kernel may reach another device: no remote copies, remote signals or barrier semaphores. Data moves between devices by JAX's collectives and lax.ppermute only.
A program may use at most 192 MiB of HBM per device.

v0:
```python
import jax
import jax.numpy as jnp
from jax import lax
from jax.sharding import PartitionSpec as P

HEAD_DIM = 64


masked_score = -1000000000.0


def from_behind(block, axis, distance):
    devices = range(lax.axis_size(axis))
    route = [(i - distance, i) for i in devices if i - distance in devices]
    return lax.ppermute(block, axis, route)


def rope_tables(lengths_row, tok):
    bounds = jnp.cumsum(lengths_row, dtype=jnp.int32)
    places = jnp.arange(tok, dtype=jnp.int32)
    segment = jnp.sum((places[:, None] >= bounds[None, :-1]).astype(jnp.int32), axis=1)
    starts = bounds - lengths_row
    picks = jnp.arange(lengths_row.shape[0], dtype=jnp.int32)
    begin = jnp.sum(jnp.where(segment[:, None] == picks[None, :], starts[None, :], 0), axis=1)
    offset = (places - begin).astype(jnp.float32)
    half = HEAD_DIM // 2
    freqs = 10000.0 ** (-jnp.arange(half, dtype=jnp.float32) / half)
    angles = offset[:, None] * freqs[None, :]
    return (jnp.cos(angles), jnp.sin(angles), segment[:, None] == segment[None, :])


def layer_norm(x, gain, bias):
    center = x - jnp.mean(x, axis=-1, keepdims=True)
    spread = jnp.mean(center * center, axis=-1, keepdims=True)
    return center * lax.rsqrt(spread + 1e-05) * gain + bias


def rotate(heads_in, cosine, sine):
    half = heads_in.shape[-1] // 2
    first = heads_in[..., :half]
    second = heads_in[..., half:]
    cosv = cosine[:, None, :]
    sinv = sine[:, None, :]
    return jnp.concatenate([first * cosv - second * sinv, second * cosv + first * sinv], axis=-1)


def inner(left, right):
    return lax.dot_general(
        left, right, (((0,), (0,)), ((), ())), preferred_element_type=jnp.float32
    )


def times_transposed(left, weight):
    return lax.dot_general(
        left, weight, (((1,), (1,)), ((), ())), preferred_element_type=jnp.float32
    )


def layer_parts(x, weights, tables):
    gain_one, bias_one, qkv_w, out_w, gain_two, bias_two, up_w, down_w = weights
    cosine, sine, same = tables
    tok, width = x.shape
    heads = width // HEAD_DIM
    normed = layer_norm(x, gain_one.astype(jnp.float32), bias_one.astype(jnp.float32)).astype(
        jnp.bfloat16
    )
    qkv = jnp.dot(normed, qkv_w, preferred_element_type=jnp.float32).reshape(
        tok, 3, heads, HEAD_DIM
    )
    query = rotate(qkv[:, 0], cosine, sine).astype(jnp.bfloat16)
    key = rotate(qkv[:, 1], cosine, sine).astype(jnp.bfloat16)
    value = qkv[:, 2].astype(jnp.bfloat16)
    scores = jnp.einsum(
        "qhd,khd->hqk", query, key, preferred_element_type=jnp.float32
    ) * HEAD_DIM ** (-0.5)
    scores = jnp.where(same[None], scores, masked_score)
    peak = jnp.max(scores, axis=-1, keepdims=True)
    expd = jnp.exp(scores - peak)
    probs = expd / jnp.sum(expd, axis=-1, keepdims=True)
    probs_low = probs.astype(jnp.bfloat16)
    mixed = jnp.einsum("hqk,khd->qhd", probs_low, value, preferred_element_type=jnp.float32)
    mixed = mixed.reshape(tok, width).astype(jnp.bfloat16)
    resid = x + jnp.dot(mixed, out_w, preferred_element_type=jnp.float32)
    normed_two = layer_norm(
        resid, gain_two.astype(jnp.float32), bias_two.astype(jnp.float32)
    ).astype(jnp.bfloat16)
    upward = jnp.dot(normed_two, up_w, preferred_element_type=jnp.float32)
    active = jax.nn.gelu(upward, approximate=False).astype(jnp.bfloat16)
    return (normed, query, key, value, probs, probs_low, mixed, resid, normed_two, upward, active)


def layer_forward(x, weights, tables):
    saved = layer_parts(x, weights, tables)
    return saved[7] + jnp.dot(saved[10], weights[7], preferred_element_type=jnp.float32)


def layer_backward(x, upstream, weights, tables):
    gain_one, bias_one, qkv_w, out_w, gain_two, bias_two, up_w, down_w = weights
    cosine, sine, same = tables
    normed, query, key, value, probs, probs_low, mixed, resid, normed_two, upward, active = (
        layer_parts(x, weights, tables)
    )
    tok, width = x.shape
    heads = width // HEAD_DIM
    scale = HEAD_DIM ** (-0.5)
    d_branch_ff = upstream.astype(jnp.bfloat16)
    g_down = inner(active, d_branch_ff)
    d_active = times_transposed(d_branch_ff, down_w)
    _, gelu_pull = jax.vjp(lambda u: jax.nn.gelu(u, approximate=False), upward)
    d_up = gelu_pull(d_active)[0].astype(jnp.bfloat16)
    g_up = inner(normed_two, d_up)
    d_normed_two = times_transposed(d_up, up_w)
    _, norm_pull_two = jax.vjp(
        layer_norm, resid, gain_two.astype(jnp.float32), bias_two.astype(jnp.float32)
    )
    d_resid_part, g_gain_two, g_bias_two = norm_pull_two(d_normed_two)
    d_resid = upstream + d_resid_part
    d_branch = d_resid.astype(jnp.bfloat16)
    g_out = inner(mixed, d_branch)
    d_mixed = times_transposed(d_branch, out_w).astype(jnp.bfloat16).reshape(tok, heads, HEAD_DIM)
    d_value = jnp.einsum("hqk,qhd->khd", probs_low, d_mixed, preferred_element_type=jnp.float32)
    d_probs = jnp.einsum("qhd,khd->hqk", d_mixed, value, preferred_element_type=jnp.float32)
    d_scores = probs * (d_probs - jnp.sum(d_probs * probs, axis=-1, keepdims=True))
    d_scores = d_scores.astype(jnp.bfloat16)
    d_query = jnp.einsum("hqk,khd->qhd", d_scores, key, preferred_element_type=jnp.float32) * scale
    d_key = jnp.einsum("hqk,qhd->khd", d_scores, query, preferred_element_type=jnp.float32) * scale
    d_qkv = jnp.stack(
        [rotate(d_query, cosine, -sine), rotate(d_key, cosine, -sine), d_value], axis=1
    )
    d_qkv = d_qkv.reshape(tok, 3 * width).astype(jnp.bfloat16)
    g_qkv = inner(normed, d_qkv)
    d_normed = times_transposed(d_qkv, qkv_w)
    _, norm_pull_one = jax.vjp(
        layer_norm, x, gain_one.astype(jnp.float32), bias_one.astype(jnp.float32)
    )
    d_x_part, g_gain_one, g_bias_one = norm_pull_one(d_normed)
    d_x = d_resid + d_x_part
    return (d_x, (g_gain_one, g_bias_one, g_qkv, g_out, g_gain_two, g_bias_two, g_up, g_down))


def pick_tables(first, early, late):
    return tuple((jnp.where(first, a, b) for a, b in zip(early, late)))


def on_device(
    tokens,
    cotangent,
    lengths,
    attend_gain,
    attend_bias,
    qkv_weight,
    out_weight,
    feed_gain,
    feed_bias,
    up_weight,
    down_weight,
):
    first = lax.axis_index("section") == 0
    micro = tokens.shape[0]
    tok = tokens.shape[1]
    width = tokens.shape[2]
    shards = (
        attend_gain[0],
        attend_bias[0],
        qkv_weight[0],
        out_weight[0],
        feed_gain[0],
        feed_bias[0],
        up_weight[0],
        down_weight[0],
    )
    weights = (
        lax.all_gather(shards[0], "dp", axis=0, tiled=True),
        lax.all_gather(shards[1], "dp", axis=0, tiled=True),
        lax.all_gather(shards[2], "dp", axis=0, tiled=True),
        lax.all_gather(shards[3], "dp", axis=0, tiled=True),
        lax.all_gather(shards[4], "dp", axis=0, tiled=True),
        lax.all_gather(shards[5], "dp", axis=0, tiled=True),
        lax.all_gather(shards[6], "dp", axis=0, tiled=True),
        lax.all_gather(shards[7], "dp", axis=0, tiled=True),
    )
    tables = [rope_tables(lengths[m, 0], tok) for m in range(micro)]
    received = jnp.zeros((tok, width), jnp.bfloat16)
    inputs = []
    outputs = []
    for tick in range(micro + 1):
        mine = min(tick, micro - 1)
        theirs = max(tick - 1, 0)
        source = jnp.where(first, tokens[mine], received).astype(jnp.float32)
        tabs = pick_tables(first, tables[mine], tables[theirs])
        result = layer_forward(source, weights, tabs).astype(jnp.bfloat16)
        inputs.append(source)
        outputs.append(result)
        if tick < micro:
            received = from_behind(result, "section", 1)
    kept = [jnp.where(first, inputs[m], inputs[m + 1]) for m in range(micro)]
    layer_out = jnp.stack([jnp.where(first, outputs[m], outputs[m + 1]) for m in range(micro)])
    totals = tuple((jnp.zeros(w.shape, jnp.float32) for w in weights))
    received = jnp.zeros((tok, width), jnp.bfloat16)
    sent_back = []
    for tick in range(micro + 1):
        late = min(micro - tick, micro - 1)
        early = max(micro - 1 - tick, 0)
        valid = jnp.where(first, float(tick >= 1), float(tick < micro))
        upstream = jnp.where(first, received, cotangent[early]).astype(jnp.float32)
        source = jnp.where(first, kept[late], kept[early])
        tabs = pick_tables(first, tables[late], tables[early])
        d_x, grads = layer_backward(source, upstream, weights, tabs)
        totals = tuple((total + valid * grad for total, grad in zip(totals, grads)))
        d_low = d_x.astype(jnp.bfloat16)
        sent_back.append(d_low)
        if tick < micro:
            received = from_behind(d_low, "section", -1)
    input_grad = jnp.stack(
        [jnp.where(first, sent_back[micro - m], sent_back[micro - 1 - m]) for m in range(micro)]
    )
    rows = (
        lax.psum_scatter(
            totals[0].astype(jnp.bfloat16), "dp", scatter_dimension=0, tiled=True
        ).astype(jnp.float32),
        lax.psum_scatter(
            totals[1].astype(jnp.bfloat16), "dp", scatter_dimension=0, tiled=True
        ).astype(jnp.float32),
        lax.psum_scatter(
            totals[2].astype(jnp.bfloat16), "dp", scatter_dimension=0, tiled=True
        ).astype(jnp.float32),
        lax.psum_scatter(
            totals[3].astype(jnp.bfloat16), "dp", scatter_dimension=0, tiled=True
        ).astype(jnp.float32),
        lax.psum_scatter(
            totals[4].astype(jnp.bfloat16), "dp", scatter_dimension=0, tiled=True
        ).astype(jnp.float32),
        lax.psum_scatter(
            totals[5].astype(jnp.bfloat16), "dp", scatter_dimension=0, tiled=True
        ).astype(jnp.float32),
        lax.psum_scatter(
            totals[6].astype(jnp.bfloat16), "dp", scatter_dimension=0, tiled=True
        ).astype(jnp.float32),
        lax.psum_scatter(
            totals[7].astype(jnp.bfloat16), "dp", scatter_dimension=0, tiled=True
        ).astype(jnp.float32),
    )
    summed = (
        lax.psum(rows[0].astype(jnp.bfloat16), "group").astype(jnp.float32),
        lax.psum(rows[1].astype(jnp.bfloat16), "group").astype(jnp.float32),
        lax.psum(rows[2].astype(jnp.bfloat16), "group").astype(jnp.float32),
        lax.psum(rows[3].astype(jnp.bfloat16), "group").astype(jnp.float32),
        lax.psum(rows[4].astype(jnp.bfloat16), "group").astype(jnp.float32),
        lax.psum(rows[5].astype(jnp.bfloat16), "group").astype(jnp.float32),
        lax.psum(rows[6].astype(jnp.bfloat16), "group").astype(jnp.float32),
        lax.psum(rows[7].astype(jnp.bfloat16), "group").astype(jnp.float32),
    )
    return (
        layer_out[None],
        input_grad[None],
        summed[0][None],
        summed[1][None],
        summed[2][None],
        summed[3][None],
        summed[4][None],
        summed[5][None],
        summed[6][None],
        summed[7][None],
    )


def solution(mesh):
    placed = (
        P(None, ("group", "dp"), None),
        P(None, ("group", "dp"), None),
        P(None, ("group", "dp"), None),
        P("section", "dp"),
        P("section", "dp"),
        P("section", "dp", None),
        P("section", "dp", None),
        P("section", "dp"),
        P("section", "dp"),
        P("section", "dp", None),
        P("section", "dp", None),
    )
    return jax.shard_map(
        on_device,
        mesh=mesh,
        in_specs=placed,
        out_specs=(
            P("section", None, ("group", "dp"), None),
            P("section", None, ("group", "dp"), None),
            P("section", "dp"),
            P("section", "dp"),
            P("section", "dp", None),
            P("section", "dp", None),
            P("section", "dp"),
            P("section", "dp"),
            P("section", "dp", None),
            P("section", "dp", None),
        ),
        check_vma=False,
    )
```

profile of v0, /device:TPU:0, one launch (start us, length us, event | category | flops | bytes accessed | tf_op | source)
XLA Modules:
  0.0 874.2 jit_solution(11148271096684498808)
XLA Ops:
  12.4 13.9 %all-reduce.9 = (bf16[768]{0:T(1024)(128)(2,1)S(1)}, bf16[768]{0:T(1024)(128)(2,1)S(1)}, bf16[768]{0:T(1024)(128)(2,1)S(1)}, bf16[768]{0:T(1024)(128)(2,1)S(1)}) all-reduce(bf16[768]{0:T(1024)(128)(2,1)S(1)} %dynamic-update-slice.1, bf16[768]{0:T(1024)(128)(2,1)S(1)} %dynamic-update-slice, ...), channel_id=3, replica_groups=mesh['section'=2,'group'=4,'dp'=4] {'dp'}, use_global_device_ids=true, to_apply=%add.1 | all-reduce | flops 3072 | bytes 12288
  29.2 53.3 %all-gather.13.cloned.1.call-done = bf16[1,768,2304]{2,1,0:T(8,128)(2,1)} async-done(((bf16[1,192,2304]{2,1,0:T(8,128)(2,1)}), bf16[1,768,2304]{2,1,0:T(8,128)(2,1)}) %all-gather.13.cloned.1.call-update) | async-done | bytes 3538960 | tf_op jit(solution)/shard_map/all_gather | solution.py:175
  82.5 5.8 copy.96
  94.2 18.9 %all-gather.15.cloned.1.call-done = bf16[1,768,768]{2,1,0:T(8,128)(2,1)} async-done(((bf16[1,192,768]{2,1,0:T(8,128)(2,1)}), bf16[1,768,768]{2,1,0:T(8,128)(2,1)}) %all-gather.15.cloned.1.call-update) | async-done | bytes 1179664 | tf_op jit(solution)/shard_map/all_gather | solution.py:176
  115.2 88.0 %all-gather.19.cloned.1.call-done = bf16[1,3072,768]{2,1,0:T(8,128)(2,1)} async-done(((bf16[1,768,768]{2,1,0:T(8,128)(2,1)}), bf16[1,3072,768]{2,1,0:T(8,128)(2,1)}) %all-gather.19.cloned.1.call-update) | async-done | bytes 4718608 | tf_op jit(solution)/shard_map/all_gather | solution.py:180
  203.3 89.3 %all-gather.17.cloned.1.call-done = bf16[1,768,3072]{2,1,0:T(8,128)(2,1)} async-done(((bf16[1,192,3072]{2,1,0:T(8,128)(2,1)}), bf16[1,768,3072]{2,1,0:T(8,128)(2,1)}) %all-gather.17.cloned.1.call-update) | async-done | bytes 4718608 | tf_op jit(solution)/shard_map/all_gather | solution.py:179
  292.6 12.8 %fusion.287 = bf16[256,768]{1,0:T(8,128)(2,1)S(1)} fusion(f32[256,768]{1,0:T(8,128)S(1)} %get-tuple-element.155, bf16[1,3072,768]{2,1,0:T(8,128)(2,1)} %all-gather.19.cloned.1.call-done, bf16[1,768,3072]{2,1,0:T(8,128)(2,1)} %all-gather.17.cloned.1.call-done, f32[768]{0:T(1024)S(1)} %convert_element_type.462, f32[768]{0:T(1024)S(1)} %convert_element_type.461, ...), kind=kOutput, calls=%fused_computation.351 | convolution fusion | flops 2468413440 | bytes 10625024 | tf_op jit(solution)/shard_map/dot_general | solution.py:94
  317.8 12.8 %fusion.280 = bf16[256,768]{1,0:T(8,128)(2,1)S(1)} fusion(f32[256,768]{1,0:T(8,128)S(1)} %get-tuple-element.159, bf16[1,3072,768]{2,1,0:T(8,128)(2,1)} %all-gather.19.cloned.1.call-done, bf16[1,768,3072]{2,1,0:T(8,128)(2,1)} %all-gather.17.cloned.1.call-done, f32[768]{0:T(1024)S(1)} %convert_element_type.462, f32[768]{0:T(1024)S(1)} %convert_element_type.461, ...), kind=kOutput, calls=%fused_computation.350 | convolution fusion | flops 2468413440 | bytes 10625024 | tf_op jit(solution)/shard_map/dot_general | solution.py:94
  354.2 9.6 %add_convert_fusion.5 = bf16[256,3072]{1,0:T(8,128)(2,1)S(1)} fusion(bf16[1,3072,768]{2,1,0:T(8,128)(2,1)S(1)} %bitcast.436, f32[256,3072]{1,0:T(8,128)S(1)} %fusion.28, bf16[2,256,768]{2,1,0:T(8,128)(2,1)S(1)} %copy-done.45, pred[]{:T(512)S(6)} %eq.69), kind=kOutput, calls=%fused_computation.112 | convolution fusion | flops 1264779264 | bytes 9830401 | tf_op jit(solution)/shard_map/dot_general | solution.py:54
  431.3 9.3 %add_convert_fusion.4 = bf16[256,3072]{1,0:T(8,128)(2,1)S(1)} fusion(bf16[256,768]{1,0:T(8,128)(2,1)S(1)} %bitcast_select_fusion.1, bf16[1,3072,768]{2,1,0:T(8,128)(2,1)S(1)} %bitcast.438, f32[256,3072]{1,0:T(8,128)S(1)} %fusion.24), kind=kOutput, calls=%fused_computation.95 | convolution fusion | flops 1264582656 | bytes 9830400 | tf_op jit(solution)/shard_map/dot_general | solution.py:54
  468.4 9.1 %add_convert_fusion.3 = bf16[256,3072]{1,0:T(8,128)(2,1)S(1)} fusion(bf16[256,768]{1,0:T(8,128)(2,1)S(1)} %bitcast_select_fusion, bf16[1,3072,768]{2,1,0:T(8,128)(2,1)S(1)} %bitcast.440, f32[256,3072]{1,0:T(8,128)S(1)} %copy-done.180), kind=kOutput, calls=%fused_computation.78 | convolution fusion | flops 1264582656 | bytes 9830400 | tf_op jit(solution)/shard_map/dot_general | solution.py:54
  481.8 5.1 multiply_reduce_fusion
  507.6 6.2 add_convert_fusion.1
  514.9 9.7 %fusion.127 = f32[3072,768]{1,0:T(8,128)S(1)} fusion(f32[256,3072]{1,0:T(8,128)} %copy-done.179, bf16[2,256,768]{2,1,0:T(8,128)(2,1)S(1)} %copy-done.49, pred[]{:T(512)S(6)} %eq.69), kind=kOutput, calls=%fused_computation.191 | convolution fusion | flops 1259274240 | bytes 12976129 | tf_op jit(solution)/shard_map/dot_general | solution.py:48
  524.7 9.9 %fusion.128 = f32[3072,768]{1,0:T(8,128)} fusion(bf16[256,768]{1,0:T(8,128)(2,1)S(1)} %copy-done.31, f32[256,3072]{1,0:T(8,128)S(1)} %copy-done.183), kind=kOutput, calls=%fused_computation.192 | convolution fusion | flops 1259077632 | bytes 12976128 | tf_op jit(solution)/shard_map/dot_general | solution.py:48
  534.6 11.8 %add_convert_fusion = bf16[3072,768]{1,0:T(8,128)(2,1)} fusion(f32[3072,768]{1,0:T(8,128)} %fusion.128, f32[3072,768]{1,0:T(8,128)S(1)} %fusion.127, bf16[256,768]{1,0:T(8,128)(2,1)S(1)} %copy-done.37, f32[]{:T(128)S(6)} %select_n.198, f32[]{:T(128)S(6)} %select_n.197, f32[256,3072]{1,0:T(8,128)S(1)} %copy-done.181), kind=kOutput, calls=%fused_computation.6 | convolution fusion | flops 1270874112 | bytes 27131912 | tf_op jit(solution)/shard_map/dot_general | solution.py:48
  557.5 27.9 %reduce-scatter.5.cloned.1.call-done = bf16[192,2304]{1,0:T(8,128)(2,1)} async-done(((bf16[768,2304]{1,0:T(8,128)(2,1)}), bf16[192,2304]{1,0:T(8,128)(2,1)}) %reduce-scatter.5.cloned.1.call-update) | async-done | bytes 884752 | tf_op jit(solution)/shard_map/reduce_scatter | solution.py:224
  585.4 87.9 %reduce-scatter.9.cloned.1.call-done = bf16[192,3072]{1,0:T(8,128)(2,1)} async-done(((bf16[768,3072]{1,0:T(8,128)(2,1)}), bf16[192,3072]{1,0:T(8,128)(2,1)}) %reduce-scatter.9.cloned.1.call-update) | async-done | bytes 1179664 | tf_op jit(solution)/shard_map/reduce_scatter | solution.py:236
  673.3 88.1 %reduce-scatter.11.cloned.1.call-done = bf16[768,768]{1,0:T(8,128)(2,1)} async-done(((bf16[3072,768]{1,0:T(8,128)(2,1)}), bf16[768,768]{1,0:T(8,128)(2,1)}) %reduce-scatter.11.cloned.1.call-update) | async-done | bytes 1179664 | tf_op jit(solution)/shard_map/reduce_scatter | solution.py:239
  761.5 13.7 %fusion.314 = bf16[1,256,768]{2,1,0:T(8,128)(2,1)} fusion(bf16[256,768]{1,0:T(8,128)(2,1)} %copy-done.88, f32[256,768]{1,0:T(8,128)S(1)} %copy-done.40, bf16[1,3072,768]{2,1,0:T(8,128)(2,1)} %all-gather.19.cloned.1.call-done, bf16[1,768,3072]{2,1,0:T(8,128)(2,1)} %all-gather.17.cloned.1.call-done, f32[768]{0:T(1024)S(1)} %convert_element_type.462, ...), kind=kOutput, calls=%fused_computation.378 | convolution fusion | flops 2468610048 | bytes 11018241 | tf_op jit(solution)/shard_map/dot_general | solution.py:94
  777.3 4.8 multiply_reduce_fusion.6
  782.2 11.1 %all-reduce.8 = (bf16[768]{0:T(1024)(128)(2,1)S(1)}, bf16[768]{0:T(1024)(128)(2,1)S(1)}, bf16[768]{0:T(1024)(128)(2,1)S(1)}, bf16[768]{0:T(1024)(128)(2,1)S(1)}) all-reduce(bf16[768]{0:T(1024)(128)(2,1)S(1)} %add_convert_fusion.46, ...), channel_id=10, replica_groups=mesh['section'=2,'group'=4,'dp'=4] {'dp'}, use_global_device_ids=true, to_apply=%region_60.61.clone | all-reduce | flops 3072 | bytes 12288
  793.6 10.2 %all-reduce.10 = (bf16[1,192]{1,0:T(2,128)(2,1)S(1)}, bf16[1,192]{1,0:T(2,128)(2,1)S(1)}, bf16[1,192]{1,0:T(2,128)(2,1)S(1)}, bf16[1,192]{1,0:T(2,128)(2,1)S(1)}) all-reduce(bf16[1,192]{1,0:T(2,128)(2,1)S(1)} %broadcast_in_dim.143, ...), channel_id=1, replica_groups=mesh['section'=2,'group'=4,'dp'=4] {'group'}, use_global_device_ids=true, to_apply=%region_61.62 | all-reduce | flops 768 | bytes 3072 | tf_op jit(solution)/shard_map/psum | solution.py:244
  809.6 50.2 %all-reduce.14.cloned.1.call-done = (bf16[1,192,2304]{2,1,0:T(8,128)(2,1)}, bf16[1,192,768]{2,1,0:T(8,128)(2,1)}, bf16[1,192,3072]{2,1,0:T(8,128)(2,1)}, bf16[1,768,768]{2,1,0:T(8,128)(2,1)}) async-done(((bf16[1,192,2304]{2,1,0:T(8,128)(2,1)}, bf16[1,192,768]{2,1,0:T(8,128)(2,1)}, bf16[1,192,3072]{2,1,0:T(8,128)(2,1)}, bf16[1,768,768]{2,1,0:T(8,128)(2,1)}), (bf16[1,192,2304]{2,1,0:T(8,128)(2,1)}, ...) | async-done | bytes 3538960 | tf_op jit(solution)/shard_map/psum | solution.py:246
  (640 shorter events, 196.7 us)
Async XLA Ops:
  7.3 75.3 %all-gather.13.cloned.1.call-start = ((), (), s32[]{:S(2)}) async-start(), calls=%async_computation.8 | async-start | bytes 4423680 | tf_op jit(solution)/shard_map/all_gather | solution.py:175
  8.0 105.1 %all-gather.15.cloned.1.call-start = ((), (), s32[]{:S(2)}) async-start(), calls=%async_computation.9 | async-start | bytes 1474560 | tf_op jit(solution)/shard_map/all_gather | solution.py:176
  8.7 194.5 %all-gather.19.cloned.1.call-start = ((), (), s32[]{:S(2)}) async-start(), calls=%async_computation.11 | async-start | bytes 5898240 | tf_op jit(solution)/shard_map/all_gather | solution.py:180
  9.5 283.1 %all-gather.17.cloned.1.call-start = ((), (), s32[]{:S(2)}) async-start(), calls=%async_computation.10 | async-start | bytes 5898240 | tf_op jit(solution)/shard_map/all_gather | solution.py:179
  10.0 547.4 %reduce-scatter.7.cloned.1.call-start = ((), (), s32[]{:S(2)}) async-start(), calls=%async_computation.5 | async-start | bytes 1474560 | tf_op jit(solution)/shard_map/reduce_scatter | solution.py:227
  28.2 64.5 %copy-start.107 = (pred[256,256]{0,1:T(8,128)(4,1)}, pred[256,256]{0,1:T(8,128)(4,1)S(1)}, u32[]{:S(2)}) copy-start(pred[256,256]{0,1:T(8,128)(4,1)S(1)} %get-tuple-element.145) | copy-start | bytes 196612
  28.2 285.5 %copy-start.108 = (pred[256,256]{0,1:T(8,128)(4,1)}, pred[256,256]{0,1:T(8,128)(4,1)S(1)}, u32[]{:S(2)}) copy-start(pred[256,256]{0,1:T(8,128)(4,1)S(1)} %get-tuple-element.144) | copy-start | bytes 196612
  29.2 62.6 %copy-start.78 = (f32[256,32]{0,1:T(8,128)}, f32[256,32]{0,1:T(8,128)S(1)}, u32[]{:S(2)}) copy-start(f32[256,32]{0,1:T(8,128)S(1)} %get-tuple-element.141) | copy-start | bytes 98308
  29.2 62.6 %copy-start.94 = (f32[256,32]{0,1:T(8,128)}, f32[256,32]{0,1:T(8,128)S(1)}, u32[]{:S(2)}) copy-start(f32[256,32]{0,1:T(8,128)S(1)} %get-tuple-element.140) | copy-start | bytes 98308
  29.2 283.6 %copy-start.81 = (f32[256,32]{0,1:T(8,128)}, f32[256,32]{0,1:T(8,128)S(1)}, u32[]{:S(2)}) copy-start(f32[256,32]{0,1:T(8,128)S(1)} %get-tuple-element.135) | copy-start | bytes 98308
  29.2 283.6 %copy-start.96 = (f32[256,32]{0,1:T(8,128)}, f32[256,32]{0,1:T(8,128)S(1)}, u32[]{:S(2)}) copy-start(f32[256,32]{0,1:T(8,128)S(1)} %get-tuple-element.136) | copy-start | bytes 98308
  305.4 3.2 collective-permute-start
  330.6 3.8 collective-permute-start.1
  335.3 90.7 %copy-start.5 = (bf16[256,768]{1,0:T(8,128)(2,1)}, bf16[256,768]{1,0:T(8,128)(2,1)S(1)}, u32[]{:S(2)}) copy-start(bf16[256,768]{1,0:T(8,128)(2,1)S(1)} %get-tuple-element.61) | copy-start | bytes 1179652
  404.2 26.0 %collective-permute-start.2 = (bf16[256,768]{1,0:T(8,128)(2,1)}, bf16[256,768]{1,0:T(8,128)(2,1)}, u32[]{:S(2)}, u32[]{:S(2)}) collective-permute-start(bf16[256,768]{1,0:T(8,128)(2,1)} %add_convert_fusion.13), channel_id=1, source_target_pairs={{16,0},{17,1},{18,2},{19,3},{20,4},{21,5},{22,6},{23,7},{24,8},{25... | collective-permute-start | bytes 1179656 | tf_op jit(solution)/shard_map/ppermute | solution.py:15
  462.5 5.8 collective-permute-start.3
  488.5 96.9 %reduce-scatter.5.cloned.1.call-start = ((), (), s32[]{:S(2)}) async-start(), calls=%async_computation.4 | async-start | bytes 4423680 | tf_op jit(solution)/shard_map/reduce_scatter | solution.py:224
  501.7 171.6 %reduce-scatter.9.cloned.1.call-start = ((), (), s32[]{:S(2)}) async-start(), calls=%async_computation.6 | async-start | bytes 5898240 | tf_op jit(solution)/shard_map/reduce_scatter | solution.py:236
  513.8 247.6 %reduce-scatter.11.cloned.1.call-start = ((), (), s32[]{:S(2)}) async-start(), calls=%async_computation.7 | async-start | bytes 5898240 | tf_op jit(solution)/shard_map/reduce_scatter | solution.py:239
  546.4 313.3 %all-reduce.14.cloned.1.call-start = ((), (), s32[]{:S(2)}) async-start(), calls=%async_computation.12 | async-start | bytes 7077888 | tf_op jit(solution)/shard_map/psum | solution.py:246
  555.8 205.6 %copy-start.154 = (f32[256]{0:T(256)}, f32[256]{0:T(256)S(1)}, u32[]{:S(2)}) copy-start(f32[256]{0:T(256)S(1)} %broadcast_multiply_fusion.6) | copy-start | bytes 3076
  556.9 204.5 %copy-start.40 = (f32[256,768]{1,0:T(8,128)S(1)}, f32[256,768]{1,0:T(8,128)}, u32[]{:S(2)}) copy-start(f32[256,768]{1,0:T(8,128)} %copy-done.39) | copy-start | bytes 2359300
  777.3 31.0 %copy-start.23 = (f32[256,768]{1,0:T(8,128)S(1)}, f32[256,768]{1,0:T(8,128)}, u32[]{:S(2)}) copy-start(f32[256,768]{1,0:T(8,128)} %copy-done.22) | copy-start | bytes 2359300
  777.3 31.0 %copy-start.38 = (bf16[256,768]{1,0:T(8,128)(2,1)S(1)}, bf16[256,768]{1,0:T(8,128)(2,1)}, u32[]{:S(2)}) copy-start(bf16[256,768]{1,0:T(8,128)(2,1)} %copy-done.36) | copy-start | bytes 1179652
  (189 other events, 865.9 us)
Sparse Core Ops, SparseCore 0:
  9.7 72.8 all-gather.12
  84.1 29.0 all-gather.14
  114.7 88.5 all-gather.18
  204.7 87.8 all-gather.16
  488.7 29.4 reduce-scatter.6
  520.3 65.0 reduce-scatter.4
  587.7 85.5 reduce-scatter.8
  675.6 85.7 reduce-scatter.10
  764.9 94.8 all-reduce.13
where the time goes:
time: 880 us; the launch traced here: 874 us
  waiting for transfers between devices  508 us (58%)
  matrix products  221 us (25%)
  other arithmetic  45.4 us (5%)
  local copies, waits for them, and re-layouts  37.6 us (4%)
  blocking collectives  35.1 us (4%)
  between operations  18.3 us (2%)
  starting transfers between devices  8.87 us (1%)
    all_gather x1, waiting for transfers between devices, on_device(): lax.all_gather(shards[6], 'dp', axis=0, tiled=True)  89.3 us
    reduce_scatter x1, waiting for transfers between devices, on_device(): lax.psum_scatter(totals[7].astype(jnp.bfloat16), 'dp', scatter_dimension=...  88.1 us
    all_gather x1, waiting for transfers between devices, on_device(): lax.all_gather(shards[7], 'dp', axis=0, tiled=True)  88 us
    reduce_scatter x1, waiting for transfers between devices, on_device(): lax.psum_scatter(totals[6].astype(jnp.bfloat16), 'dp', scatter_dimension=...  87.9 us
    dot_general x12, matrix products, inner(): lax.dot_general(left, right, (((0,), (0,)), ((), ())), preferred_element_...  59.4 us
    all_gather x1, waiting for transfers between devices, on_device(): lax.all_gather(shards[2], 'dp', axis=0, tiled=True)  53.3 us
    psum x1, waiting for transfers between devices, on_device(): lax.psum(rows[2].astype(jnp.bfloat16), 'group').astype(jnp.float32)  50.2 us
    dot_general x12, matrix products, times_transposed(): lax.dot_general(left, weight, (((1,), (1,)), ((), ())), preferred_element...  46.3 us
  transfers between devices with their start and end apart: 13, of which 10 were waited for; matrix products, arithmetic and copies ran while one was open for 15% of the time, Pallas kernels for 0%

commit v1 on v0

v1 whole, which is shorter than its diff:
```python
import functools

import jax
import jax.numpy as jnp
from jax import lax
from jax.experimental import pallas as pl
from jax.experimental.pallas import tpu as pltpu
from jax.sharding import PartitionSpec as P

HEAD_DIM = 64
LANES = 128
BLOCK = 384
PARTS = 4


masked_score = -1000000000.0


def rope_tables(lengths_row, tok):
    bounds = jnp.cumsum(lengths_row, dtype=jnp.int32)
    places = jnp.arange(tok, dtype=jnp.int32)
    segment = jnp.sum((places[:, None] >= bounds[None, :-1]).astype(jnp.int32), axis=1)
    starts = bounds - lengths_row
    picks = jnp.arange(lengths_row.shape[0], dtype=jnp.int32)
    begin = jnp.sum(jnp.where(segment[:, None] == picks[None, :], starts[None, :], 0), axis=1)
    offset = (places - begin).astype(jnp.float32)
    half = HEAD_DIM // 2
    freqs = 10000.0 ** (-jnp.arange(half, dtype=jnp.float32) / half)
    angles = offset[:, None] * freqs[None, :]
    cosine, sine = jnp.cos(angles), jnp.sin(angles)
    heads = LANES // HEAD_DIM
    cosine = jnp.concatenate([cosine, cosine] * heads, axis=1)
    sine = jnp.concatenate([-sine, sine] * heads, axis=1)
    return cosine, sine, segment


def mm(left, right, left_dim, right_dim):
    return lax.dot_general(
        left, right, (((left_dim,), (right_dim,)), ((), ())), preferred_element_type=jnp.float32
    )


def normalize(x):
    center = x - jnp.mean(x, axis=-1, keepdims=True)
    spread = jnp.mean(center * center, axis=-1, keepdims=True)
    scale = lax.rsqrt(spread + 1e-05)
    return center * scale, scale


def norm_backward(d_out, hat, scale, gain):
    d_hat = d_out * gain
    part = d_hat - jnp.mean(d_hat, axis=-1, keepdims=True)
    part = part - hat * jnp.mean(d_hat * hat, axis=-1, keepdims=True)
    return part * scale


def swap_halves(x):
    half = HEAD_DIM // 2
    lane = lax.broadcasted_iota(jnp.int32, x.shape, 1)
    low = lane % HEAD_DIM < half
    return jnp.where(low, pltpu.roll(x, LANES - half, 1), pltpu.roll(x, half, 1))


def head_of(x, which):
    lane = lax.broadcasted_iota(jnp.int32, x.shape, 1)
    inside = lane < HEAD_DIM if which == 0 else lane >= HEAD_DIM
    return jnp.where(inside, x, jnp.zeros_like(x))


def masks_of(groups, low_first):
    bits = [1 << i for i in range(groups.bit_length() - 1)]
    turn = len(bits) // 2
    tables = []
    for order in (bits, bits[turn:] + bits[:turn]):
        if not low_first:
            order = order[::-1]
        tables.append([sum(b for t, b in enumerate(order) if (j >> t) & 1) for j in range(groups)])
    return tables


def pick(flag, a, b):
    return a if a == b else jnp.where(flag, a, b)


class Plan:
    def __init__(self, groups, rows, tok, width):
        self.groups = groups
        self.rows = rows
        self.tok = tok
        self.width = width
        self.pieces = groups * rows
        self.tall = width // self.pieces
        self.direct = self.tall % 16 == 0


def start_weights(plan, layer, kind, ids, own, others, whole, dst, sem):
    width, tall = plan.width, plan.tall
    if not plan.direct:
        for h in range(2):
            lanes = pl.ds(h * BLOCK, BLOCK)
            if kind == "down":
                pltpu.make_async_copy(whole.at[h], dst.at[:, lanes], sem).start()
            else:
                pltpu.make_async_copy(whole.at[h], dst.at[:, :, lanes], sem).start()
        return
    core, group, row = ids[0], ids[1], ids[2]
    share = width // plan.rows
    mine, theirs = own

    def from_shard(refs):
        if kind == "down":
            at = pl.multiple_of(row * (share * PARTS), 16)
            pltpu.make_async_copy(refs[0].at[0], dst.at[pl.ds(at, share * PARTS)], sem).start()
            return
        at = pl.multiple_of(row * share, 16)
        j = 0
        for ref in refs:
            for b in range(ref.shape[2] // width):
                pltpu.make_async_copy(
                    ref.at[0, :, pl.ds(b * width, width)], dst.at[j, pl.ds(at, share)], sem
                ).start()
                j += 1

    @pl.when(core == layer)
    def _():
        from_shard(mine)

    @pl.when(core != layer)
    def _():
        from_shard(theirs)

    tables = masks_of(plan.groups, True)
    for source, flag in zip(others, (core == 0, core != 0)):
        half = core if source is others[0] else 1 - core
        lanes = pl.ds(pl.multiple_of(half * BLOCK, LANES), BLOCK)
        for j in range(plan.groups):
            peer = group ^ pick(flag, tables[0][j], tables[1][j])
            for k in range(plan.rows - 1):
                at = ((row + (plan.rows - 1 - k)) % plan.rows) * plan.groups + peer
                if kind == "down":
                    at = pl.multiple_of(at * (tall * PARTS), 16)
                    to = dst.at[pl.ds(at, tall * PARTS), lanes]
                else:
                    to = dst.at[:, pl.ds(pl.multiple_of(at * tall, 16), tall), lanes]
                pltpu.make_async_copy(source.at[j, k], to, sem).start()


def wait_all(ref, sem):
    pltpu.make_async_copy(ref, ref, sem).wait()


def start_grads(plan, kind, ids, src, keep, send, sem):
    width, tall = plan.width, plan.tall
    core, group, row = ids[0], ids[1], ids[2]
    if not plan.direct:
        for out, half in ((keep, core), (send, 1 - core)):
            lanes = pl.ds(pl.multiple_of(half * BLOCK, LANES), BLOCK)
            if kind == "down":
                pltpu.make_async_copy(src.at[:, lanes], out, sem).start()
            else:
                pltpu.make_async_copy(src.at[:, :, lanes], out, sem).start()
        return
    tables = masks_of(plan.groups, False)
    for out, half, flag in ((keep, core, core == 0), (send, 1 - core, core != 0)):
        lanes = pl.ds(pl.multiple_of(half * BLOCK, LANES), BLOCK)
        for j in range(plan.groups):
            peer = group ^ pick(flag, tables[0][j], tables[1][j])
            for k in range(plan.rows):
                at = ((row + k) % plan.rows) * plan.groups + peer
                if kind == "down":
                    part = src.at[pl.ds(pl.multiple_of(at * (tall * PARTS), 16), tall * PARTS), lanes]
                else:
                    part = src.at[:, pl.ds(pl.multiple_of(at * tall, 16), tall), lanes]
                pltpu.make_async_copy(part, out.at[j, k], sem).start()


def attend_forward(plan, layer, ids, lens, x_ref, small, cosv, sinv, *refs):
    n = 7
    own, others, whole = weight_refs(plan, "attend", refs[: plan_inputs(plan, "attend")])
    refs = refs[plan_inputs(plan, "attend") :]
    normed, qkv, probs, mixed, resid, w, same, sem = refs
    width, tok = plan.width, plan.tok
    start_weights(plan, layer, "attend", ids, own, others, whole, w, sem)
    x = x_ref[...].astype(jnp.float32)
    hat, _ = normalize(x)
    low = (hat * small[0:1, :] + small[1:2, :]).astype(jnp.bfloat16)
    normed[...] = low
    first_end = lens[0]
    second_end = lens[0] + lens[1]

    def seg(axis):
        at = lax.broadcasted_iota(jnp.int32, (tok, tok), axis)
        return (at >= first_end).astype(jnp.int32) + (at >= second_end).astype(jnp.int32)

    same[...] = (seg(0) == seg(1)).astype(jnp.float32)
    wait_all(w, sem)
    for j in range(3):
        full = mm(low, w[j], 1, 0)
        if j == 2:
            qkv[:, j * width : (j + 1) * width] = full.astype(jnp.bfloat16)
            continue
        for t in range(width // LANES):
            part = full[:, t * LANES : (t + 1) * LANES]
            part = part * cosv[...] + swap_halves(part) * sinv[...]
            qkv[:, j * width + t * LANES : j * width + (t + 1) * LANES] = part.astype(jnp.bfloat16)

    def tile(t, carry):
        at = pl.multiple_of(t * LANES, LANES)
        q = qkv[:, pl.ds(at, LANES)]
        k = qkv[:, pl.ds(width + at, LANES)]
        v = qkv[:, pl.ds(2 * width + at, LANES)]
        total = None
        for h in range(2):
            scores = mm(head_of(q, h), k, 1, 1) * HEAD_DIM ** (-0.5)
            scores = jnp.where(same[...] > 0.5, scores, masked_score)
            peak = jnp.max(scores, axis=-1, keepdims=True)
            expd = jnp.exp(scores - peak)
            p = expd * (1.0 / jnp.sum(expd, axis=-1, keepdims=True))
            probs[2 * t + h] = p
            part = mm(p.astype(jnp.bfloat16), head_of(v, h), 1, 0)
            total = part if total is None else total + part
        mixed[:, pl.ds(at, LANES)] = total.astype(jnp.bfloat16)
        return carry

    lax.fori_loop(0, width // LANES, tile, 0)
    resid[...] = x + mm(mixed[...], w[3], 1, 0)


def feed_forward(plan, layer, ids, resid, small, *refs):
    a = plan_inputs(plan, "up")
    b = plan_inputs(plan, "down")
    up_refs = weight_refs(plan, "up", refs[:a])
    down_refs = weight_refs(plan, "down", refs[a : a + b])
    normed, active, slope, y, wu, wd, sem_u, sem_d = refs[a + b :]
    width = plan.width
    start_weights(plan, layer, "up", ids, *up_refs, wu, sem_u)
    start_weights(plan, layer, "down", ids, *down_refs, wd, sem_d)
    hat, _ = normalize(resid[...])
    low = (hat * small[2:3, :] + small[3:4, :]).astype(jnp.bfloat16)
    normed[...] = low
    wait_all(wu, sem_u)
    total = resid[...]
    for j in range(PARTS):
        v = mm(low, wu[j], 1, 0)
        cdf = 0.5 * (1.0 + lax.erf(v * (2.0**-0.5)))
        act = (v * cdf).astype(jnp.bfloat16)
        lanes = slice(j * width, (j + 1) * width)
        active[:, lanes] = act
        slope[:, lanes] = cdf + v * (jnp.exp(v * v * -0.5) * 0.3989422804014327)
        if j == 0:
            wait_all(wd, sem_d)
        total = total + mm(act, wd[lanes, :], 1, 0)
    y[...] = total.astype(jnp.bfloat16)


def down_grad(plan, ids, active, d_out, keep, send, g, sem):
    width = plan.width
    d = d_out[...]
    for j in range(PARTS):
        g[j * width : (j + 1) * width, :] = mm(
            active[:, j * width : (j + 1) * width], d, 0, 0
        ).astype(jnp.bfloat16)
    start_grads(plan, "down", ids, g, keep, send, sem)
    wait_all(g, sem)


def feed_backward(plan, layer, ids, d_out, resid, normed, slope, small, *refs):
    a = plan_inputs(plan, "up")
    b = plan_inputs(plan, "down")
    up_refs = weight_refs(plan, "up", refs[:a])
    down_refs = weight_refs(plan, "down", refs[a : a + b])
    keep, send, d_resid, sums, wu, wd, g, sem_u, sem_d, sem_g = refs[a + b :]
    width = plan.width
    start_weights(plan, layer, "down", ids, *down_refs, wd, sem_d)
    start_weights(plan, layer, "up", ids, *up_refs, wu, sem_u)
    d = d_out[...]
    low = normed[...]
    wait_all(wd, sem_d)
    total = None
    for j in range(PARTS):
        lanes = slice(j * width, (j + 1) * width)
        d_up = (mm(d, wd[lanes, :], 1, 1) * slope[:, lanes]).astype(jnp.bfloat16)
        g[j] = mm(low, d_up, 0, 0).astype(jnp.bfloat16)
        if j == 0:
            wait_all(wu, sem_u)
        part = mm(d_up, wu[j], 1, 1)
        total = part if total is None else total + part
    start_grads(plan, "up", ids, g, keep, send, sem_g)
    hat, scale = normalize(resid[...])
    sums[0:1, :] = jnp.sum(total * hat, axis=0, keepdims=True)
    sums[1:2, :] = jnp.sum(total, axis=0, keepdims=True)
    d_resid[...] = d.astype(jnp.float32) + norm_backward(total, hat, scale, small[2:3, :])
    wait_all(g, sem_g)


def attend_backward(plan, layer, ids, x_ref, d_resid, normed, qkv, probs, mixed, small, cosv, sinv, *refs):
    a = plan_inputs(plan, "attend")
    own, others, whole = weight_refs(plan, "attend", refs[:a])
    keep, send, dx, sums, w, g, d_mixed, d_qkv, sem_w, sem_g = refs[a:]
    width = plan.width
    start_weights(plan, layer, "attend", ids, own, others, whole, w, sem_w)
    d = d_resid[...].astype(jnp.bfloat16)
    g[3] = mm(mixed[...], d, 0, 0).astype(jnp.bfloat16)
    wait_all(w, sem_w)
    d_mixed[...] = mm(d, w[3], 1, 1).astype(jnp.bfloat16)

    def tile(t, carry):
        at = pl.multiple_of(t * LANES, LANES)
        q = qkv[:, pl.ds(at, LANES)]
        k = qkv[:, pl.ds(width + at, LANES)]
        v = qkv[:, pl.ds(2 * width + at, LANES)]
        dm = d_mixed[:, pl.ds(at, LANES)]
        dq = dk = dv = None
        for h in range(2):
            p = probs[2 * t + h]
            dm_h = head_of(dm, h)
            dv_h = mm(p.astype(jnp.bfloat16), dm_h, 0, 0)
            dp = mm(dm_h, v, 1, 1)
            ds = p * (dp - jnp.sum(dp * p, axis=-1, keepdims=True))
            ds = ds.astype(jnp.bfloat16)
            dq_h = mm(ds, head_of(k, h), 1, 0)
            dk_h = mm(ds, head_of(q, h), 0, 0)
            dq = dq_h if dq is None else dq + dq_h
            dk = dk_h if dk is None else dk + dk_h
            dv = dv_h if dv is None else dv + dv_h
        scale = HEAD_DIM ** (-0.5)
        dq = dq * scale
        dk = dk * scale
        dq = dq * cosv[...] - swap_halves(dq) * sinv[...]
        dk = dk * cosv[...] - swap_halves(dk) * sinv[...]
        d_qkv[:, pl.ds(at, LANES)] = dq.astype(jnp.bfloat16)
        d_qkv[:, pl.ds(width + at, LANES)] = dk.astype(jnp.bfloat16)
        d_qkv[:, pl.ds(2 * width + at, LANES)] = dv.astype(jnp.bfloat16)
        return carry

    lax.fori_loop(0, width // LANES, tile, 0)
    low = normed[...]
    total = None
    for j in range(3):
        part_in = d_qkv[:, j * width : (j + 1) * width]
        g[j] = mm(low, part_in, 0, 0).astype(jnp.bfloat16)
        part = mm(part_in, w[j], 1, 1)
        total = part if total is None else total + part
    start_grads(plan, "attend", ids, g, keep, send, sem_g)
    hat, scale = normalize(x_ref[...].astype(jnp.float32))
    sums[0:1, :] = jnp.sum(total * hat, axis=0, keepdims=True)
    sums[1:2, :] = jnp.sum(total, axis=0, keepdims=True)
    back = d_resid[...] + norm_backward(total, hat, scale, small[0:1, :])
    dx[...] = back.astype(jnp.bfloat16)
    wait_all(g, sem_g)


SHARDS = {"attend": 2, "up": 1, "down": 1}


def plan_inputs(plan, kind):
    return 2 * SHARDS[kind] + 2 if plan.direct else 1


def weight_refs(plan, kind, refs):
    if not plan.direct:
        return None, None, refs[0]
    n = SHARDS[kind]
    return (refs[:n], refs[n : 2 * n]), refs[2 * n :], None


VMEM = pl.BlockSpec(memory_space=pltpu.VMEM)
SMEM = pl.BlockSpec(memory_space=pltpu.SMEM)
HBM = pl.BlockSpec(memory_space=pl.ANY)


def call(body, name, args, specs, outs, out_specs, scratch, flops):
    moved = sum(x.size * x.dtype.itemsize for x in list(args) + list(outs))
    return pl.pallas_call(
        body,
        out_shape=outs,
        in_specs=specs,
        out_specs=out_specs,
        scratch_shapes=scratch,
        name=name,
        cost_estimate=pl.CostEstimate(flops=flops, transcendentals=0, bytes_accessed=moved),
        compiler_params=pltpu.CompilerParams(vmem_limit_bytes=58 << 20),
    )(*args)


def shape(dims, dtype):
    return jax.ShapeDtypeStruct(dims, dtype)


BF, F32 = jnp.bfloat16, jnp.float32


class Kernels:
    def __init__(self, plan, ids, lens, tables, heads):
        self.plan, self.ids, self.lens, self.tables, self.heads = plan, ids, lens, tables, heads
        self.part = pltpu.VMEM((PARTS, plan.width, plan.width), BF)
        self.tall = pltpu.VMEM((PARTS * plan.width, plan.width), BF)
        self.sem = pltpu.SemaphoreType.DMA(())

    def attend_forward(self, layer, x, small, weights):
        p = self.plan
        t, d = p.tok, p.width
        return call(
            functools.partial(attend_forward, p, layer),
            f"attend_forward_{layer}",
            (self.ids, self.lens, x, small, *self.tables, *weights),
            [SMEM, SMEM] + [VMEM] * 4 + [HBM] * len(weights),
            (
                shape((t, d), BF),
                shape((t, 3 * d), BF),
                shape((self.heads, t, t), F32),
                shape((t, d), BF),
                shape((t, d), F32),
            ),
            (VMEM,) * 5,
            [self.part, pltpu.VMEM((t, t), F32), self.sem],
            2 * t * d * d * 4 + 4 * self.heads * t * t * LANES,
        )

    def feed_forward(self, layer, resid, small, weights):
        p = self.plan
        t, d = p.tok, p.width
        return call(
            functools.partial(feed_forward, p, layer),
            f"feed_forward_{layer}",
            (self.ids, resid, small, *weights),
            [SMEM, VMEM, VMEM] + [HBM] * len(weights),
            (
                shape((t, d), BF),
                shape((t, PARTS * d), BF),
                shape((t, PARTS * d), F32),
                shape((t, d), BF),
            ),
            (VMEM,) * 4,
            [self.part, self.tall, self.sem, self.sem],
            2 * t * d * d * 8,
        )

    def grads(self, kind):
        p = self.plan
        rows = p.tall * PARTS if kind == "down" else None
        if not p.direct:
            dims = (PARTS * p.width, BLOCK) if kind == "down" else (PARTS, p.width, BLOCK)
        elif kind == "down":
            dims = (p.groups, p.rows, rows, BLOCK)
        else:
            dims = (p.groups, p.rows, PARTS, p.tall, BLOCK)
        return (shape(dims, BF), shape(dims, BF))

    def down_grad(self, layer, active, d_out):
        p = self.plan
        return call(
            functools.partial(down_grad, p),
            f"down_grad_{layer}",
            (self.ids, active, d_out),
            [SMEM, VMEM, VMEM],
            self.grads("down"),
            (HBM, HBM),
            [self.tall, self.sem],
            2 * p.tok * p.width * p.width * 4,
        )

    def feed_backward(self, layer, d_out, resid, normed, slope, small, weights):
        p = self.plan
        t, d = p.tok, p.width
        return call(
            functools.partial(feed_backward, p, layer),
            f"feed_backward_{layer}",
            (self.ids, d_out, resid, normed, slope, small, *weights),
            [SMEM] + [VMEM] * 5 + [HBM] * len(weights),
            (*self.grads("up"), shape((t, d), F32), shape((2, d), F32)),
            (HBM, HBM, VMEM, VMEM),
            [self.part, self.tall, self.part, self.sem, self.sem, self.sem],
            2 * t * d * d * 12,
        )

    def attend_backward(self, layer, x, d_resid, normed, qkv, probs, mixed, small, weights):
        p = self.plan
        t, d = p.tok, p.width
        return call(
            functools.partial(attend_backward, p, layer),
            f"attend_backward_{layer}",
            (self.ids, x, d_resid, normed, qkv, probs, mixed, small, *self.tables, *weights),
            [SMEM] + [VMEM] * 9 + [HBM] * len(weights),
            (*self.grads("attend"), shape((t, d), BF), shape((2, d), F32)),
            (HBM, HBM, VMEM, VMEM),
            [self.part, self.part, pltpu.VMEM((t, d), BF), pltpu.VMEM((t, 3 * d), BF), self.sem, self.sem],
            2 * t * d * d * 8 + 10 * self.heads * t * t * LANES,
        )


def swap_cores(x):
    return lax.ppermute(x, "section", [(0, 1), (1, 0)])


def stage_bits(groups):
    bits = [1 << i for i in range(groups.bit_length() - 1)]
    turn = len(bits) // 2
    return bits, bits[turn:] + bits[:turn]


def swap_groups(x, groups, stage):
    pairs = []
    for core, bits in enumerate(stage_bits(groups)):
        pairs += [(core * groups + g, core * groups + (g ^ bits[stage])) for g in range(groups)]
    return lax.ppermute(x, ("section", "group"), pairs)


def along(x, distance):
    rows = lax.axis_size("dp")
    return lax.ppermute(x, "dp", [(i, (i + distance) % rows) for i in range(rows)])


def gate(x, after):
    return lax.optimization_barrier((x, *after))[0] if after else x


KINDS = ("attend", "up", "down")


def piece_of(plan, group, kind, shards):
    tall = plan.tall

    def cut(w, inside):
        if inside:
            w = lax.dynamic_slice_in_dim(w[0], group * (tall * PARTS), tall * PARTS, 0)
            return w.reshape(PARTS, tall, 2, BLOCK).transpose(2, 0, 1, 3)
        w = lax.dynamic_slice_in_dim(w[0], group * tall, tall, 0)
        return w.reshape(tall, -1, 2, BLOCK).transpose(2, 1, 0, 3)

    return jnp.concatenate([cut(w, kind == "down") for w in shards], axis=1)


def whole_of(plan, core, group, row, kind, shard, half_mine, half_theirs):
    groups, rows, tall = plan.groups, plan.rows, plan.tall
    tables = jnp.array(masks_of(groups, True), jnp.int32)
    first = core == 0
    halves = []
    for h in range(2):
        got = jnp.where(core == h, half_mine, half_theirs)
        got = jnp.take(got, jnp.argsort(group ^ tables[h]), axis=0)
        own = []
        for w in shard:
            if kind == "down":
                w = w[0].reshape(groups, PARTS, tall, 2, BLOCK)[:, :, :, h]
            else:
                w = w[0].reshape(groups, tall, -1, 2, BLOCK)[:, :, :, h].transpose(0, 2, 1, 3)
            own.append(w)
        own = jnp.concatenate(own, axis=1)[:, None]
        got = jnp.concatenate([got, own], axis=1)
        got = jnp.take(got, (row - 1 - jnp.arange(rows)) % rows, axis=1)
        if kind == "down":
            halves.append(got.transpose(1, 0, 2, 3, 4).reshape(PARTS * plan.width, BLOCK))
        else:
            halves.append(got.transpose(2, 1, 0, 3, 4).reshape(PARTS, plan.width, BLOCK))
    return jnp.stack(halves)


def ordered_grads(plan, kind, core, group, row, keep, send):
    groups, rows, tall = plan.groups, plan.rows, plan.tall
    tables = jnp.array(masks_of(groups, False), jnp.int32)
    outs = []
    for x, half in ((keep, core), (send, 1 - core)):
        if kind == "down":
            x = x.reshape(rows, groups, PARTS, tall, BLOCK).transpose(1, 0, 2, 3, 4)
        else:
            x = x.reshape(PARTS, rows, groups, tall, BLOCK).transpose(2, 1, 0, 3, 4)
        x = jnp.take(x, group ^ jnp.where(half == 0, tables[0], tables[1]), axis=0)
        x = jnp.take(x, (row + jnp.arange(rows)) % rows, axis=1)
        outs.append(x)
    return outs


def on_device(
    tokens,
    cotangent,
    lengths,
    attend_gain,
    attend_bias,
    qkv_weight,
    out_weight,
    feed_gain,
    feed_bias,
    up_weight,
    down_weight,
):
    core = lax.axis_index("section")
    group = lax.axis_index("group")
    row = lax.axis_index("dp")
    groups = lax.axis_size("group")
    rows = lax.axis_size("dp")
    stages = groups.bit_length() - 1
    tok, width = tokens.shape[1:]
    plan = Plan(groups, rows, tok, width)
    few = rows <= 4
    first = core == 0
    share = width // rows
    ids = jnp.stack([core, group, row]).astype(jnp.int32)
    lens = lax.dynamic_index_in_dim(lengths, core, 0, False)[0]

    shards = {"attend": (qkv_weight, out_weight), "up": (up_weight,), "down": (down_weight,)}
    pieces = {}
    for kind in KINDS:
        both = piece_of(plan, group, kind, shards[kind])
        keep = lax.dynamic_index_in_dim(both, core, 0, False)
        got = swap_cores(lax.dynamic_index_in_dim(both, 1 - core, 0, False))
        pieces[0, kind] = jnp.where(first, keep, got)
        pieces[1, kind] = jnp.where(first, got, keep)
    theirs = {}
    chunks = [(layer, kind) for layer in range(2) for kind in KINDS]
    history = []
    bufs = {}
    for slot in range(len(chunks) + stages):
        after = history[slot - DEPTH] if slot >= DEPTH else []
        done = []
        for stage in range(stages, 0, -1):
            c = slot - stage
            if 0 <= c < len(chunks):
                got = swap_groups(gate(bufs[c], after), groups, stage - 1)
                bufs[c] = jnp.concatenate([bufs[c], got], axis=0)
                done.append(got)
        if slot < len(chunks):
            piece = gate(pieces[chunks[slot]], after)
            if few:
                got = [along(piece, k) for k in range(1, rows)]
                bufs[slot] = jnp.stack(got)[None]
            else:
                got = [lax.all_gather(piece, "dp")]
                back = (row - 1 - jnp.arange(rows - 1)) % rows
                bufs[slot] = jnp.take(got[0], back, axis=0)[None]
            done += got
        if slot == 0:
            small = jnp.stack([attend_gain[0], attend_bias[0], feed_gain[0], feed_bias[0]])
            smalls = lax.all_gather(gate(small, done[:1]), ("section", "dp"))
            smalls = smalls.reshape(2, rows, PARTS, share).transpose(0, 2, 1, 3)
            smalls = smalls.reshape(2, PARTS, width).astype(F32)
        if slot == 1:
            for kind in KINDS:
                theirs[kind] = tuple(swap_cores(gate(w, done[:1])) for w in shards[kind])
        history.append(done)
    gathered = {}
    for c, (layer, kind) in enumerate(chunks):
        mine = bufs[c]
        other = swap_cores(mine)
        if plan.direct:
            if kind == "down":
                flat = (groups, rows - 1, PARTS * plan.tall, BLOCK)
                mine, other = mine.reshape(flat), other.reshape(flat)
            gathered[layer, kind] = (*shards[kind], *theirs[kind], mine, other)
        else:
            shard = [jnp.where(core == layer, a, b) for a, b in zip(shards[kind], theirs[kind])]
            gathered[layer, kind] = (
                whole_of(plan, core, group, row, kind, shard, mine, other),
            )

    x0 = lax.dynamic_index_in_dim(tokens, core, 0, False)
    cot = lax.dynamic_index_in_dim(cotangent, core, 0, False)
    cosine, sine, _ = rope_tables(lens, tok)
    kernels = Kernels(plan, ids, lens, (cosine, sine), width // HEAD_DIM)
    xs, saved = [x0], []
    for layer in range(2):
        a = kernels.attend_forward(layer, xs[layer], smalls[layer], gathered[layer, "attend"])
        weights = gathered[layer, "up"] + gathered[layer, "down"]
        f = kernels.feed_forward(layer, a[4], smalls[layer], weights)
        xs.append(f[3])
        saved.append((a, f))
    grads, sums, backs = {}, {}, [None, None]
    d_out = cot
    for layer in (1, 0):
        (normed, qkv, probs, mixed, resid), (normed_two, active, slope, _) = saved[layer]
        grads[layer, "down"] = kernels.down_grad(layer, active, d_out)
        weights = gathered[layer, "up"] + gathered[layer, "down"]
        *g, d_resid, sums_two = kernels.feed_backward(
            layer, d_out, resid, normed_two, slope, smalls[layer], weights
        )
        grads[layer, "up"] = g
        *g, d_out, sums_one = kernels.attend_backward(
            layer, xs[layer], d_resid, normed, qkv, probs, mixed, smalls[layer], gathered[layer, "attend"]
        )
        grads[layer, "attend"] = g
        sums[layer] = jnp.concatenate([sums_one, sums_two])
        backs[layer] = d_out

    def home(low, high):
        got = swap_cores(jnp.where(first, high, low))
        keep = jnp.where(first, low, high)
        return jnp.where(first, jnp.stack([keep, got]), jnp.stack([got, keep]))

    layer_out = home(xs[1], xs[2])
    input_grad = home(*backs)

    def add(a, b):
        return (a.astype(F32) + b.astype(F32)).astype(BF)

    def reduce(kind, keep, send):
        if plan.direct:
            dims = (groups, rows, PARTS, plan.tall, BLOCK)
            keep, send = keep.reshape(dims), send.reshape(dims)
        else:
            keep, send = ordered_grads(plan, kind, core, group, row, keep, send)
        got = swap_cores(send)
        for stage in range(stages):
            half = keep.shape[0] // 2
            high = add(keep[half:], got[half:])
            keep = add(keep[:half], got[:half])
            got = swap_groups(high, groups, stage)
        keep, got = keep[0], got[0]
        if few:
            moved = [along(add(keep[k], got[k]), k) for k in range(1, rows)]
            total = keep[0].astype(F32) + got[0].astype(F32)
            for m in moved:
                total = total + m.astype(F32)
        else:
            total = add(keep, got)
            total = jnp.take(total, (jnp.arange(rows) - row) % rows, axis=0)
            total = lax.psum_scatter(total, "dp", scatter_dimension=0, tiled=False)
        total = total.astype(BF)[None]
        for stage in range(stages - 1, -1, -1):
            total = jnp.concatenate([total, swap_groups(total, groups, stage)], axis=0)
        return total

    reduced = {}
    for layer in (1, 0):
        for kind in ("down", "up", "attend"):
            reduced[layer, kind] = reduce(kind, *grads[layer, kind])
    tables = jnp.array(masks_of(groups, False), jnp.int32)
    final = {}
    for kind in KINDS:
        own = jnp.where(first, reduced[0, kind], reduced[1, kind])
        other = swap_cores(jnp.where(first, reduced[1, kind], reduced[0, kind]))
        low = jnp.where(first, own, other)
        high = jnp.where(first, other, own)
        low = jnp.take(low, jnp.argsort(group ^ tables[0]), axis=0)
        high = jnp.take(high, jnp.argsort(group ^ tables[1]), axis=0)
        final[kind] = jnp.stack([low, high])

    def outside(x):
        return x.transpose(1, 3, 2, 0, 4).reshape(share, -1).astype(F32)

    qkv_grad = outside(final["attend"][:, :, 0:3])
    out_grad = outside(final["attend"][:, :, 3:4])
    up_grad = outside(final["up"])
    down_grads = final["down"].transpose(1, 2, 3, 0, 4).reshape(-1, width).astype(F32)

    small_grads = jnp.stack([sums[0], sums[1]])
    small_grads = lax.psum(small_grads, ("section", "group", "dp"))
    own = lax.dynamic_index_in_dim(small_grads, core, 0, False)
    own = lax.dynamic_slice_in_dim(own, row * share, share, 1)
    return (
        layer_out[None],
        input_grad[None],
        own[0][None],
        own[1][None],
        qkv_grad[None],
        out_grad[None],
        own[2][None],
        own[3][None],
        up_grad[None],
        down_grads[None],
    )


DEPTH = 2


def solution(mesh):
    placed = (
        P(None, ("group", "dp"), None),
        P(None, ("group", "dp"), None),
        P(None, ("group", "dp"), None),
        P("section", "dp"),
        P("section", "dp"),
        P("section", "dp", None),
        P("section", "dp", None),
        P("section", "dp"),
        P("section", "dp"),
        P("section", "dp", None),
        P("section", "dp", None),
    )
    return jax.shard_map(
        on_device,
        mesh=mesh,
        in_specs=placed,
        out_specs=(
            P("section", None, ("group", "dp"), None),
            P("section", None, ("group", "dp"), None),
            P("section", "dp"),
            P("section", "dp"),
            P("section", "dp", None),
            P("section", "dp", None),
            P("section", "dp"),
            P("section", "dp"),
            P("section", "dp", None),
            P("section", "dp", None),
        ),
        check_vma=False,
    )
```

time: 880 us -> 604 us (0.69)
  waiting for transfers between devices: 508 us -> 162 us
  matrix products: 221 us -> 0 us
  starting transfers between devices: 8.87 us -> 156 us
  Pallas kernels: 0 us -> 105 us
  blocking collectives: 35.1 us -> 60.9 us
  other arithmetic: 45.4 us -> 67.6 us
  between operations: 18.3 us -> 2.14 us
    all_gather x4 -> x0, waiting for transfers between devices: 250 us -> none  [the longest x1 89.3 us: on_device(): lax.all_gather(shards[6], 'dp', axis=0, tiled=True)]
    dot_general x63 -> x0, matrix products: 207 us -> none  [the longest x12 59.4 us: inner(): lax.dot_general(left, right, (((0,), (0,)), ((), ())), preferred_element_...]
    reduce_scatter x4 -> x0, waiting for transfers between devices: 204 us -> none  [the longest x1 88.1 us: on_device(): lax.psum_scatter(totals[7].astype(jnp.bfloat16), 'dp', scatter_dimension=...]
    ppermute x4 -> x96, waiting for transfers between devices: 1.6 us -> 162 us  [the longest x36 104 us: swap_groups(): return lax.ppermute(x, ('section', 'group'), pairs)]
    ppermute x4 -> x96, starting transfers between devices: 8.1 us -> 156 us  [the longest x36 90.1 us: along(): lax.ppermute(x, 'dp', [(i, (i + distance) % rows) for i in range(rows)])]
    pallas_call x0 -> x10, Pallas kernels: none -> 105 us  [call(): pl.pallas_call(body, out_shape=outs, in_specs=specs, out_specs=out_specs,...]
    psum x1 -> x0, waiting for transfers between devices: 50.2 us -> none  [on_device(): lax.psum(rows[2].astype(jnp.bfloat16), 'group').astype(jnp.float32)]
    concatenate x0 -> x22, other arithmetic: none -> 29.9 us  [the longest x14 27.9 us: on_device(): bufs[c] = jnp.concatenate([bufs[c], got], axis=0)]
  transfers between devices with their start and end apart: 13 -> 96, of which waited for: 10 -> 33; matrix products, arithmetic and copies ran while one was open for 15% -> 12% of each run, Pallas kernels for 0% -> 7%
where the time goes in v1:
time: 604 us; the launch traced here: 595 us
  waiting for transfers between devices  162 us (27%)
  starting transfers between devices  156 us (26%)
  Pallas kernels  105 us (17%)
  other arithmetic  67.6 us (11%)
  blocking collectives  60.9 us (10%)
  local copies, waits for them, and re-layouts  41.1 us (7%)
    pallas_call x10, Pallas kernels, call(): pl.pallas_call(body, out_shape=outs, in_specs=specs, out_specs=out_specs,...  105 us
    ppermute x36, waiting for transfers between devices, swap_groups(): return lax.ppermute(x, ('section', 'group'), pairs)  104 us
    ppermute x36, starting transfers between devices, along(): lax.ppermute(x, 'dp', [(i, (i + distance) % rows) for i in range(rows)])  90.1 us
    ppermute x36, waiting for transfers between devices, along(): lax.ppermute(x, 'dp', [(i, (i + distance) % rows) for i in range(rows)])  56.9 us
    ppermute x36, starting transfers between devices, swap_groups(): return lax.ppermute(x, ('section', 'group'), pairs)  51.1 us
    psum x1, blocking collectives, on_device(): small_grads = lax.psum(small_grads, ('section', 'group', 'dp'))  39.4 us
    concatenate x14, other arithmetic, on_device(): bufs[c] = jnp.concatenate([bufs[c], got], axis=0)  27.9 us
    all_gather x1, blocking collectives, on_device(): smalls = lax.all_gather(gate(small, done[:1]), ('section', 'dp'))  21.5 us
  transfers between devices with their start and end apart: 96, of which 33 were waited for; matrix products, arithmetic and copies ran while one was open for 12% of the time, Pallas kernels for 7%

profile of v1, /device:TPU:0, one launch (start us, length us, event | category | flops | bytes accessed | tf_op | source)
XLA Modules:
  0.0 595.4 jit_solution(15390618435854325552)
XLA Ops:
  15.5 5.8 collective-permute-done.2
  54.7 5.9 collective-permute-done.20
  91.5 6.3 %collective-permute-start.38 = (bf16[4,48,384]{2,1,0:T(8,128)(2,1)}, bf16[4,48,384]{2,1,0:T(8,128)(2,1)S(1)}, u32[]{:S(2)}, u32[]{:S(2)}) collective-permute-start(bf16[4,48,384]{2,1,0:T(8,128)(2,1)} %get-tuple-element.91), channel_id=1, source_target_pairs={{0,2},{1,3},{2,0},{3,1},{4,6},{5,7},{6,4},{7,5},{8,10},{9,11},{10,... | collective-permute-start | bytes 442376 | tf_op jit(solution)/shard_map/ppermute | solution.py:511
  100.0 10.8 %collective-permute-start.33 = (bf16[4,48,384]{2,1,0:T(8,128)(2,1)}, bf16[4,48,384]{2,1,0:T(8,128)(2,1)S(1)}, u32[]{:S(2)}, u32[]{:S(2)}) collective-permute-start(bf16[4,48,384]{2,1,0:T(8,128)(2,1)} %get-tuple-element.88), channel_id=1, source_target_pairs={{0,3},{1,0},{2,1},{3,2},{4,7},{5,4},{6,5},{7,6},{8,11},{9,8},{10,9... | collective-permute-start | bytes 442376 | tf_op jit(solution)/shard_map/ppermute | solution.py:511
  128.1 5.1 collective-permute-start.9
  149.1 6.9 %collective-permute-done.41 = bf16[2,3,4,48,384]{4,3,2,1,0:T(8,128)(2,1)} collective-permute-done((bf16[2,3,4,48,384]{4,3,2,1,0:T(8,128)(2,1)}, bf16[2,3,4,48,384]{4,3,2,1,0:T(8,128)(2,1)}, u32[]{:S(2)}, u32[]{:S(2)}) %collective-permute-start.41) | collective-permute-done | bytes 884768 | tf_op jit(solution)/shard_map/ppermute | solution.py:506
  163.0 21.5 %all-gather.1 = bf16[8,4,192]{2,1,0:T(4,128)(2,1)S(1)} all-gather(bf16[1,4,192]{2,1,0:T(4,128)(2,1)S(1)} %bitcast.291), channel_id=2, replica_groups=mesh['section'=2,'group'=4,'dp'=4] {'section','dp'}, dimensions={0}, use_global_device_ids=true | all-gather | bytes 13824 | tf_op jit(solution)/shard_map/all_gather | solution.py:634
  188.5 10.0 %attend_forward_0.1 = (bf16[256,768]{1,0:T(8,128)(2,1)}, bf16[256,2304]{1,0:T(8,128)(2,1)}, f32[12,256,256]{2,1,0:T(8,128)}, bf16[256,768]{1,0:T(8,128)(2,1)}, f32[256,768]{1,0:T(8,128)}) custom-call(s32[3]{0:T(128)} %pad_add_fusion.ids, s32[3]{0:T(128)} %get-tuple-element.132.lens, bf16[256,768]{1,0:T(8,128)(2,1)} %dynamic-slice_bitcast_fusion.1.x_ref, ...), custom_call_target="tpu_custom_call" | custom-call | flops 1610612736 | bytes 12464152 | tf_op jit(solution)/shard_map/attend_forward_0/pallas_call | solution.py:374
  201.2 9.5 %feed_forward_0.1 = (bf16[256,768]{1,0:T(8,128)(2,1)}, bf16[256,3072]{1,0:T(8,128)(2,1)}, f32[256,3072]{1,0:T(8,128)}, bf16[256,768]{1,0:T(8,128)(2,1)}) custom-call(s32[3]{0:T(128)} %pad_add_fusion.ids, f32[256,768]{1,0:T(8,128)} %get-tuple-element.75.resid, f32[4,768]{1,0:T(4,128)} %squeeze.39.small, bf16[1,192,3072]{2,1,0:T(8,128)(2,1)} %refs_0_.14, ...), custom_call_target="tpu_custom_call" | custom-call | flops 2415919104 | bytes 18100236 | tf_op jit(solution)/shard_map/feed_forward_0/pallas_call | solution.py:374
  210.7 9.9 %attend_forward_1.1 = (bf16[256,768]{1,0:T(8,128)(2,1)}, bf16[256,2304]{1,0:T(8,128)(2,1)}, f32[12,256,256]{2,1,0:T(8,128)}, bf16[256,768]{1,0:T(8,128)(2,1)}, f32[256,768]{1,0:T(8,128)}) custom-call(s32[3]{0:T(128)} %pad_add_fusion.ids, s32[3]{0:T(128)} %get-tuple-element.132.lens, bf16[256,768]{1,0:T(8,128)(2,1)} %get-tuple-element.83.x_ref, ...), custom_call_target="tpu_custom_call" | custom-call | flops 1610612736 | bytes 12464152 | tf_op jit(solution)/shard_map/attend_forward_1/pallas_call | solution.py:374
  222.0 9.5 %feed_forward_1.1 = (bf16[256,768]{1,0:T(8,128)(2,1)}, bf16[256,3072]{1,0:T(8,128)(2,1)}, f32[256,3072]{1,0:T(8,128)}, bf16[256,768]{1,0:T(8,128)(2,1)}) custom-call(s32[3]{0:T(128)} %pad_add_fusion.ids, f32[256,768]{1,0:T(8,128)} %get-tuple-element.87.resid, f32[4,768]{1,0:T(4,128)} %squeeze.44.small, bf16[1,192,3072]{2,1,0:T(8,128)(2,1)} %refs_0_.14, ...), custom_call_target="tpu_custom_call" | custom-call | flops 2415919104 | bytes 18100236 | tf_op jit(solution)/shard_map/feed_forward_1/pallas_call | solution.py:374
  231.5 12.2 %feed_backward_1.1 = (bf16[4,4,4,48,384]{4,3,2,1,0:T(8,128)(2,1)}, bf16[4,4,4,48,384]{4,3,2,1,0:T(8,128)(2,1)}, f32[256,768]{1,0:T(8,128)}, f32[2,768]{1,0:T(2,128)}) custom-call(s32[3]{0:T(128)} %pad_add_fusion.ids, bf16[256,768]{1,0:T(8,128)(2,1)} %dynamic-slice_bitcast_fusion.d_out, f32[256,768]{1,0:T(8,128)} %get-tuple-element.87.resid, ...), custom_call_target="tpu_custom_call" | custom-call | flops 3623878656 | bytes 22038540 | tf_op jit(solution)/shard_map/feed_backward_1/pallas_call | solution.py:374
  243.7 15.6 %attend_backward_1.1 = (bf16[4,4,4,48,384]{4,3,2,1,0:T(8,128)(2,1)}, bf16[4,4,4,48,384]{4,3,2,1,0:T(8,128)(2,1)}, bf16[256,768]{1,0:T(8,128)(2,1)}, f32[2,768]{1,0:T(2,128)}) custom-call(s32[3]{0:T(128)} %pad_add_fusion.ids, bf16[256,768]{1,0:T(8,128)(2,1)} %get-tuple-element.83.x_ref, f32[256,768]{1,0:T(8,128)} %get-tuple-element.97.d_resid, ...), custom_call_target="tpu_custom_call" | custom-call | flops 3422552064 | bytes 17582092 | tf_op jit(solution)/shard_map/attend_backward_1/pallas_call | solution.py:374
  259.4 12.2 %feed_backward_0.1 = (bf16[4,4,4,48,384]{4,3,2,1,0:T(8,128)(2,1)}, bf16[4,4,4,48,384]{4,3,2,1,0:T(8,128)(2,1)}, f32[256,768]{1,0:T(8,128)}, f32[2,768]{1,0:T(2,128)}) custom-call(s32[3]{0:T(128)} %pad_add_fusion.ids, bf16[256,768]{1,0:T(8,128)(2,1)} %get-tuple-element.102.d_out, f32[256,768]{1,0:T(8,128)} %get-tuple-element.75.resid, ...), custom_call_target="tpu_custom_call" | custom-call | flops 3623878656 | bytes 22038540 | tf_op jit(solution)/shard_map/feed_backward_0/pallas_call | solution.py:374
  271.6 15.5 %attend_backward_0.1 = (bf16[4,4,4,48,384]{4,3,2,1,0:T(8,128)(2,1)}, bf16[4,4,4,48,384]{4,3,2,1,0:T(8,128)(2,1)}, bf16[256,768]{1,0:T(8,128)(2,1)}, f32[2,768]{1,0:T(2,128)}) custom-call(s32[3]{0:T(128)} %pad_add_fusion.ids, bf16[256,768]{1,0:T(8,128)(2,1)} %dynamic-slice_bitcast_fusion.1.x_ref, f32[256,768]{1,0:T(8,128)} %get-tuple-element.105.d_resid, ...), custom_call_target="tpu_custom_call" | custom-call | flops 3422552064 | bytes 17582092 | tf_op jit(solution)/shard_map/attend_backward_0/pallas_call | solution.py:374
  290.1 5.2 down_grad_0.1
  295.9 39.4 %psum.7 = f32[2,4,768]{2,1,0:T(4,128)} all-reduce(f32[2,4,768]{2,1,0:T(4,128)S(1)} %pad_maximum_fusion.29), channel_id=1, replica_groups=mesh['section'=2,'group'=4,'dp'=4] {'section','group','dp'}, use_global_device_ids=true, to_apply=%region_3.4 | all-reduce | flops 6144 | bytes 49152 | tf_op jit(solution)/shard_map/psum | solution.py:746
  336.1 5.3 down_grad_1.1
  364.4 10.3 %collective-permute-done.54 = bf16[2,4,4,48,384]{4,3,2,1,0:T(8,128)(2,1)S(1)} collective-permute-done((bf16[2,4,4,48,384]{4,3,2,1,0:T(8,128)(2,1)S(1)}, bf16[2,4,4,48,384]{4,3,2,1,0:T(8,128)(2,1)S(1)}, u32[]{:S(2)}, u32[]{:S(2)}) %collective-permute-start.54) | collective-permute-done | bytes 1179680 | tf_op jit(solution)/shard_map/ppermute | solution.py:506
  377.3 16.4 %collective-permute-done.63 = bf16[2,4,4,48,384]{4,3,2,1,0:T(8,128)(2,1)S(1)} collective-permute-done((bf16[2,4,4,48,384]{4,3,2,1,0:T(8,128)(2,1)S(1)}, bf16[2,4,4,48,384]{4,3,2,1,0:T(8,128)(2,1)S(1)}, u32[]{:S(2)}, u32[]{:S(2)}) %collective-permute-start.63) | collective-permute-done | bytes 1179680 | tf_op jit(solution)/shard_map/ppermute | solution.py:506
  396.3 16.4 %collective-permute-done.71 = bf16[2,4,4,48,384]{4,3,2,1,0:T(8,128)(2,1)S(1)} collective-permute-done((bf16[2,4,4,48,384]{4,3,2,1,0:T(8,128)(2,1)S(1)}, bf16[2,4,4,48,384]{4,3,2,1,0:T(8,128)(2,1)S(1)}, u32[]{:S(2)}, u32[]{:S(2)}) %collective-permute-start.71) | collective-permute-done | bytes 1179680 | tf_op jit(solution)/shard_map/ppermute | solution.py:506
  415.3 16.4 %collective-permute-done.80 = bf16[2,4,4,48,384]{4,3,2,1,0:T(8,128)(2,1)S(1)} collective-permute-done((bf16[2,4,4,48,384]{4,3,2,1,0:T(8,128)(2,1)S(1)}, bf16[2,4,4,48,384]{4,3,2,1,0:T(8,128)(2,1)S(1)}, u32[]{:S(2)}, u32[]{:S(2)}) %collective-permute-start.80) | collective-permute-done | bytes 1179680 | tf_op jit(solution)/shard_map/ppermute | solution.py:506
  434.2 16.4 %collective-permute-done.88 = bf16[2,4,4,48,384]{4,3,2,1,0:T(8,128)(2,1)S(1)} collective-permute-done((bf16[2,4,4,48,384]{4,3,2,1,0:T(8,128)(2,1)S(1)}, bf16[2,4,4,48,384]{4,3,2,1,0:T(8,128)(2,1)S(1)}, u32[]{:S(2)}, u32[]{:S(2)}) %collective-permute-start.88) | collective-permute-done | bytes 1179680 | tf_op jit(solution)/shard_map/ppermute | solution.py:506
  480.1 5.7 collective-permute-done.57
  (471 shorter events, 305.0 us)
Async XLA Ops:
  43.6 35.1 %collective-permute-start.7 = (bf16[2,3,4,48,384]{4,3,2,1,0:T(8,128)(2,1)S(1)}, bf16[2,3,4,48,384]{4,3,2,1,0:T(8,128)(2,1)S(1)}, u32[]{:S(2)}, u32[]{:S(2)}) collective-permute-start(bf16[2,3,4,48,384]{4,3,2,1,0:T(8,128)(2,1)S(1)} %pad_maximum_fusion.8), channel_id=1, source_target_pairs={{0,8},{4,12},{8,0},{12,4},{16,20},{20,16},{24,28},{28,24},{1,9},{5... | collective-permute-start | bytes 2654216 | tf_op jit(solution)/shard_map/ppermute | solution.py:506
  52.1 35.0 %collective-permute-start.15 = (bf16[2,3,4,48,384]{4,3,2,1,0:T(8,128)(2,1)}, bf16[2,3,4,48,384]{4,3,2,1,0:T(8,128)(2,1)}, u32[]{:S(2)}, u32[]{:S(2)}) collective-permute-start(bf16[2,3,4,48,384]{4,3,2,1,0:T(8,128)(2,1)} %pad_maximum_fusion.9), channel_id=1, source_target_pairs={{0,8},{4,12},{8,0},{12,4},{16,20},{20,16},{24,28},{28,24},{1,9},{5... | collective-permute-start | bytes 2654216 | tf_op jit(solution)/shard_map/ppermute | solution.py:506
  80.9 36.5 %collective-permute-start.23 = (bf16[2,3,4,48,384]{4,3,2,1,0:T(8,128)(2,1)}, bf16[2,3,4,48,384]{4,3,2,1,0:T(8,128)(2,1)}, u32[]{:S(2)}, u32[]{:S(2)}) collective-permute-start(bf16[2,3,4,48,384]{4,3,2,1,0:T(8,128)(2,1)} %pad_maximum_fusion.10), channel_id=1, source_target_pairs={{0,8},{4,12},{8,0},{12,4},{16,20},{20,16},{24,28},{28,24},{1,9},{5... | collective-permute-start | bytes 2654216 | tf_op jit(solution)/shard_map/ppermute | solution.py:506
  85.0 25.8 %collective-permute-start.32 = (bf16[4,48,384]{2,1,0:T(8,128)(2,1)}, bf16[4,48,384]{2,1,0:T(8,128)(2,1)S(1)}, u32[]{:S(2)}, u32[]{:S(2)}) collective-permute-start(bf16[4,48,384]{2,1,0:T(8,128)(2,1)} %get-tuple-element.88), channel_id=1, source_target_pairs={{0,2},{1,3},{2,0},{3,1},{4,6},{5,7},{6,4},{7,5},{8,10},{9,11},{10,... | collective-permute-start | bytes 442376 | tf_op jit(solution)/shard_map/ppermute | solution.py:511
  117.4 41.8 %collective-permute-start.8 = (bf16[4,3,4,48,384]{4,3,2,1,0:T(8,128)(2,1)}, bf16[4,3,4,48,384]{4,3,2,1,0:T(8,128)(2,1)}, u32[]{:S(2)}, u32[]{:S(2)}) collective-permute-start(bf16[4,3,4,48,384]{4,3,2,1,0:T(8,128)(2,1)} %pad_maximum_fusion.refs_4_), channel_id=1, source_target_pairs={{0,16},{16,0},{1,17},{17,1},{2,18},{18,2},{3,19},{19,3},{4,20},{20... | collective-permute-start | bytes 5308424 | tf_op jit(solution)/shard_map/ppermute | solution.py:493
  128.1 30.6 %collective-permute-start.9 = (bf16[1,192,3072]{2,1,0:T(8,128)(2,1)S(1)}, bf16[1,192,3072]{2,1,0:T(8,128)(2,1)}, u32[]{:S(2)}, u32[]{:S(2)}) collective-permute-start(bf16[1,192,3072]{2,1,0:T(8,128)(2,1)S(1)} %copy-done.2), channel_id=1, source_target_pairs={{0,16},{16,0},{1,17},{17,1},{2,18},{18,2},{3,19},{19,3},{4,20},{20... | collective-permute-start | bytes 3538952 | tf_op jit(solution)/shard_map/ppermute | solution.py:493
  144.7 56.5 %collective-permute-start.16 = (bf16[4,3,4,48,384]{4,3,2,1,0:T(8,128)(2,1)}, bf16[4,3,4,48,384]{4,3,2,1,0:T(8,128)(2,1)}, u32[]{:S(2)}, u32[]{:S(2)}) collective-permute-start(bf16[4,3,4,48,384]{4,3,2,1,0:T(8,128)(2,1)} %pad_maximum_fusion.1.refs_2_), channel_id=1, source_target_pairs={{0,16},{16,0},{1,17},{17,1},{2,18},{18,2},{3,19},{19,3},{4,20},{20... | collective-permute-start | bytes 5308424 | tf_op jit(solution)/shard_map/ppermute | solution.py:493
  146.5 54.6 %collective-permute-start.24 = (bf16[4,3,4,48,384]{4,3,2,1,0:T(8,128)(2,1)}, bf16[4,3,4,48,384]{4,3,2,1,0:T(8,128)(2,1)}, u32[]{:S(2)}, u32[]{:S(2)}) collective-permute-start(bf16[4,3,4,48,384]{4,3,2,1,0:T(8,128)(2,1)} %pad_maximum_fusion.3), channel_id=1, source_target_pairs={{0,16},{16,0},{1,17},{17,1},{2,18},{18,2},{3,19},{19,3},{4,20},{20... | collective-permute-start | bytes 5308424 | tf_op jit(solution)/shard_map/ppermute | solution.py:493
  156.0 54.7 %collective-permute-start.30 = (bf16[4,3,4,48,384]{4,3,2,1,0:T(8,128)(2,1)}, bf16[4,3,4,48,384]{4,3,2,1,0:T(8,128)(2,1)}, u32[]{:S(2)}, u32[]{:S(2)}) collective-permute-start(bf16[4,3,4,48,384]{4,3,2,1,0:T(8,128)(2,1)} %pad_maximum_fusion.4.refs_4_), channel_id=1, source_target_pairs={{0,16},{16,0},{1,17},{17,1},{2,18},{18,2},{3,19},{19,3},{4,20},{20... | collective-permute-start | bytes 5308424 | tf_op jit(solution)/shard_map/ppermute | solution.py:493
  158.6 62.0 %collective-permute-start.36 = (bf16[4,3,4,48,384]{4,3,2,1,0:T(8,128)(2,1)}, bf16[4,3,4,48,384]{4,3,2,1,0:T(8,128)(2,1)S(1)}, u32[]{:S(2)}, u32[]{:S(2)}) collective-permute-start(bf16[4,3,4,48,384]{4,3,2,1,0:T(8,128)(2,1)} %pad_maximum_fusion.5.refs_2_), channel_id=1, source_target_pairs={{0,16},{16,0},{1,17},{17,1},{2,18},{18,2},{3,19},{19,3},{4,20},{20... | collective-permute-start | bytes 5308424 | tf_op jit(solution)/shard_map/ppermute | solution.py:493
  159.2 61.5 %collective-permute-start.42 = (bf16[4,3,4,48,384]{4,3,2,1,0:T(8,128)(2,1)}, bf16[4,3,4,48,384]{4,3,2,1,0:T(8,128)(2,1)}, u32[]{:S(2)}, u32[]{:S(2)}) collective-permute-start(bf16[4,3,4,48,384]{4,3,2,1,0:T(8,128)(2,1)} %pad_maximum_fusion.7), channel_id=1, source_target_pairs={{0,16},{16,0},{1,17},{17,1},{2,18},{18,2},{3,19},{19,3},{4,20},{20... | collective-permute-start | bytes 5308424 | tf_op jit(solution)/shard_map/ppermute | solution.py:493
  287.1 54.3 %collective-permute-start.45 = (bf16[4,4,4,48,384]{4,3,2,1,0:T(8,128)(2,1)}, bf16[4,4,4,48,384]{4,3,2,1,0:T(8,128)(2,1)S(1)}, u32[]{:S(2)}, u32[]{:S(2)}) collective-permute-start(bf16[4,4,4,48,384]{4,3,2,1,0:T(8,128)(2,1)} %get-tuple-element.116), channel_id=1, source_target_pairs={{0,16},{16,0},{1,17},{17,1},{2,18},{18,2},{3,19},{19,3},{4,20},{20... | collective-permute-start | bytes 7077896 | tf_op jit(solution)/shard_map/ppermute | solution.py:493
  289.3 56.2 %collective-permute-start.53 = (bf16[4,4,4,48,384]{4,3,2,1,0:T(8,128)(2,1)}, bf16[4,4,4,48,384]{4,3,2,1,0:T(8,128)(2,1)}, u32[]{:S(2)}, u32[]{:S(2)}) collective-permute-start(bf16[4,4,4,48,384]{4,3,2,1,0:T(8,128)(2,1)} %get-tuple-element.118), channel_id=1, source_target_pairs={{0,16},{16,0},{1,17},{17,1},{2,18},{18,2},{3,19},{19,3},{4,20},{20... | collective-permute-start | bytes 7077896 | tf_op jit(solution)/shard_map/ppermute | solution.py:493
  289.5 60.9 %collective-permute-start.62 = (bf16[4,4,4,48,384]{4,3,2,1,0:T(8,128)(2,1)}, bf16[4,4,4,48,384]{4,3,2,1,0:T(8,128)(2,1)}, u32[]{:S(2)}, u32[]{:S(2)}) collective-permute-start(bf16[4,4,4,48,384]{4,3,2,1,0:T(8,128)(2,1)} %get-tuple-element.122), channel_id=1, source_target_pairs={{0,16},{16,0},{1,17},{17,1},{2,18},{18,2},{3,19},{19,3},{4,20},{20... | collective-permute-start | bytes 7077896 | tf_op jit(solution)/shard_map/ppermute | solution.py:493
  290.0 63.8 %collective-permute-start.70 = (bf16[4,4,4,48,384]{4,3,2,1,0:T(8,128)(2,1)}, bf16[4,4,4,48,384]{4,3,2,1,0:T(8,128)(2,1)}, u32[]{:S(2)}, u32[]{:S(2)}) collective-permute-start(bf16[4,4,4,48,384]{4,3,2,1,0:T(8,128)(2,1)} %get-tuple-element.124), channel_id=1, source_target_pairs={{0,16},{16,0},{1,17},{17,1},{2,18},{18,2},{3,19},{19,3},{4,20},{20... | collective-permute-start | bytes 7077896 | tf_op jit(solution)/shard_map/ppermute | solution.py:493
  295.3 62.1 %collective-permute-start.79 = (bf16[4,4,4,48,384]{4,3,2,1,0:T(8,128)(2,1)}, bf16[4,4,4,48,384]{4,3,2,1,0:T(8,128)(2,1)}, u32[]{:S(2)}, u32[]{:S(2)}) collective-permute-start(bf16[4,4,4,48,384]{4,3,2,1,0:T(8,128)(2,1)} %bitcast.292), channel_id=1, source_target_pairs={{0,16},{16,0},{1,17},{17,1},{2,18},{18,2},{3,19},{19,3},{4,20},{20... | collective-permute-start | bytes 7077896 | tf_op jit(solution)/shard_map/ppermute | solution.py:493
  353.9 39.9 %collective-permute-start.63 = (bf16[2,4,4,48,384]{4,3,2,1,0:T(8,128)(2,1)S(1)}, bf16[2,4,4,48,384]{4,3,2,1,0:T(8,128)(2,1)S(1)}, u32[]{:S(2)}, u32[]{:S(2)}) collective-permute-start(bf16[2,4,4,48,384]{4,3,2,1,0:T(8,128)(2,1)S(1)} %get-tuple-element.134), channel_id=1, source_target_pairs={{0,4},{4,0},{8,12},{12,8},{16,24},{20,28},{24,16},{28,20},{1,5},{5... | collective-permute-start | bytes 3538952 | tf_op jit(solution)/shard_map/ppermute | solution.py:506
  357.4 55.2 %collective-permute-start.71 = (bf16[2,4,4,48,384]{4,3,2,1,0:T(8,128)(2,1)S(1)}, bf16[2,4,4,48,384]{4,3,2,1,0:T(8,128)(2,1)S(1)}, u32[]{:S(2)}, u32[]{:S(2)}) collective-permute-start(bf16[2,4,4,48,384]{4,3,2,1,0:T(8,128)(2,1)S(1)} %get-tuple-element.136), channel_id=1, source_target_pairs={{0,4},{4,0},{8,12},{12,8},{16,24},{20,28},{24,16},{28,20},{1,5},{5... | collective-permute-start | bytes 3538952 | tf_op jit(solution)/shard_map/ppermute | solution.py:506
  360.7 70.9 %collective-permute-start.80 = (bf16[2,4,4,48,384]{4,3,2,1,0:T(8,128)(2,1)S(1)}, bf16[2,4,4,48,384]{4,3,2,1,0:T(8,128)(2,1)S(1)}, u32[]{:S(2)}, u32[]{:S(2)}) collective-permute-start(bf16[2,4,4,48,384]{4,3,2,1,0:T(8,128)(2,1)S(1)} %get-tuple-element.144), channel_id=1, source_target_pairs={{0,4},{4,0},{8,12},{12,8},{16,24},{20,28},{24,16},{28,20},{1,5},{5... | collective-permute-start | bytes 3538952 | tf_op jit(solution)/shard_map/ppermute | solution.py:506
  362.7 87.9 %collective-permute-start.88 = (bf16[2,4,4,48,384]{4,3,2,1,0:T(8,128)(2,1)S(1)}, bf16[2,4,4,48,384]{4,3,2,1,0:T(8,128)(2,1)S(1)}, u32[]{:S(2)}, u32[]{:S(2)}) collective-permute-start(bf16[2,4,4,48,384]{4,3,2,1,0:T(8,128)(2,1)S(1)} %get-tuple-element.150), channel_id=1, source_target_pairs={{0,4},{4,0},{8,12},{12,8},{16,24},{20,28},{24,16},{28,20},{1,5},{5... | collective-permute-start | bytes 3538952 | tf_op jit(solution)/shard_map/ppermute | solution.py:506
  374.7 78.4 %collective-permute-start.47 = (bf16[1,4,4,48,384]{4,3,2,1,0:T(8,128)(2,1)S(1)}, bf16[1,4,4,48,384]{4,3,2,1,0:T(8,128)(2,1)S(1)}, u32[]{:S(2)}, u32[]{:S(2)}) collective-permute-start(bf16[1,4,4,48,384]{4,3,2,1,0:T(8,128)(2,1)S(1)} %get-tuple-element.158), channel_id=1, source_target_pairs={{0,8},{4,12},{8,0},{12,4},{16,20},{20,16},{24,28},{28,24},{1,9},{5... | collective-permute-start | bytes 1769480 | tf_op jit(solution)/shard_map/ppermute | solution.py:506
  393.7 59.7 %collective-permute-start.55 = (bf16[1,4,4,48,384]{4,3,2,1,0:T(8,128)(2,1)S(1)}, bf16[1,4,4,48,384]{4,3,2,1,0:T(8,128)(2,1)S(1)}, u32[]{:S(2)}, u32[]{:S(2)}) collective-permute-start(bf16[1,4,4,48,384]{4,3,2,1,0:T(8,128)(2,1)S(1)} %get-tuple-element.160), channel_id=1, source_target_pairs={{0,8},{4,12},{8,0},{12,4},{16,20},{20,16},{24,28},{28,24},{1,9},{5... | collective-permute-start | bytes 1769480 | tf_op jit(solution)/shard_map/ppermute | solution.py:506
  412.7 42.9 %collective-permute-start.64 = (bf16[1,4,4,48,384]{4,3,2,1,0:T(8,128)(2,1)S(1)}, bf16[1,4,4,48,384]{4,3,2,1,0:T(8,128)(2,1)S(1)}, u32[]{:S(2)}, u32[]{:S(2)}) collective-permute-start(bf16[1,4,4,48,384]{4,3,2,1,0:T(8,128)(2,1)S(1)} %get-tuple-element.154), channel_id=1, source_target_pairs={{0,8},{4,12},{8,0},{12,4},{16,20},{20,16},{24,28},{28,24},{1,9},{5... | collective-permute-start | bytes 1769480 | tf_op jit(solution)/shard_map/ppermute | solution.py:506
  471.6 25.7 %collective-permute-start.66 = (bf16[4,48,384]{2,1,0:T(8,128)(2,1)S(1)}, bf16[4,48,384]{2,1,0:T(8,128)(2,1)S(1)}, u32[]{:S(2)}, u32[]{:S(2)}) collective-permute-start(bf16[4,48,384]{2,1,0:T(8,128)(2,1)S(1)} %get-tuple-element.175), channel_id=1, source_target_pairs={{0,2},{1,3},{2,0},{3,1},{4,6},{5,7},{6,4},{7,5},{8,10},{9,11},{10,... | collective-permute-start | bytes 442376 | tf_op jit(solution)/shard_map/ppermute | solution.py:511
  (152 other events, 2050.2 us)

commit v2 on v1

--- a/solution.py
+++ b/solution.py
@@ -78,6 +78,21 @@
     return tables
 
 
+def row_masks(rows):
+    bits = [1 << i for i in reversed(range(rows.bit_length() - 1))]
+    return [sum(b for t, b in enumerate(bits) if (k >> t) & 1) for k in range(rows)]
+
+
+def row_to(plan, row, k):
+    return row ^ row_masks(plan.rows)[k] if plan.few else (row + k) % plan.rows
+
+
+def row_from(plan, row, k):
+    if plan.few:
+        return row ^ row_masks(plan.rows)[k + 1]
+    return (row + (plan.rows - 1 - k)) % plan.rows
+
+
 def pick(flag, a, b):
     return a if a == b else jnp.where(flag, a, b)
 
@@ -91,6 +106,7 @@
         self.pieces = groups * rows
         self.tall = width // self.pieces
         self.direct = self.tall % 16 == 0
+        self.few = rows <= 4 and rows & (rows - 1) == 0
 
 
 def start_weights(plan, layer, kind, ids, own, others, whole, dst, sem):
@@ -130,19 +146,19 @@
         from_shard(theirs)
 
     tables = masks_of(plan.groups, True)
-    for source, flag in zip(others, (core == 0, core != 0)):
-        half = core if source is others[0] else 1 - core
+    for half, flag, sources in ((core, core == 0, others[:2]), (1 - core, core != 0, others[2:])):
         lanes = pl.ds(pl.multiple_of(half * BLOCK, LANES), BLOCK)
         for j in range(plan.groups):
             peer = group ^ pick(flag, tables[0][j], tables[1][j])
+            source = sources[j // (plan.groups // 2)]
             for k in range(plan.rows - 1):
-                at = ((row + (plan.rows - 1 - k)) % plan.rows) * plan.groups + peer
+                at = row_from(plan, row, k) * plan.groups + peer
                 if kind == "down":
                     at = pl.multiple_of(at * (tall * PARTS), 16)
                     to = dst.at[pl.ds(at, tall * PARTS), lanes]
                 else:
                     to = dst.at[:, pl.ds(pl.multiple_of(at * tall, 16), tall), lanes]
-                pltpu.make_async_copy(source.at[j, k], to, sem).start()
+                pltpu.make_async_copy(source.at[j % (plan.groups // 2), k], to, sem).start()
 
 
 def wait_all(ref, sem):
@@ -166,7 +182,7 @@
         for j in range(plan.groups):
             peer = group ^ pick(flag, tables[0][j], tables[1][j])
             for k in range(plan.rows):
-                at = ((row + k) % plan.rows) * plan.groups + peer
+                at = row_to(plan, row, k) * plan.groups + peer
                 if kind == "down":
                     part = src.at[pl.ds(pl.multiple_of(at * (tall * PARTS), 16), tall * PARTS), lanes]
                 else:
@@ -350,11 +366,47 @@
     wait_all(g, sem_g)
 
 
+def pack(plan, ids, qkv, out, up, down, keep, send):
+    width, tall = plan.width, plan.tall
+    first = ids[0] == 0
+    at = 0
+    for ref in (qkv, out, up, down):
+        for b in range(PARTS if ref is down else ref.shape[2] // width):
+            if ref is down:
+                block = ref[0, b * tall : (b + 1) * tall, :]
+            else:
+                block = ref[0, :, b * width : (b + 1) * width]
+            low, high = block[:, :BLOCK], block[:, BLOCK:]
+            keep[at] = jnp.where(first, low, high)
+            send[at] = jnp.where(first, high, low)
+            at += 1
+
+
+def final_layout(plan, kind, ids, x, *outs):
+    width, tall = plan.width, plan.tall
+    core, group = ids[0], ids[1]
+    tables = masks_of(plan.groups, False)
+    for j in range(plan.groups):
+        peer = group ^ pick(core == 0, tables[0][j], tables[1][j])
+        for h in range(2):
+            for b in range(PARTS):
+                value = x[j, h ^ core, b].astype(jnp.float32)
+                if kind == "down":
+                    at = pl.multiple_of(peer * (tall * PARTS) + b * tall, 8)
+                    outs[0][0, pl.ds(at, tall), h * BLOCK : (h + 1) * BLOCK] = value
+                    continue
+                at = pl.multiple_of(peer * tall, 8)
+                out = outs[-1] if kind == "attend" and b == PARTS - 1 else outs[0]
+                c = 0 if kind == "attend" and b == PARTS - 1 else b
+                lanes = slice(c * width + h * BLOCK, c * width + (h + 1) * BLOCK)
+                out[0, pl.ds(at, tall), lanes] = value
+
+
 SHARDS = {"attend": 2, "up": 1, "down": 1}
 
 
 def plan_inputs(plan, kind):
-    return 2 * SHARDS[kind] + 2 if plan.direct else 1
+    return 2 * SHARDS[kind] + 4 if plan.direct else 1
 
 
 def weight_refs(plan, kind, refs):
@@ -363,6 +415,11 @@
     n = SHARDS[kind]
     return (refs[:n], refs[n : 2 * n]), refs[2 * n :], None
 
+
+DEPTH = 2
+DEPTH_BACK = 3
+SHIFT = 0
+ROWS_FIRST = ()
 
 VMEM = pl.BlockSpec(memory_space=pltpu.VMEM)
 SMEM = pl.BlockSpec(memory_space=pltpu.SMEM)
@@ -489,6 +546,40 @@
         )
 
 
+    def pack(self, shards):
+        p = self.plan
+        dims = (3 * PARTS, p.tall, BLOCK)
+        specs = []
+        for i, w in enumerate(shards):
+            tall = p.tall * PARTS if i == len(shards) - 1 else p.tall
+            specs.append(pl.BlockSpec((1, tall, w.shape[2]), lambda i, ids: (0, ids[1], 0)))
+        whole = pl.BlockSpec(dims, lambda i, ids: (0, 0, 0))
+        return pl.pallas_call(
+            functools.partial(pack, p),
+            out_shape=(shape(dims, BF),) * 2,
+            grid_spec=pltpu.PrefetchScalarGridSpec(
+                num_scalar_prefetch=1, grid=(1,), in_specs=specs, out_specs=(whole, whole)
+            ),
+            name="pack",
+        )(self.ids, *shards)
+
+    def final(self, kind, x):
+        p = self.plan
+        share, d = p.width // p.rows, p.width
+        dims = {"attend": ((share, 3 * d), (share, d)), "up": ((share, PARTS * d),), "down": ((share * PARTS, d),)}
+        outs = tuple(shape((1, *dim), F32) for dim in dims[kind])
+        return call(
+            functools.partial(final_layout, p, kind),
+            f"final_{kind}",
+            (self.ids, x),
+            [SMEM, VMEM],
+            outs,
+            (VMEM,) * len(outs),
+            [],
+            0,
+        )
+
+
 def swap_cores(x):
     return lax.ppermute(x, "section", [(0, 1), (1, 0)])
 
@@ -513,6 +604,11 @@
 
 def gate(x, after):
     return lax.optimization_barrier((x, *after))[0] if after else x
+
+
+def swap_rows(x, bit):
+    rows = lax.axis_size("dp")
+    return lax.ppermute(x, "dp", [(i, i ^ bit) for i in range(rows)])
 
 
 KINDS = ("attend", "up", "down")
@@ -548,7 +644,8 @@
             own.append(w)
         own = jnp.concatenate(own, axis=1)[:, None]
         got = jnp.concatenate([got, own], axis=1)
-        got = jnp.take(got, (row - 1 - jnp.arange(rows)) % rows, axis=1)
+        held = jnp.stack([row_from(plan, row, k) for k in range(rows - 1)] + [row])
+        got = jnp.take(got, jnp.argsort(held), axis=1)
         if kind == "down":
             halves.append(got.transpose(1, 0, 2, 3, 4).reshape(PARTS * plan.width, BLOCK))
         else:
@@ -566,7 +663,7 @@
         else:
             x = x.reshape(PARTS, rows, groups, tall, BLOCK).transpose(2, 1, 0, 3, 4)
         x = jnp.take(x, group ^ jnp.where(half == 0, tables[0], tables[1]), axis=0)
-        x = jnp.take(x, (row + jnp.arange(rows)) % rows, axis=1)
+        x = jnp.take(x, jnp.stack([row_to(plan, row, k) for k in range(rows)]), axis=1)
         outs.append(x)
     return outs
 
@@ -592,94 +689,240 @@
     stages = groups.bit_length() - 1
     tok, width = tokens.shape[1:]
     plan = Plan(groups, rows, tok, width)
-    few = rows <= 4
+    few = plan.few
     first = core == 0
     share = width // rows
     ids = jnp.stack([core, group, row]).astype(jnp.int32)
     lens = lax.dynamic_index_in_dim(lengths, core, 0, False)[0]
 
     shards = {"attend": (qkv_weight, out_weight), "up": (up_weight,), "down": (down_weight,)}
-    pieces = {}
-    for kind in KINDS:
-        both = piece_of(plan, group, kind, shards[kind])
-        keep = lax.dynamic_index_in_dim(both, core, 0, False)
-        got = swap_cores(lax.dynamic_index_in_dim(both, 1 - core, 0, False))
-        pieces[0, kind] = jnp.where(first, keep, got)
-        pieces[1, kind] = jnp.where(first, got, keep)
-    theirs = {}
     chunks = [(layer, kind) for layer in range(2) for kind in KINDS]
-    history = []
-    bufs = {}
-    for slot in range(len(chunks) + stages):
-        after = history[slot - DEPTH] if slot >= DEPTH else []
-        done = []
-        for stage in range(stages, 0, -1):
-            c = slot - stage
-            if 0 <= c < len(chunks):
-                got = swap_groups(gate(bufs[c], after), groups, stage - 1)
-                bufs[c] = jnp.concatenate([bufs[c], got], axis=0)
-                done.append(got)
-        if slot < len(chunks):
-            piece = gate(pieces[chunks[slot]], after)
-            if few:
-                got = [along(piece, k) for k in range(1, rows)]
-                bufs[slot] = jnp.stack(got)[None]
-            else:
-                got = [lax.all_gather(piece, "dp")]
-                back = (row - 1 - jnp.arange(rows - 1)) % rows
-                bufs[slot] = jnp.take(got[0], back, axis=0)[None]
-            done += got
-        if slot == 0:
-            small = jnp.stack([attend_gain[0], attend_bias[0], feed_gain[0], feed_bias[0]])
-            smalls = lax.all_gather(gate(small, done[:1]), ("section", "dp"))
-            smalls = smalls.reshape(2, rows, PARTS, share).transpose(0, 2, 1, 3)
-            smalls = smalls.reshape(2, PARTS, width).astype(F32)
-        if slot == 1:
-            for kind in KINDS:
-                theirs[kind] = tuple(swap_cores(gate(w, done[:1])) for w in shards[kind])
-        history.append(done)
-    gathered = {}
-    for c, (layer, kind) in enumerate(chunks):
-        mine = bufs[c]
-        other = swap_cores(mine)
-        if plan.direct:
-            if kind == "down":
-                flat = (groups, rows - 1, PARTS * plan.tall, BLOCK)
-                mine, other = mine.reshape(flat), other.reshape(flat)
-            gathered[layer, kind] = (*shards[kind], *theirs[kind], mine, other)
-        else:
-            shard = [jnp.where(core == layer, a, b) for a, b in zip(shards[kind], theirs[kind])]
-            gathered[layer, kind] = (
-                whole_of(plan, core, group, row, kind, shard, mine, other),
-            )
-
+    n_chunks = len(chunks)
     x0 = lax.dynamic_index_in_dim(tokens, core, 0, False)
     cot = lax.dynamic_index_in_dim(cotangent, core, 0, False)
     cosine, sine, _ = rope_tables(lens, tok)
     kernels = Kernels(plan, ids, lens, (cosine, sine), width // HEAD_DIM)
-    xs, saved = [x0], []
+    history = {}
+    pieces, bufs, gots, theirs, saved = {}, {}, {}, {}, {}
+    xs = {0: x0}
+    small = jnp.stack([attend_gain[0], attend_bias[0], feed_gain[0], feed_bias[0]])[None]
+
+    if plan.direct:
+        keep, send = kernels.pack([w for kind in KINDS for w in shards[kind]])
+    else:
+        both = jnp.concatenate([piece_of(plan, group, kind, shards[kind]) for kind in KINDS], axis=1)
+        keep = lax.dynamic_index_in_dim(both, core, 0, False)
+        send = lax.dynamic_index_in_dim(both, 1 - core, 0, False)
+    got = swap_cores(send)
     for layer in range(2):
-        a = kernels.attend_forward(layer, xs[layer], smalls[layer], gathered[layer, "attend"])
-        weights = gathered[layer, "up"] + gathered[layer, "down"]
-        f = kernels.feed_forward(layer, a[4], smalls[layer], weights)
-        xs.append(f[3])
-        saved.append((a, f))
-    grads, sums, backs = {}, {}, [None, None]
-    d_out = cot
-    for layer in (1, 0):
-        (normed, qkv, probs, mixed, resid), (normed_two, active, slope, _) = saved[layer]
-        grads[layer, "down"] = kernels.down_grad(layer, active, d_out)
-        weights = gathered[layer, "up"] + gathered[layer, "down"]
-        *g, d_resid, sums_two = kernels.feed_backward(
-            layer, d_out, resid, normed_two, slope, smalls[layer], weights
+        part = jnp.where(core == layer, keep, got)
+        for i, kind in enumerate(KINDS):
+            pieces[layer, kind] = part[i * PARTS : (i + 1) * PARTS][None, None]
+
+    def weights_of(layer, kind):
+        parts = [*bufs[layer, kind], *gots[layer, kind]]
+        if plan.direct:
+            if kind == "down":
+                parts = [p.reshape(*p.shape[:2], PARTS * plan.tall, BLOCK) for p in parts]
+            return (*shards[kind], *theirs[kind], *parts)
+        mine, other = (jnp.concatenate(p, axis=0) for p in (parts[:2], parts[2:]))
+        shard = [jnp.where(core == layer, a, b) for a, b in zip(shards[kind], theirs[kind])]
+        return (whole_of(plan, core, group, row, kind, shard, mine, other),)
+
+    def run_attend(layer, after):
+        x = gate(xs[layer], after)
+        out = kernels.attend_forward(layer, x, smalls[layer], weights_of(layer, "attend"))
+        saved[layer, "attend"] = out
+        return out[4]
+
+    def run_feed(layer, after):
+        resid = gate(saved[layer, "attend"][4], after)
+        weights = weights_of(layer, "up") + weights_of(layer, "down")
+        *out, y = kernels.feed_forward(layer, resid, smalls[layer], weights)
+        saved[layer, "feed"] = out
+        xs[layer + 1] = y
+        return y
+
+    row_bits = [1 << i for i in range(rows.bit_length() - 1)]
+    hops = len(row_bits) if few else 1
+    depth = hops + stages
+    kernel_at = {depth + SHIFT: (run_attend, 0), depth + 2 + SHIFT: (run_feed, 0), depth + 3 + SHIFT: (run_attend, 1)}
+    small_steps = row_bits + [0]
+    gotten = {}
+    for slot in range(n_chunks + depth + 1):
+        after = history.get(slot - DEPTH, [])
+        done = []
+        for stage in range(depth, -1, -1):
+            c = slot - stage
+            if not 0 <= c < n_chunks:
+                continue
+            chunk = chunks[c]
+            if stage == depth:
+                gots[chunk].append(swap_cores(gate(bufs[chunk][1], after)))
+                done.append(gots[chunk][-1])
+                continue
+            if stage < hops:
+                piece = pieces[chunk]
+                if few:
+                    got = swap_rows(gate(piece, after), row_bits[hops - 1 - stage])
+                    pieces[chunk] = jnp.concatenate([piece, got], axis=1)
+                    gotten.setdefault(chunk, []).append(got)
+                else:
+                    got = lax.all_gather(gate(piece[0, 0], after), "dp")
+                    back = (row - 1 - jnp.arange(rows - 1)) % rows
+                    gotten[chunk] = [jnp.take(got, back, axis=0)[None]]
+                done.append(got)
+                continue
+            if stage == hops:
+                bufs[chunk] = jnp.concatenate(gotten[chunk], axis=1)
+            buf = bufs[chunk]
+            got = swap_groups(gate(buf, after), groups, stage - hops)
+            done.append(got)
+            if stage + 1 < depth:
+                bufs[chunk] = jnp.concatenate([buf, got], axis=0)
+            else:
+                bufs[chunk] = [buf, got]
+                gots[chunk] = [swap_cores(gate(buf, after))]
+                done.append(gots[chunk][0])
+        if few and slot < len(small_steps):
+            bit = small_steps[slot]
+            held = gate(small, history.get(slot - 1, []))
+            got = swap_rows(held, bit) if bit else swap_cores(held)
+            done.append(got)
+            small = jnp.concatenate([small, got])
+        elif slot == 0:
+            small = lax.all_gather(small, ("section", "dp"))
+        if slot == (len(small_steps) if few else 1):
+            got = small.reshape(2, rows, PARTS, share)
+            if few:
+                got = jnp.take(got, row ^ jnp.arange(rows), axis=1)
+                got = jnp.take(got, core ^ jnp.arange(2), axis=0)
+            smalls = got.transpose(0, 2, 1, 3).reshape(2, PARTS, width).astype(F32)
+        if 1 <= slot <= len(KINDS):
+            kind = KINDS[slot - 1]
+            theirs[kind] = tuple(swap_cores(gate(w, history[slot - 1])) for w in shards[kind])
+            done += theirs[kind]
+        if slot in kernel_at:
+            run, layer = kernel_at[slot]
+            done.append(run(layer, history[slot - 1]))
+        history[slot] = done
+    run_feed(1, [])
+
+    grads, backs, sums = {}, [None, None], {}
+    order = [(layer, kind) for layer in (1, 0) for kind in ("down", "up", "attend")]
+
+    def run_backward(flow, layer, kind, after):
+        normed, qkv, probs, mixed, resid = saved[layer, "attend"]
+        normed_two, active, slope = saved[layer, "feed"]
+        d_out, d_resid = flow
+        if kind == "down":
+            return kernels.down_grad(layer, active, gate(d_out, after)), flow
+        if kind == "up":
+            weights = weights_of(layer, "up") + weights_of(layer, "down")
+            *g, d_resid, sums[layer, kind] = kernels.feed_backward(
+                layer, gate(d_out, after), resid, normed_two, slope, smalls[layer], weights
+            )
+            return g, (d_out, d_resid)
+        *g, d_x, sums[layer, kind] = kernels.attend_backward(
+            layer,
+            xs[layer],
+            gate(d_resid, after),
+            normed,
+            qkv,
+            probs,
+            mixed,
+            smalls[layer],
+            weights_of(layer, "attend"),
         )
-        grads[layer, "up"] = g
-        *g, d_out, sums_one = kernels.attend_backward(
-            layer, xs[layer], d_resid, normed, qkv, probs, mixed, smalls[layer], gathered[layer, "attend"]
-        )
-        grads[layer, "attend"] = g
-        sums[layer] = jnp.concatenate([sums_one, sums_two])
-        backs[layer] = d_out
+        backs[layer] = d_x
+        return g, (d_x, d_resid)
+
+    def total_of(parts):
+        total = parts[0].astype(F32)
+        for part in parts[1:]:
+            total = total + part.astype(F32)
+        return total.astype(BF)
+
+    def ready(kind, keep, send):
+        if plan.direct:
+            dims = (groups, rows, PARTS, plan.tall, BLOCK)
+            return {"sum": [keep.reshape(dims), send.reshape(dims)]}
+        return {"sum": ordered_grads(plan, kind, core, group, row, keep, send)}
+
+    def way_of(kind):
+        over_groups = [(0, i) for i in range(stages)]
+        over_rows = [(1, bit) for bit in row_bits] if few else [(1, 0)]
+        return over_rows + over_groups if few and kind in ROWS_FIRST else over_groups + over_rows
+
+    last = 1 + stages + hops
+
+    def step(kind, parts, stage, after):
+        if stage == 0:
+            parts["sum"] = [parts["sum"][0], swap_cores(gate(parts["sum"][1], after))]
+            parts["left"] = [groups, rows]
+            return parts["sum"][1]
+        axis, bit = way_of(kind)[stage - 1]
+        if axis == 1 and not few:
+            send = total_of([p[0] for p in parts["sum"]])
+            held = jnp.argsort(jnp.stack([row_to(plan, row, k) for k in range(rows)]))
+            send = gate(jnp.take(send, held, axis=0), after)
+            got = lax.psum_scatter(send, "dp", scatter_dimension=0, tiled=True)
+            parts["sum"] = [got[None]]
+            parts["left"] = [1, 1]
+            return got
+        low, high = [0, 0], list(parts["left"])
+        low[axis] = high[axis] // 2
+        send = total_of([p[low[0] : high[0], low[1] : high[1]] for p in parts["sum"]])
+        parts["left"][axis] //= 2
+        send = gate(send, after)
+        got = swap_groups(send, groups, bit) if axis == 0 else swap_rows(send, bit)
+        parts["sum"] = parts["sum"] + [got]
+        return got
+
+    def result_of(parts):
+        return total_of([p[:1, 0] for p in parts["sum"]])
+
+    history = {}
+    flow = (cot, None)
+    g, flow = run_backward(flow, *order[0], [])
+    live = {0: ready(order[0][1], *g)}
+    final = {}
+    small_sum, small_stage = None, 0
+    for slot in range(n_chunks + last + stages + 1):
+        after = history.get(slot - DEPTH_BACK, [])
+        done = []
+        for c in range(n_chunks):
+            if 0 <= slot - c < last:
+                done.append(step(order[c][1], live[c], slot - c, after))
+        for i, kind in enumerate(("down", "up", "attend")):
+            stage = slot - (i + len(KINDS) + last)
+            if stage == 0:
+                low, high = (result_of(live[order.index((layer, kind))]) for layer in range(2))
+                other = swap_cores(jnp.where(first, high, low))
+                final[kind] = jnp.stack([jnp.where(first, low, high), other], axis=1)
+                done.append(other)
+            elif 1 <= stage <= stages:
+                got = swap_groups(gate(final[kind], after), groups, stages - stage)
+                final[kind] = jnp.concatenate([final[kind], got], axis=0)
+                done.append(got)
+        if slot + 1 < n_chunks:
+            layer, kind = order[slot + 1]
+            g, flow = run_backward(flow, layer, kind, history.get(slot - 1, []))
+            live[slot + 1] = ready(kind, *g)
+            done.append(flow[0] if kind == "attend" else flow[1] if kind == "up" else g[0])
+        if slot + 1 == n_chunks:
+            small_sum = jnp.stack([jnp.concatenate([sums[i, "attend"], sums[i, "up"]]) for i in range(2)])
+        if small_sum is not None and small_stage <= stages + len(row_bits):
+            held = gate(small_sum, history.get(slot - 1, []))
+            if small_stage == 0:
+                got = swap_cores(held)
+            elif small_stage <= stages:
+                got = swap_groups(held, groups, small_stage - 1)
+            else:
+                got = swap_rows(held, row_bits[small_stage - stages - 1])
+            small_stage += 1
+            small_sum = small_sum + got
+        history[slot] = done
 
     def home(low, high):
         got = swap_cores(jnp.where(first, high, low))
@@ -689,61 +932,25 @@
     layer_out = home(xs[1], xs[2])
     input_grad = home(*backs)
 
-    def add(a, b):
-        return (a.astype(F32) + b.astype(F32)).astype(BF)
-
-    def reduce(kind, keep, send):
-        if plan.direct:
-            dims = (groups, rows, PARTS, plan.tall, BLOCK)
-            keep, send = keep.reshape(dims), send.reshape(dims)
-        else:
-            keep, send = ordered_grads(plan, kind, core, group, row, keep, send)
-        got = swap_cores(send)
-        for stage in range(stages):
-            half = keep.shape[0] // 2
-            high = add(keep[half:], got[half:])
-            keep = add(keep[:half], got[:half])
-            got = swap_groups(high, groups, stage)
-        keep, got = keep[0], got[0]
-        if few:
-            moved = [along(add(keep[k], got[k]), k) for k in range(1, rows)]
-            total = keep[0].astype(F32) + got[0].astype(F32)
-            for m in moved:
-                total = total + m.astype(F32)
-        else:
-            total = add(keep, got)
-            total = jnp.take(total, (jnp.arange(rows) - row) % rows, axis=0)
-            total = lax.psum_scatter(total, "dp", scatter_dimension=0, tiled=False)
-        total = total.astype(BF)[None]
-        for stage in range(stages - 1, -1, -1):
-            total = jnp.concatenate([total, swap_groups(total, groups, stage)], axis=0)
-        return total
-
-    reduced = {}
-    for layer in (1, 0):
-        for kind in ("down", "up", "attend"):
-            reduced[layer, kind] = reduce(kind, *grads[layer, kind])
-    tables = jnp.array(masks_of(groups, False), jnp.int32)
-    final = {}
-    for kind in KINDS:
-        own = jnp.where(first, reduced[0, kind], reduced[1, kind])
-        other = swap_cores(jnp.where(first, reduced[1, kind], reduced[0, kind]))
-        low = jnp.where(first, own, other)
-        high = jnp.where(first, other, own)
-        low = jnp.take(low, jnp.argsort(group ^ tables[0]), axis=0)
-        high = jnp.take(high, jnp.argsort(group ^ tables[1]), axis=0)
-        final[kind] = jnp.stack([low, high])
-
     def outside(x):
-        return x.transpose(1, 3, 2, 0, 4).reshape(share, -1).astype(F32)
-
-    qkv_grad = outside(final["attend"][:, :, 0:3])
-    out_grad = outside(final["attend"][:, :, 3:4])
-    up_grad = outside(final["up"])
-    down_grads = final["down"].transpose(1, 2, 3, 0, 4).reshape(-1, width).astype(F32)
-
-    small_grads = jnp.stack([sums[0], sums[1]])
-    small_grads = lax.psum(small_grads, ("section", "group", "dp"))
+        return x.transpose(0, 3, 2, 1, 4).reshape(1, share, -1).astype(F32)
+
+    if plan.direct:
+        qkv_grad, out_grad = kernels.final("attend", final["attend"])
+        (up_grad,) = kernels.final("up", final["up"])
+        (down_grads,) = kernels.final("down", final["down"])
+    else:
+        tables = jnp.array(masks_of(groups, False), jnp.int32)
+        at = jnp.argsort(group ^ jnp.where(first, tables[0], tables[1]))
+        for kind in KINDS:
+            x = jnp.take(final[kind], at, axis=0)
+            final[kind] = jnp.take(x, jnp.arange(2) ^ core, axis=1)
+        qkv_grad = outside(final["attend"][:, :, 0:3])
+        out_grad = outside(final["attend"][:, :, 3:4])
+        up_grad = outside(final["up"])
+        down_grads = final["down"].transpose(0, 2, 3, 1, 4).reshape(1, -1, width).astype(F32)
+
+    small_grads = small_sum
     own = lax.dynamic_index_in_dim(small_grads, core, 0, False)
     own = lax.dynamic_slice_in_dim(own, row * share, share, 1)
     return (
@@ -751,16 +958,13 @@
         input_grad[None],
         own[0][None],
         own[1][None],
-        qkv_grad[None],
-        out_grad[None],
+        qkv_grad,
+        out_grad,
         own[2][None],
         own[3][None],
-        up_grad[None],
-        down_grads[None],
+        up_grad,
+        down_grads,
     )
-
-
-DEPTH = 2
 
 
 def solution(mesh):

time: 604 us -> 426 us (0.71)
  starting transfers between devices: 156 us -> 71 us
  blocking collectives: 60.9 us -> 0 us
  local copies, waits for them, and re-layouts: 41.1 us -> 18.6 us
  Pallas kernels: 105 us -> 118 us
  other arithmetic: 67.6 us -> 56.1 us
  waiting for transfers between devices: 162 us -> 153 us
    ppermute x36 -> x28, starting transfers between devices: 90.1 us -> 31.7 us  [swap_rows(): return lax.ppermute(x, 'dp', [(i, i ^ bit) for i in range(rows)])]
    psum x1 -> x0, blocking collectives: 39.4 us -> none  [on_device(): small_grads = lax.psum(small_grads, ('section', 'group', 'dp'))]
    all_gather x1 -> x0, blocking collectives: 21.5 us -> none  [on_device(): smalls = lax.all_gather(gate(small, done[:1]), ('section', 'dp'))]
    ppermute x36 -> x32, waiting for transfers between devices: 104 us -> 83.1 us  [swap_groups(): return lax.ppermute(x, ('section', 'group'), pairs)]
    convert_element_type x9 -> x0, local copies, waits for them, and re-layouts: 17 us -> none  [the longest x6 12 us: outside(): return x.transpose(1, 3, 2, 0, 4).reshape(share, -1).astype(F32)]
    concatenate x21, other arithmetic: 28.9 us -> 12.2 us  [the longest x6 6.54 us: on_device(): bufs[chunk] = jnp.concatenate([buf, got], axis=0)]
    ppermute x36 -> x32, starting transfers between devices: 51.1 us -> 34.7 us  [swap_groups(): return lax.ppermute(x, ('section', 'group'), pairs)]
    convert_element_type x22 -> x25, other arithmetic: 17 us -> 33 us  [the longest x24 32.9 us: total_of(): return total.astype(BF)]
  transfers between devices with their start and end apart: 96 -> 90, of which waited for: 33 -> 35; matrix products, arithmetic and copies ran while one was open for 12% -> 16% of each run, Pallas kernels for 7% -> 23%
where the time goes in v2:
time: 426 us; the launch traced here: 419 us
  waiting for transfers between devices  153 us (36%)
  Pallas kernels  118 us (28%)
  starting transfers between devices  71 us (17%)
  other arithmetic  56.1 us (13%)
  local copies, waits for them, and re-layouts  18.6 us (4%)
    pallas_call x13, Pallas kernels, call(): pl.pallas_call(body, out_shape=outs, in_specs=specs, out_specs=out_specs,...  115 us
    ppermute x32, waiting for transfers between devices, swap_groups(): return lax.ppermute(x, ('section', 'group'), pairs)  83.1 us
    ppermute x28, waiting for transfers between devices, swap_rows(): return lax.ppermute(x, 'dp', [(i, i ^ bit) for i in range(rows)])  68.8 us
    ppermute x32, starting transfers between devices, swap_groups(): return lax.ppermute(x, ('section', 'group'), pairs)  34.7 us
    convert_element_type x24, other arithmetic, total_of(): return total.astype(BF)  32.9 us
    ppermute x28, starting transfers between devices, swap_rows(): return lax.ppermute(x, 'dp', [(i, i ^ bit) for i in range(rows)])  31.7 us
  transfers between devices with their start and end apart: 90, of which 35 were waited for; matrix products, arithmetic and copies ran while one was open for 16% of the time, Pallas kernels for 23%

profile of v2, /device:TPU:0, one launch (start us, length us, event | category | flops | bytes accessed | tf_op | source)
XLA Modules:
  0.0 419.4 jit_solution(13263420536085663320)
XLA Ops:
  12.3 7.4 %collective-permute-done.1 = bf16[1,1,4,48,384]{4,3,2,1,0:T(8,128)(2,1)S(1)} collective-permute-done((bf16[1,1,4,48,384]{4,3,2,1,0:T(8,128)(2,1)S(1)}, bf16[1,1,4,48,384]{4,3,2,1,0:T(8,128)(2,1)S(1)}, u32[]{:S(2)}, u32[]{:S(2)}) %collective-permute-start.1) | collective-permute-done | bytes 147488 | tf_op jit(solution)/shard_map/ppermute | solution.py:611
  26.0 6.6 %collective-permute-done.5 = bf16[1,1,4,48,384]{4,3,2,1,0:T(8,128)(2,1)S(1)} collective-permute-done((bf16[1,1,4,48,384]{4,3,2,1,0:T(8,128)(2,1)S(1)}, bf16[1,1,4,48,384]{4,3,2,1,0:T(8,128)(2,1)S(1)}, u32[]{:S(2)}, u32[]{:S(2)}) %collective-permute-start.5) | collective-permute-done | bytes 147488 | tf_op jit(solution)/shard_map/ppermute | solution.py:611
  79.6 5.4 %collective-permute-done.25 = bf16[1,2,4,48,384]{4,3,2,1,0:T(8,128)(2,1)S(1)} collective-permute-done((bf16[1,2,4,48,384]{4,3,2,1,0:T(8,128)(2,1)S(1)}, bf16[1,2,4,48,384]{4,3,2,1,0:T(8,128)(2,1)S(1)}, u32[]{:S(2)}, u32[]{:S(2)}) %collective-permute-start.25) | collective-permute-done | bytes 294944 | tf_op jit(solution)/shard_map/ppermute | solution.py:611
  91.1 10.4 %attend_forward_0.1 = (bf16[256,768]{1,0:T(8,128)(2,1)}, bf16[256,2304]{1,0:T(8,128)(2,1)}, f32[12,256,256]{2,1,0:T(8,128)}, bf16[256,768]{1,0:T(8,128)(2,1)}, f32[256,768]{1,0:T(8,128)}) custom-call(s32[3]{0:T(128)} %pad_add_fusion.ids, s32[3]{0:T(128)} %get-tuple-element.254.lens, bf16[256,768]{1,0:T(8,128)(2,1)} %dynamic-slice_bitcast_fusion.1.x_ref, ...), custom_call_target="tpu_custom_call" | custom-call | flops 1610612736 | bytes 12464152 | tf_op jit(solution)/shard_map/attend_forward_0/pallas_call | solution.py:431
  106.0 5.4 %collective-permute-done.28 = bf16[1,2,4,48,384]{4,3,2,1,0:T(8,128)(2,1)S(1)} collective-permute-done((bf16[1,2,4,48,384]{4,3,2,1,0:T(8,128)(2,1)S(1)}, bf16[1,2,4,48,384]{4,3,2,1,0:T(8,128)(2,1)S(1)}, u32[]{:S(2)}, u32[]{:S(2)}) %collective-permute-start.28) | collective-permute-done | bytes 294944 | tf_op jit(solution)/shard_map/ppermute | solution.py:611
  111.5 5.9 %collective-permute-done.35 = bf16[1,2,4,48,384]{4,3,2,1,0:T(8,128)(2,1)S(1)} collective-permute-done((bf16[1,2,4,48,384]{4,3,2,1,0:T(8,128)(2,1)S(1)}, bf16[1,2,4,48,384]{4,3,2,1,0:T(8,128)(2,1)S(1)}, u32[]{:S(2)}, u32[]{:S(2)}) %collective-permute-start.35) | collective-permute-done | bytes 294944 | tf_op jit(solution)/shard_map/ppermute | solution.py:611
  119.6 6.0 %collective-permute-done.34 = bf16[1,3,4,48,384]{4,3,2,1,0:T(8,128)(2,1)S(1)} collective-permute-done((bf16[1,3,4,48,384]{4,3,2,1,0:T(8,128)(2,1)S(1)}, bf16[1,3,4,48,384]{4,3,2,1,0:T(8,128)(2,1)S(1)}, u32[]{:S(2)}, u32[]{:S(2)}) %collective-permute-start.34) | collective-permute-done | bytes 442400 | tf_op jit(solution)/shard_map/ppermute | solution.py:597
  126.2 7.1 %collective-permute-done.40 = bf16[1,3,4,48,384]{4,3,2,1,0:T(8,128)(2,1)S(1)} collective-permute-done((bf16[1,3,4,48,384]{4,3,2,1,0:T(8,128)(2,1)S(1)}, bf16[1,3,4,48,384]{4,3,2,1,0:T(8,128)(2,1)S(1)}, u32[]{:S(2)}, u32[]{:S(2)}) %collective-permute-start.40) | collective-permute-done | bytes 442400 | tf_op jit(solution)/shard_map/ppermute | solution.py:597
  134.5 9.6 %feed_forward_0.1 = (bf16[256,768]{1,0:T(8,128)(2,1)}, bf16[256,3072]{1,0:T(8,128)(2,1)}, f32[256,3072]{1,0:T(8,128)}, bf16[256,768]{1,0:T(8,128)(2,1)}) custom-call(s32[3]{0:T(128)} %pad_add_fusion.ids, f32[256,768]{1,0:T(8,128)} %get-tuple-element.154.resid, f32[4,768]{1,0:T(4,128)} %squeeze.18.small, bf16[1,192,3072]{2,1,0:T(8,128)(2,1)} %refs_0_.14, ...), custom_call_target="tpu_custom_call" | custom-call | flops 2415919104 | bytes 18100236 | tf_op jit(solution)/shard_map/feed_forward_0/pallas_call | solution.py:431
  146.6 9.9 %attend_forward_1.1 = (bf16[256,768]{1,0:T(8,128)(2,1)}, bf16[256,2304]{1,0:T(8,128)(2,1)}, f32[12,256,256]{2,1,0:T(8,128)}, bf16[256,768]{1,0:T(8,128)(2,1)}, f32[256,768]{1,0:T(8,128)}) custom-call(s32[3]{0:T(128)} %pad_add_fusion.ids, s32[3]{0:T(128)} %get-tuple-element.254.lens, bf16[256,768]{1,0:T(8,128)(2,1)} %get-tuple-element.160.x_ref, ...), custom_call_target="tpu_custom_call" | custom-call | flops 1610612736 | bytes 12464152 | tf_op jit(solution)/shard_map/attend_forward_1/pallas_call | solution.py:431
  161.4 9.6 %feed_forward_1.1 = (bf16[256,768]{1,0:T(8,128)(2,1)}, bf16[256,3072]{1,0:T(8,128)(2,1)}, f32[256,3072]{1,0:T(8,128)}, bf16[256,768]{1,0:T(8,128)(2,1)}) custom-call(s32[3]{0:T(128)} %pad_add_fusion.ids, f32[256,768]{1,0:T(8,128)} %get-tuple-element.162.resid, f32[4,768]{1,0:T(4,128)} %squeeze.19.small, bf16[1,192,3072]{2,1,0:T(8,128)(2,1)} %refs_0_.14, ...), custom_call_target="tpu_custom_call" | custom-call | flops 2415919104 | bytes 18100236 | tf_op jit(solution)/shard_map/feed_forward_1/pallas_call | solution.py:431
  171.0 5.1 %down_grad_1.1 = (bf16[4,4,192,384]{3,2,1,0:T(8,128)(2,1)}, bf16[4,4,192,384]{3,2,1,0:T(8,128)(2,1)}) custom-call(s32[3]{0:T(128)} %pad_add_fusion.ids, bf16[256,3072]{1,0:T(8,128)(2,1)} %get-tuple-element.172.active, bf16[256,768]{1,0:T(8,128)(2,1)} %dynamic-slice_bitcast_fusion.d_out), custom_call_target="tpu_custom_call" | custom-call | flops 1207959552 | bytes 6684684 | tf_op jit(solution)/shard_map/down_grad_1/pallas_call | solution.py:431
  176.3 12.3 %feed_backward_1.1 = (bf16[4,4,4,48,384]{4,3,2,1,0:T(8,128)(2,1)}, bf16[4,4,4,48,384]{4,3,2,1,0:T(8,128)(2,1)}, f32[256,768]{1,0:T(8,128)}, f32[2,768]{1,0:T(2,128)}) custom-call(s32[3]{0:T(128)} %pad_add_fusion.ids, bf16[256,768]{1,0:T(8,128)(2,1)} %dynamic-slice_bitcast_fusion.d_out, f32[256,768]{1,0:T(8,128)} %get-tuple-element.162.resid, ...), custom_call_target="tpu_custom_call" | custom-call | flops 3623878656 | bytes 22038540 | tf_op jit(solution)/shard_map/feed_backward_1/pallas_call | solution.py:431
  189.3 16.7 %attend_backward_1.1 = (bf16[4,4,4,48,384]{4,3,2,1,0:T(8,128)(2,1)}, bf16[4,4,4,48,384]{4,3,2,1,0:T(8,128)(2,1)}, bf16[256,768]{1,0:T(8,128)(2,1)}, f32[2,768]{1,0:T(2,128)}) custom-call(s32[3]{0:T(128)} %pad_add_fusion.ids, bf16[256,768]{1,0:T(8,128)(2,1)} %get-tuple-element.160.x_ref, f32[256,768]{1,0:T(8,128)} %get-tuple-element.174.d_resid, ...), custom_call_target="tpu_custom_call" | custom-call | flops 3422552064 | bytes 17582092 | tf_op jit(solution)/shard_map/attend_backward_1/pallas_call | solution.py:431
  213.0 11.2 %collective-permute-done.46 = bf16[2,4,4,48,384]{4,3,2,1,0:T(8,128)(2,1)} collective-permute-done((bf16[2,4,4,48,384]{4,3,2,1,0:T(8,128)(2,1)S(1)}, bf16[2,4,4,48,384]{4,3,2,1,0:T(8,128)(2,1)}, u32[]{:S(2)}, u32[]{:S(2)}) %collective-permute-start.46) | collective-permute-done | bytes 1179680 | tf_op jit(solution)/shard_map/ppermute | solution.py:597
  224.2 5.1 %down_grad_0.1 = (bf16[4,4,192,384]{3,2,1,0:T(8,128)(2,1)}, bf16[4,4,192,384]{3,2,1,0:T(8,128)(2,1)}) custom-call(s32[3]{0:T(128)} %pad_add_fusion.ids, bf16[256,3072]{1,0:T(8,128)(2,1)} %get-tuple-element.184.active, bf16[256,768]{1,0:T(8,128)(2,1)} %get-tuple-element.187.d_out), custom_call_target="tpu_custom_call" | custom-call | flops 1207959552 | bytes 6684684 | tf_op jit(solution)/shard_map/down_grad_0/pallas_call | solution.py:431
  240.7 6.1 %collective-permute-done.47 = bf16[1,4,4,48,384]{4,3,2,1,0:T(8,128)(2,1)S(1)} collective-permute-done((bf16[1,4,4,48,384]{4,3,2,1,0:T(8,128)(2,1)S(1)}, bf16[1,4,4,48,384]{4,3,2,1,0:T(8,128)(2,1)S(1)}, u32[]{:S(2)}, u32[]{:S(2)}) %collective-permute-start.47) | collective-permute-done | bytes 589856 | tf_op jit(solution)/shard_map/ppermute | solution.py:597
  246.8 12.4 %feed_backward_0.1 = (bf16[4,4,4,48,384]{4,3,2,1,0:T(8,128)(2,1)}, bf16[4,4,4,48,384]{4,3,2,1,0:T(8,128)(2,1)}, f32[256,768]{1,0:T(8,128)}, f32[2,768]{1,0:T(2,128)}) custom-call(s32[3]{0:T(128)} %pad_add_fusion.ids, bf16[256,768]{1,0:T(8,128)(2,1)} %get-tuple-element.187.d_out, f32[256,768]{1,0:T(8,128)} %get-tuple-element.154.resid, ...), custom_call_target="tpu_custom_call" | custom-call | flops 3623878656 | bytes 22038540 | tf_op jit(solution)/shard_map/feed_backward_0/pallas_call | solution.py:431
  273.4 15.5 %attend_backward_0.1 = (bf16[4,4,4,48,384]{4,3,2,1,0:T(8,128)(2,1)}, bf16[4,4,4,48,384]{4,3,2,1,0:T(8,128)(2,1)}, bf16[256,768]{1,0:T(8,128)(2,1)}, f32[2,768]{1,0:T(2,128)}) custom-call(s32[3]{0:T(128)} %pad_add_fusion.ids, bf16[256,768]{1,0:T(8,128)(2,1)} %dynamic-slice_bitcast_fusion.1.x_ref, f32[256,768]{1,0:T(8,128)} %get-tuple-element.197.d_resid, ...), custom_call_target="tpu_custom_call" | custom-call | flops 3422552064 | bytes 17582092 | tf_op jit(solution)/shard_map/attend_backward_0/pallas_call | solution.py:431
  311.2 8.9 %collective-permute-done.64 = bf16[1,4,4,48,384]{4,3,2,1,0:T(8,128)(2,1)S(1)} collective-permute-done((bf16[1,4,4,48,384]{4,3,2,1,0:T(8,128)(2,1)S(1)}, bf16[1,4,4,48,384]{4,3,2,1,0:T(8,128)(2,1)S(1)}, u32[]{:S(2)}, u32[]{:S(2)}) %collective-permute-start.64) | collective-permute-done | bytes 589856 | tf_op jit(solution)/shard_map/ppermute | solution.py:597
  332.7 11.1 %collective-permute-done.70 = bf16[1,4,4,48,384]{4,3,2,1,0:T(8,128)(2,1)S(1)} collective-permute-done((bf16[1,4,4,48,384]{4,3,2,1,0:T(8,128)(2,1)S(1)}, bf16[1,4,4,48,384]{4,3,2,1,0:T(8,128)(2,1)S(1)}, u32[]{:S(2)}, u32[]{:S(2)}) %collective-permute-start.70) | collective-permute-done | bytes 589856 | tf_op jit(solution)/shard_map/ppermute | solution.py:597
  347.2 5.4 %collective-permute-done.73 = bf16[1,1,4,48,384]{4,3,2,1,0:T(8,128)(2,1)S(1)} collective-permute-done((bf16[1,1,4,48,384]{4,3,2,1,0:T(8,128)(2,1)S(1)}, bf16[1,1,4,48,384]{4,3,2,1,0:T(8,128)(2,1)S(1)}, u32[]{:S(2)}, u32[]{:S(2)}) %collective-permute-start.73) | collective-permute-done | bytes 147488 | tf_op jit(solution)/shard_map/ppermute | solution.py:611
  364.0 5.8 %collective-permute-done.77 = bf16[1,1,4,48,384]{4,3,2,1,0:T(8,128)(2,1)S(1)} collective-permute-done((bf16[1,1,4,48,384]{4,3,2,1,0:T(8,128)(2,1)S(1)}, bf16[1,1,4,48,384]{4,3,2,1,0:T(8,128)(2,1)S(1)}, u32[]{:S(2)}, u32[]{:S(2)}) %collective-permute-start.77) | collective-permute-done | bytes 147488 | tf_op jit(solution)/shard_map/ppermute | solution.py:611
  374.1 7.3 %collective-permute-done.81 = bf16[1,1,4,48,384]{4,3,2,1,0:T(8,128)(2,1)S(1)} collective-permute-done((bf16[1,1,4,48,384]{4,3,2,1,0:T(8,128)(2,1)S(1)}, bf16[1,1,4,48,384]{4,3,2,1,0:T(8,128)(2,1)S(1)}, u32[]{:S(2)}, u32[]{:S(2)}) %collective-permute-start.81) | collective-permute-done | bytes 147488 | tf_op jit(solution)/shard_map/ppermute | solution.py:611
  (384 shorter events, 211.2 us)
Async XLA Ops:
  45.2 22.9 %collective-permute-start.9 = (bf16[2,3,4,48,384]{4,3,2,1,0:T(8,128)(2,1)}, bf16[2,3,4,48,384]{4,3,2,1,0:T(8,128)(2,1)}, u32[]{:S(2)}, u32[]{:S(2)}) collective-permute-start(bf16[2,3,4,48,384]{4,3,2,1,0:T(8,128)(2,1)} %pad_maximum_fusion.3.refs_4_), channel_id=1, source_target_pairs={{0,8},{4,12},{8,0},{12,4},{16,20},{20,16},{24,28},{28,24},{1,9},{5... | collective-permute-start | bytes 2654216 | tf_op jit(solution)/shard_map/ppermute | solution.py:597
  55.1 22.7 %collective-permute-start.18 = (bf16[1,768,768]{2,1,0:T(8,128)(2,1)S(1)}, bf16[1,768,768]{2,1,0:T(8,128)(2,1)S(1)}, u32[]{:S(2)}, u32[]{:S(2)}) collective-permute-start(bf16[1,768,768]{2,1,0:T(8,128)(2,1)S(1)} %copy-done.3), channel_id=1, source_target_pairs={{0,16},{16,0},{1,17},{17,1},{2,18},{18,2},{3,19},{19,3},{4,20},{20... | collective-permute-start | bytes 3538952 | tf_op jit(solution)/shard_map/ppermute | solution.py:584
  86.4 31.1 %collective-permute-start.21 = (bf16[2,3,4,48,384]{4,3,2,1,0:T(8,128)(2,1)}, bf16[2,3,4,48,384]{4,3,2,1,0:T(8,128)(2,1)}, u32[]{:S(2)}, u32[]{:S(2)}) collective-permute-start(bf16[2,3,4,48,384]{4,3,2,1,0:T(8,128)(2,1)} %collective-permute-done.20.refs_3_), channel_id=1, source_target_pairs={{0,16},{16,0},{1,17},{17,1},{2,18},{18,2},{3,19},{19,3},{4,20},{20... | collective-permute-start | bytes 2654216 | tf_op jit(solution)/shard_map/ppermute | solution.py:584
  90.1 27.5 %collective-permute-start.24 = (bf16[2,3,4,48,384]{4,3,2,1,0:T(8,128)(2,1)}, bf16[2,3,4,48,384]{4,3,2,1,0:T(8,128)(2,1)S(1)}, u32[]{:S(2)}, u32[]{:S(2)}) collective-permute-start(bf16[2,3,4,48,384]{4,3,2,1,0:T(8,128)(2,1)} %pad_maximum_fusion.5), channel_id=1, source_target_pairs={{0,16},{16,0},{1,17},{17,1},{2,18},{18,2},{3,19},{19,3},{4,20},{20... | collective-permute-start | bytes 2654216 | tf_op jit(solution)/shard_map/ppermute | solution.py:584
  111.4 22.0 %collective-permute-start.31 = (bf16[2,3,4,48,384]{4,3,2,1,0:T(8,128)(2,1)S(1)}, bf16[2,3,4,48,384]{4,3,2,1,0:T(8,128)(2,1)S(1)}, u32[]{:S(2)}, u32[]{:S(2)}) collective-permute-start(bf16[2,3,4,48,384]{4,3,2,1,0:T(8,128)(2,1)S(1)} %collective-permute-done.23), channel_id=1, source_target_pairs={{0,16},{16,0},{1,17},{17,1},{2,18},{18,2},{3,19},{19,3},{4,20},{20... | collective-permute-start | bytes 2654216 | tf_op jit(solution)/shard_map/ppermute | solution.py:584
  117.4 26.6 %collective-permute-start.33 = (bf16[2,3,4,48,384]{4,3,2,1,0:T(8,128)(2,1)S(1)}, bf16[2,3,4,48,384]{4,3,2,1,0:T(8,128)(2,1)S(1)}, u32[]{:S(2)}, u32[]{:S(2)}) collective-permute-start(bf16[2,3,4,48,384]{4,3,2,1,0:T(8,128)(2,1)S(1)} %pad_maximum_fusion.6.refs_4_), channel_id=1, source_target_pairs={{0,16},{16,0},{1,17},{17,1},{2,18},{18,2},{3,19},{19,3},{4,20},{20... | collective-permute-start | bytes 2654216 | tf_op jit(solution)/shard_map/ppermute | solution.py:584
  126.2 30.3 %collective-permute-start.38 = (bf16[2,3,4,48,384]{4,3,2,1,0:T(8,128)(2,1)S(1)}, bf16[2,3,4,48,384]{4,3,2,1,0:T(8,128)(2,1)}, u32[]{:S(2)}, u32[]{:S(2)}) collective-permute-start(bf16[2,3,4,48,384]{4,3,2,1,0:T(8,128)(2,1)S(1)} %pad_maximum_fusion.7.refs_2_), channel_id=1, source_target_pairs={{0,16},{16,0},{1,17},{17,1},{2,18},{18,2},{3,19},{19,3},{4,20},{20... | collective-permute-start | bytes 2654216 | tf_op jit(solution)/shard_map/ppermute | solution.py:584
  206.0 27.8 %collective-permute-start.50 = (bf16[4,4,4,48,384]{4,3,2,1,0:T(8,128)(2,1)}, bf16[4,4,4,48,384]{4,3,2,1,0:T(8,128)(2,1)}, u32[]{:S(2)}, u32[]{:S(2)}) collective-permute-start(bf16[4,4,4,48,384]{4,3,2,1,0:T(8,128)(2,1)} %get-tuple-element.183), channel_id=1, source_target_pairs={{0,16},{16,0},{1,17},{17,1},{2,18},{18,2},{3,19},{19,3},{4,20},{20... | collective-permute-start | bytes 7077896 | tf_op jit(solution)/shard_map/ppermute | solution.py:584
  208.3 22.2 %collective-permute-start.44 = (bf16[256,768]{1,0:T(8,128)(2,1)S(1)}, bf16[256,768]{1,0:T(8,128)(2,1)S(1)}, u32[]{:S(2)}, u32[]{:S(2)}) collective-permute-start(bf16[256,768]{1,0:T(8,128)(2,1)S(1)} %get-tuple-element.260), channel_id=1, source_target_pairs={{0,16},{16,0},{1,17},{17,1},{2,18},{18,2},{3,19},{19,3},{4,20},{20... | collective-permute-start | bytes 1179656 | tf_op jit(solution)/shard_map/ppermute | solution.py:584
  211.1 27.0 %collective-permute-start.49 = (bf16[2,4,4,48,384]{4,3,2,1,0:T(8,128)(2,1)}, bf16[2,4,4,48,384]{4,3,2,1,0:T(8,128)(2,1)}, u32[]{:S(2)}, u32[]{:S(2)}) collective-permute-start(bf16[2,4,4,48,384]{4,3,2,1,0:T(8,128)(2,1)} %add_convert_fusion.3), channel_id=1, source_target_pairs={{0,4},{4,0},{8,12},{12,8},{16,24},{20,28},{24,16},{28,20},{1,5},{5... | collective-permute-start | bytes 3538952 | tf_op jit(solution)/shard_map/ppermute | solution.py:597
  229.3 41.3 %collective-permute-start.54 = (bf16[4,4,4,48,384]{4,3,2,1,0:T(8,128)(2,1)}, bf16[4,4,4,48,384]{4,3,2,1,0:T(8,128)(2,1)}, u32[]{:S(2)}, u32[]{:S(2)}) collective-permute-start(bf16[4,4,4,48,384]{4,3,2,1,0:T(8,128)(2,1)} %bitcast.122), channel_id=1, source_target_pairs={{0,16},{16,0},{1,17},{17,1},{2,18},{18,2},{3,19},{19,3},{4,20},{20... | collective-permute-start | bytes 7077896 | tf_op jit(solution)/shard_map/ppermute | solution.py:584
  236.3 34.3 %collective-permute-start.53 = (bf16[2,4,4,48,384]{4,3,2,1,0:T(8,128)(2,1)}, bf16[2,4,4,48,384]{4,3,2,1,0:T(8,128)(2,1)}, u32[]{:S(2)}, u32[]{:S(2)}) collective-permute-start(bf16[2,4,4,48,384]{4,3,2,1,0:T(8,128)(2,1)} %add_convert_fusion.2), channel_id=1, source_target_pairs={{0,4},{4,0},{8,12},{12,8},{16,24},{20,28},{24,16},{28,20},{1,5},{5... | collective-permute-start | bytes 3538952 | tf_op jit(solution)/shard_map/ppermute | solution.py:597
  240.3 22.9 %collective-permute-start.52 = (bf16[1,4,4,48,384]{4,3,2,1,0:T(8,128)(2,1)}, bf16[1,4,4,48,384]{4,3,2,1,0:T(8,128)(2,1)S(1)}, u32[]{:S(2)}, u32[]{:S(2)}) collective-permute-start(bf16[1,4,4,48,384]{4,3,2,1,0:T(8,128)(2,1)} %add_convert_fusion.7), channel_id=1, source_target_pairs={{0,8},{4,12},{8,0},{12,4},{16,20},{20,16},{24,28},{28,24},{1,9},{5... | collective-permute-start | bytes 1769480 | tf_op jit(solution)/shard_map/ppermute | solution.py:597
  259.2 40.6 %collective-permute-start.60 = (bf16[4,4,4,48,384]{4,3,2,1,0:T(8,128)(2,1)}, bf16[4,4,4,48,384]{4,3,2,1,0:T(8,128)(2,1)}, u32[]{:S(2)}, u32[]{:S(2)}) collective-permute-start(bf16[4,4,4,48,384]{4,3,2,1,0:T(8,128)(2,1)} %get-tuple-element.212), channel_id=1, source_target_pairs={{0,16},{16,0},{1,17},{17,1},{2,18},{18,2},{3,19},{19,3},{4,20},{20... | collective-permute-start | bytes 7077896 | tf_op jit(solution)/shard_map/ppermute | solution.py:584
  265.2 28.1 %collective-permute-start.57 = (bf16[1,2,4,48,384]{4,3,2,1,0:T(8,128)(2,1)}, bf16[1,2,4,48,384]{4,3,2,1,0:T(8,128)(2,1)S(1)}, u32[]{:S(2)}, u32[]{:S(2)}) collective-permute-start(bf16[1,2,4,48,384]{4,3,2,1,0:T(8,128)(2,1)} %add_convert_fusion.12), channel_id=1, source_target_pairs={{0,1},{1,0},{2,3},{3,2},{4,5},{5,4},{6,7},{7,6},{8,9},{9,8},{10,11... | collective-permute-start | bytes 884744 | tf_op jit(solution)/shard_map/ppermute | solution.py:611
  273.4 24.2 %collective-permute-start.59 = (bf16[2,4,4,48,384]{4,3,2,1,0:T(8,128)(2,1)}, bf16[2,4,4,48,384]{4,3,2,1,0:T(8,128)(2,1)}, u32[]{:S(2)}, u32[]{:S(2)}) collective-permute-start(bf16[2,4,4,48,384]{4,3,2,1,0:T(8,128)(2,1)} %fusion), channel_id=1, source_target_pairs={{0,4},{4,0},{8,12},{12,8},{16,24},{20,28},{24,16},{28,20},{1,5},{5... | collective-permute-start | bytes 3538952 | tf_op jit(solution)/shard_map/ppermute | solution.py:597
  288.9 32.5 %collective-permute-start.66 = (bf16[4,4,4,48,384]{4,3,2,1,0:T(8,128)(2,1)}, bf16[4,4,4,48,384]{4,3,2,1,0:T(8,128)(2,1)S(1)}, u32[]{:S(2)}, u32[]{:S(2)}) collective-permute-start(bf16[4,4,4,48,384]{4,3,2,1,0:T(8,128)(2,1)} %get-tuple-element.220), channel_id=1, source_target_pairs={{0,16},{16,0},{1,17},{17,1},{2,18},{18,2},{3,19},{19,3},{4,20},{20... | collective-permute-start | bytes 7077896 | tf_op jit(solution)/shard_map/ppermute | solution.py:584
  299.2 20.8 %collective-permute-start.64 = (bf16[1,4,4,48,384]{4,3,2,1,0:T(8,128)(2,1)S(1)}, bf16[1,4,4,48,384]{4,3,2,1,0:T(8,128)(2,1)S(1)}, u32[]{:S(2)}, u32[]{:S(2)}) collective-permute-start(bf16[1,4,4,48,384]{4,3,2,1,0:T(8,128)(2,1)S(1)} %fusion.3), channel_id=1, source_target_pairs={{0,8},{4,12},{8,0},{12,4},{16,20},{20,16},{24,28},{28,24},{1,9},{5... | collective-permute-start | bytes 1769480 | tf_op jit(solution)/shard_map/ppermute | solution.py:597
  301.5 22.9 %collective-permute-start.65 = (bf16[2,4,4,48,384]{4,3,2,1,0:T(8,128)(2,1)S(1)}, bf16[2,4,4,48,384]{4,3,2,1,0:T(8,128)(2,1)S(1)}, u32[]{:S(2)}, u32[]{:S(2)}) collective-permute-start(bf16[2,4,4,48,384]{4,3,2,1,0:T(8,128)(2,1)S(1)} %add_convert_fusion.1), channel_id=1, source_target_pairs={{0,4},{4,0},{8,12},{12,8},{16,24},{20,28},{24,16},{28,20},{1,5},{5... | collective-permute-start | bytes 3538952 | tf_op jit(solution)/shard_map/ppermute | solution.py:597
  307.4 47.2 %collective-permute-start.62 = (bf16[1,1,4,48,384]{4,3,2,1,0:T(8,128)(2,1)S(1)}, bf16[1,1,4,48,384]{4,3,2,1,0:T(8,128)(2,1)S(1)}, u32[]{:S(2)}, u32[]{:S(2)}) collective-permute-start(bf16[1,1,4,48,384]{4,3,2,1,0:T(8,128)(2,1)S(1)} %add_convert_fusion.24), channel_id=1, source_target_pairs={{0,2},{1,3},{2,0},{3,1},{4,6},{5,7},{6,4},{7,5},{8,10},{9,11},{10,... | collective-permute-start | bytes 442376 | tf_op jit(solution)/shard_map/ppermute | solution.py:611
  324.4 22.5 %collective-permute-start.71 = (bf16[2,4,4,48,384]{4,3,2,1,0:T(8,128)(2,1)S(1)}, bf16[2,4,4,48,384]{4,3,2,1,0:T(8,128)(2,1)S(1)}, u32[]{:S(2)}, u32[]{:S(2)}) collective-permute-start(bf16[2,4,4,48,384]{4,3,2,1,0:T(8,128)(2,1)S(1)} %add_convert_fusion), channel_id=1, source_target_pairs={{0,4},{4,0},{8,12},{12,8},{16,24},{20,28},{24,16},{28,20},{1,5},{5... | collective-permute-start | bytes 3538952 | tf_op jit(solution)/shard_map/ppermute | solution.py:597
  328.7 58.6 %collective-permute-start.55 = (bf16[256,768]{1,0:T(8,128)(2,1)S(1)}, bf16[256,768]{1,0:T(8,128)(2,1)S(1)}, u32[]{:S(2)}, u32[]{:S(2)}) collective-permute-start(bf16[256,768]{1,0:T(8,128)(2,1)S(1)} %get-tuple-element.258), channel_id=1, source_target_pairs={{0,16},{16,0},{1,17},{17,1},{2,18},{18,2},{3,19},{19,3},{4,20},{20... | collective-permute-start | bytes 1179656 | tf_op jit(solution)/shard_map/ppermute | solution.py:584
  330.9 43.1 %collective-permute-start.68 = (bf16[1,1,4,48,384]{4,3,2,1,0:T(8,128)(2,1)S(1)}, bf16[1,1,4,48,384]{4,3,2,1,0:T(8,128)(2,1)S(1)}, u32[]{:S(2)}, u32[]{:S(2)}) collective-permute-start(bf16[1,1,4,48,384]{4,3,2,1,0:T(8,128)(2,1)S(1)} %add_convert_fusion.23), channel_id=1, source_target_pairs={{0,2},{1,3},{2,0},{3,1},{4,6},{5,7},{6,4},{7,5},{8,10},{9,11},{10,... | collective-permute-start | bytes 442376 | tf_op jit(solution)/shard_map/ppermute | solution.py:611
  358.2 24.6 %collective-permute-start.67 = (f32[2,4,768]{2,1,0:T(4,128)S(1)}, f32[2,4,768]{2,1,0:T(4,128)S(1)}, u32[]{:S(2)}, u32[]{:S(2)}) collective-permute-start(f32[2,4,768]{2,1,0:T(4,128)S(1)} %fusion.12), channel_id=1, source_target_pairs={{0,4},{4,0},{8,12},{12,8},{16,24},{20,28},{24,16},{28,20},{1,5},{5... | collective-permute-start | bytes 73736 | tf_op jit(solution)/shard_map/ppermute | solution.py:597
  (115 other events, 1152.0 us)

commit v3 on v2

--- a/solution.py
+++ b/solution.py
@@ -108,6 +108,9 @@
         self.direct = self.tall % 16 == 0
         self.few = rows <= 4 and rows & (rows - 1) == 0
 
+    def rows_first(self, layer, kind):
+        return self.few and self.direct and (layer, kind) in ROWS_FIRST
+
 
 def start_weights(plan, layer, kind, ids, own, others, whole, dst, sem):
     width, tall = plan.width, plan.tall
@@ -165,42 +168,40 @@
     pltpu.make_async_copy(ref, ref, sem).wait()
 
 
-def start_grads(plan, kind, ids, src, keep, send, sem):
-    width, tall = plan.width, plan.tall
+def start_grads(plan, kind, ids, src, outs, sem, rows_first):
+    tall = plan.tall
     core, group, row = ids[0], ids[1], ids[2]
     if not plan.direct:
-        for out, half in ((keep, core), (send, 1 - core)):
-            lanes = pl.ds(pl.multiple_of(half * BLOCK, LANES), BLOCK)
-            if kind == "down":
-                pltpu.make_async_copy(src.at[:, lanes], out, sem).start()
-            else:
-                pltpu.make_async_copy(src.at[:, :, lanes], out, sem).start()
+        pltpu.make_async_copy(src, outs[0], sem).start()
         return
     tables = masks_of(plan.groups, False)
-    for out, half, flag in ((keep, core, core == 0), (send, 1 - core, core != 0)):
-        lanes = pl.ds(pl.multiple_of(half * BLOCK, LANES), BLOCK)
-        for j in range(plan.groups):
-            peer = group ^ pick(flag, tables[0][j], tables[1][j])
-            for k in range(plan.rows):
-                at = row_to(plan, row, k) * plan.groups + peer
-                if kind == "down":
-                    part = src.at[pl.ds(pl.multiple_of(at * (tall * PARTS), 16), tall * PARTS), lanes]
-                else:
-                    part = src.at[:, pl.ds(pl.multiple_of(at * tall, 16), tall), lanes]
-                pltpu.make_async_copy(part, out.at[j, k], sem).start()
+    half = plan.groups // 2
+    for j in range(plan.groups):
+        peer = group ^ pick(core == 0, tables[0][j], tables[1][j])
+        for k in range(plan.rows):
+            at = row_to(plan, row, k) * plan.groups + peer
+            if kind == "down":
+                part = src.at[pl.ds(pl.multiple_of(at * (tall * PARTS), 16), tall * PARTS)]
+            else:
+                part = src.at[:, pl.ds(pl.multiple_of(at * tall, 16), tall)]
+            if rows_first:
+                out = outs[k // (plan.rows // 2)].at[j, k % (plan.rows // 2)]
+            else:
+                out = outs[j // half].at[j % half, k]
+            pltpu.make_async_copy(part, out, sem).start()
 
 
 def attend_forward(plan, layer, ids, lens, x_ref, small, cosv, sinv, *refs):
     n = 7
     own, others, whole = weight_refs(plan, "attend", refs[: plan_inputs(plan, "attend")])
     refs = refs[plan_inputs(plan, "attend") :]
-    normed, qkv, probs, mixed, resid, w, same, sem = refs
+    qkv, probs, acts, resid, w, same, sem = refs
     width, tok = plan.width, plan.tok
     start_weights(plan, layer, "attend", ids, own, others, whole, w, sem)
     x = x_ref[...].astype(jnp.float32)
     hat, _ = normalize(x)
     low = (hat * small[0:1, :] + small[1:2, :]).astype(jnp.bfloat16)
-    normed[...] = low
+    acts[:, :width] = low
     first_end = lens[0]
     second_end = lens[0] + lens[1]
 
@@ -235,11 +236,11 @@
             probs[2 * t + h] = p
             part = mm(p.astype(jnp.bfloat16), head_of(v, h), 1, 0)
             total = part if total is None else total + part
-        mixed[:, pl.ds(at, LANES)] = total.astype(jnp.bfloat16)
+        acts[:, pl.ds(width + at, LANES)] = total.astype(jnp.bfloat16)
         return carry
 
     lax.fori_loop(0, width // LANES, tile, 0)
-    resid[...] = x + mm(mixed[...], w[3], 1, 0)
+    resid[...] = x + mm(acts[:, width:], w[3], 1, 0)
 
 
 def feed_forward(plan, layer, ids, resid, small, *refs):
@@ -247,13 +248,13 @@
     b = plan_inputs(plan, "down")
     up_refs = weight_refs(plan, "up", refs[:a])
     down_refs = weight_refs(plan, "down", refs[a : a + b])
-    normed, active, slope, y, wu, wd, sem_u, sem_d = refs[a + b :]
+    acts, slope, y, wu, wd, sem_u, sem_d = refs[a + b :]
     width = plan.width
     start_weights(plan, layer, "up", ids, *up_refs, wu, sem_u)
     start_weights(plan, layer, "down", ids, *down_refs, wd, sem_d)
     hat, _ = normalize(resid[...])
     low = (hat * small[2:3, :] + small[3:4, :]).astype(jnp.bfloat16)
-    normed[...] = low
+    acts[:, PARTS * width :] = low
     wait_all(wu, sem_u)
     total = resid[...]
     for j in range(PARTS):
@@ -261,7 +262,7 @@
         cdf = 0.5 * (1.0 + lax.erf(v * (2.0**-0.5)))
         act = (v * cdf).astype(jnp.bfloat16)
         lanes = slice(j * width, (j + 1) * width)
-        active[:, lanes] = act
+        acts[:, lanes] = act
         slope[:, lanes] = cdf + v * (jnp.exp(v * v * -0.5) * 0.3989422804014327)
         if j == 0:
             wait_all(wd, sem_d)
@@ -269,54 +270,87 @@
     y[...] = total.astype(jnp.bfloat16)
 
 
-def down_grad(plan, ids, active, d_out, keep, send, g, sem):
+def split(first, own, send, at, x):
+    low, high = x[:, :BLOCK], x[:, BLOCK:]
+    own[:, at : at + BLOCK] = jnp.where(first, low, high)
+    send[:, at : at + BLOCK] = jnp.where(first, high, low)
+
+
+def both(own, other, lanes):
+    return jnp.concatenate([own[:, lanes], other[:, lanes]], axis=0)
+
+
+def down_grad(plan, rows_first, at, ids, active, active_too, d, d_too, *refs):
+    *outs, g, sem = refs
     width = plan.width
-    d = d_out[...]
+    right = both(d, d_too, slice(at, at + BLOCK))
     for j in range(PARTS):
-        g[j * width : (j + 1) * width, :] = mm(
-            active[:, j * width : (j + 1) * width], d, 0, 0
-        ).astype(jnp.bfloat16)
-    start_grads(plan, "down", ids, g, keep, send, sem)
+        lanes = slice(j * width, (j + 1) * width)
+        g[lanes, :] = mm(both(active, active_too, lanes), right, 0, 0).astype(jnp.bfloat16)
+    start_grads(plan, "down", ids, g, outs, sem, rows_first)
     wait_all(g, sem)
 
 
-def feed_backward(plan, layer, ids, d_out, resid, normed, slope, small, *refs):
+def up_grad(plan, rows_first, ids, normed, normed_too, d, d_too, *refs):
+    *outs, g, sem = refs
+    left = both(normed, normed_too, slice(0, plan.width))
+    for j in range(0, PARTS, 2):
+        two = mm(left, both(d, d_too, slice(j * BLOCK, (j + 2) * BLOCK)), 0, 0).astype(jnp.bfloat16)
+        g[j] = two[:, :BLOCK]
+        g[j + 1] = two[:, BLOCK:]
+    start_grads(plan, "up", ids, g, outs, sem, rows_first)
+    wait_all(g, sem)
+
+
+def attend_grad(plan, rows_first, ids, acts, acts_too, d, d_too, *refs):
+    *outs, g, sem = refs
+    width = plan.width
+    left = both(acts, acts_too, slice(0, width))
+    two = mm(left, both(d, d_too, slice(0, 2 * BLOCK)), 0, 0).astype(jnp.bfloat16)
+    g[0] = two[:, :BLOCK]
+    g[1] = two[:, BLOCK:]
+    g[2] = mm(left, both(d, d_too, slice(2 * BLOCK, 3 * BLOCK)), 0, 0).astype(jnp.bfloat16)
+    left = both(acts, acts_too, slice(width, 2 * width))
+    g[3] = mm(left, both(d, d_too, slice(3 * BLOCK, 4 * BLOCK)), 0, 0).astype(jnp.bfloat16)
+    start_grads(plan, "attend", ids, g, outs, sem, rows_first)
+    wait_all(g, sem)
+
+
+def feed_backward(plan, layer, ids, d_out, resid, slope, small, *refs):
     a = plan_inputs(plan, "up")
     b = plan_inputs(plan, "down")
     up_refs = weight_refs(plan, "up", refs[:a])
     down_refs = weight_refs(plan, "down", refs[a : a + b])
-    keep, send, d_resid, sums, wu, wd, g, sem_u, sem_d, sem_g = refs[a + b :]
+    own, send, d_resid, sums, wu, wd, sem_u, sem_d = refs[a + b :]
     width = plan.width
     start_weights(plan, layer, "down", ids, *down_refs, wd, sem_d)
     start_weights(plan, layer, "up", ids, *up_refs, wu, sem_u)
     d = d_out[...]
-    low = normed[...]
     wait_all(wd, sem_d)
     total = None
     for j in range(PARTS):
         lanes = slice(j * width, (j + 1) * width)
         d_up = (mm(d, wd[lanes, :], 1, 1) * slope[:, lanes]).astype(jnp.bfloat16)
-        g[j] = mm(low, d_up, 0, 0).astype(jnp.bfloat16)
+        split(ids[0] == 0, own, send, j * BLOCK, d_up)
         if j == 0:
             wait_all(wu, sem_u)
         part = mm(d_up, wu[j], 1, 1)
         total = part if total is None else total + part
-    start_grads(plan, "up", ids, g, keep, send, sem_g)
     hat, scale = normalize(resid[...])
     sums[0:1, :] = jnp.sum(total * hat, axis=0, keepdims=True)
     sums[1:2, :] = jnp.sum(total, axis=0, keepdims=True)
     d_resid[...] = d.astype(jnp.float32) + norm_backward(total, hat, scale, small[2:3, :])
-    wait_all(g, sem_g)
-
-
-def attend_backward(plan, layer, ids, x_ref, d_resid, normed, qkv, probs, mixed, small, cosv, sinv, *refs):
+
+
+def attend_backward(plan, layer, ids, x_ref, d_resid, qkv, probs, small, cosv, sinv, *refs):
     a = plan_inputs(plan, "attend")
-    own, others, whole = weight_refs(plan, "attend", refs[:a])
-    keep, send, dx, sums, w, g, d_mixed, d_qkv, sem_w, sem_g = refs[a:]
+    shard, others, whole = weight_refs(plan, "attend", refs[:a])
+    own, send, dx, sums, w, d_mixed, d_qkv, sem_w = refs[a:]
     width = plan.width
-    start_weights(plan, layer, "attend", ids, own, others, whole, w, sem_w)
+    first = ids[0] == 0
+    start_weights(plan, layer, "attend", ids, shard, others, whole, w, sem_w)
     d = d_resid[...].astype(jnp.bfloat16)
-    g[3] = mm(mixed[...], d, 0, 0).astype(jnp.bfloat16)
+    split(first, own, send, 3 * BLOCK, d)
     wait_all(w, sem_w)
     d_mixed[...] = mm(d, w[3], 1, 1).astype(jnp.bfloat16)
 
@@ -350,20 +384,18 @@
         return carry
 
     lax.fori_loop(0, width // LANES, tile, 0)
-    low = normed[...]
     total = None
     for j in range(3):
         part_in = d_qkv[:, j * width : (j + 1) * width]
-        g[j] = mm(low, part_in, 0, 0).astype(jnp.bfloat16)
+        split(first, own, send, j * BLOCK, part_in)
         part = mm(part_in, w[j], 1, 1)
         total = part if total is None else total + part
-    start_grads(plan, "attend", ids, g, keep, send, sem_g)
     hat, scale = normalize(x_ref[...].astype(jnp.float32))
     sums[0:1, :] = jnp.sum(total * hat, axis=0, keepdims=True)
     sums[1:2, :] = jnp.sum(total, axis=0, keepdims=True)
-    back = d_resid[...] + norm_backward(total, hat, scale, small[0:1, :])
-    dx[...] = back.astype(jnp.bfloat16)
-    wait_all(g, sem_g)
+    back = (d_resid[...] + norm_backward(total, hat, scale, small[0:1, :])).astype(jnp.bfloat16)
+    dx[...] = back
+    split(first, own, send, 4 * BLOCK, back)
 
 
 def pack(plan, ids, qkv, out, up, down, keep, send):
@@ -382,22 +414,23 @@
             at += 1
 
 
-def final_layout(plan, kind, ids, x, *outs):
+def final_layout(plan, kind, ids, low_own, low_got, high_own, high_got, *outs):
     width, tall = plan.width, plan.tall
-    core, group = ids[0], ids[1]
+    group = ids[1]
+    first = ids[0] == 0
     tables = masks_of(plan.groups, False)
-    for j in range(plan.groups):
-        peer = group ^ pick(core == 0, tables[0][j], tables[1][j])
-        for h in range(2):
-            for b in range(PARTS):
-                value = x[j, h ^ core, b].astype(jnp.float32)
+    for h, (a, b) in enumerate(((low_own, high_got), (low_got, high_own))):
+        for j in range(plan.groups):
+            peer = group ^ tables[h][j]
+            for p in range(PARTS):
+                value = jnp.where(first, a[j, p], b[j, p]).astype(jnp.float32)
                 if kind == "down":
-                    at = pl.multiple_of(peer * (tall * PARTS) + b * tall, 8)
+                    at = pl.multiple_of(peer * (tall * PARTS) + p * tall, 8)
                     outs[0][0, pl.ds(at, tall), h * BLOCK : (h + 1) * BLOCK] = value
                     continue
                 at = pl.multiple_of(peer * tall, 8)
-                out = outs[-1] if kind == "attend" and b == PARTS - 1 else outs[0]
-                c = 0 if kind == "attend" and b == PARTS - 1 else b
+                out = outs[-1] if kind == "attend" and p == PARTS - 1 else outs[0]
+                c = 0 if kind == "attend" and p == PARTS - 1 else p
                 lanes = slice(c * width + h * BLOCK, c * width + (h + 1) * BLOCK)
                 out[0, pl.ds(at, tall), lanes] = value
 
@@ -417,9 +450,14 @@
 
 
 DEPTH = 2
-DEPTH_BACK = 3
-SHIFT = 0
-ROWS_FIRST = ()
+DEPTH_BACK = 9
+EARLY = "down"
+LATE = 2
+GATHERS = {"upper": (1, ("down", "up", "attend")), "feed": (0, ("down", "up")), "attend": (0, ("attend",))}
+SHIFT = 1
+OLD = False
+BESIDE = 0
+ROWS_FIRST = ((1, "down"),)
 
 VMEM = pl.BlockSpec(memory_space=pltpu.VMEM)
 SMEM = pl.BlockSpec(memory_space=pltpu.SMEM)
@@ -463,13 +501,12 @@
             (self.ids, self.lens, x, small, *self.tables, *weights),
             [SMEM, SMEM] + [VMEM] * 4 + [HBM] * len(weights),
             (
-                shape((t, d), BF),
                 shape((t, 3 * d), BF),
                 shape((self.heads, t, t), F32),
-                shape((t, d), BF),
+                shape((t, 2 * d), BF),
                 shape((t, d), F32),
             ),
-            (VMEM,) * 5,
+            (VMEM,) * 4,
             [self.part, pltpu.VMEM((t, t), F32), self.sem],
             2 * t * d * d * 4 + 4 * self.heads * t * t * LANES,
         )
@@ -483,68 +520,93 @@
             (self.ids, resid, small, *weights),
             [SMEM, VMEM, VMEM] + [HBM] * len(weights),
             (
-                shape((t, d), BF),
-                shape((t, PARTS * d), BF),
+                shape((t, (PARTS + 1) * d), BF),
                 shape((t, PARTS * d), F32),
                 shape((t, d), BF),
             ),
-            (VMEM,) * 4,
+            (VMEM,) * 3,
             [self.part, self.tall, self.sem, self.sem],
             2 * t * d * d * 8,
         )
 
-    def grads(self, kind):
+    def weight_grad(self, layer, kind, body, args, specs, flops):
         p = self.plan
-        rows = p.tall * PARTS if kind == "down" else None
         if not p.direct:
             dims = (PARTS * p.width, BLOCK) if kind == "down" else (PARTS, p.width, BLOCK)
-        elif kind == "down":
-            dims = (p.groups, p.rows, rows, BLOCK)
+            outs = (shape(dims, BF),)
         else:
-            dims = (p.groups, p.rows, PARTS, p.tall, BLOCK)
-        return (shape(dims, BF), shape(dims, BF))
-
-    def down_grad(self, layer, active, d_out):
+            halved = (p.groups, p.rows // 2) if p.rows_first(layer, kind) else (p.groups // 2, p.rows)
+            piece = (p.tall * PARTS, BLOCK) if kind == "down" else (PARTS, p.tall, BLOCK)
+            outs = (shape((*halved, *piece), BF),) * 2
+        dims = (PARTS * p.width, BLOCK) if kind == "down" else (PARTS, p.width, BLOCK)
+        return pl.pallas_call(
+            body,
+            out_shape=outs,
+            grid_spec=pltpu.PrefetchScalarGridSpec(
+                num_scalar_prefetch=1,
+                grid=(1,),
+                in_specs=specs,
+                out_specs=(HBM,) * len(outs),
+                scratch_shapes=[pltpu.VMEM(dims, BF), self.sem],
+            ),
+            name=f"{kind}_grad_{layer}",
+            cost_estimate=pl.CostEstimate(flops=flops, transcendentals=0, bytes_accessed=1 << 22),
+        )(self.ids, *args)
+
+    def down_grad(self, layer, acts, d, at):
         p = self.plan
-        return call(
-            functools.partial(down_grad, p),
-            f"down_grad_{layer}",
-            (self.ids, active, d_out),
-            [SMEM, VMEM, VMEM],
-            self.grads("down"),
-            (HBM, HBM),
-            [self.tall, self.sem],
-            2 * p.tok * p.width * p.width * 4,
+        left = pl.BlockSpec((p.tok, PARTS * p.width), lambda i, ids: (0, 0))
+        right = pl.BlockSpec(d[0].shape, lambda i, ids: (0, 0))
+        flops = 4 * p.tok * p.width * PARTS * BLOCK
+        return self.weight_grad(
+            layer, "down", functools.partial(down_grad, p, p.rows_first(layer, "down"), at), (*acts, *d), [left] * 2 + [right] * 2, flops
         )
 
-    def feed_backward(self, layer, d_out, resid, normed, slope, small, weights):
+    def up_grad(self, layer, acts, d):
+        p = self.plan
+        left = pl.BlockSpec((p.tok, p.width), lambda i, ids: (0, PARTS))
+        right = pl.BlockSpec(d[0].shape, lambda i, ids: (0, 0))
+        flops = 4 * p.tok * p.width * PARTS * BLOCK
+        return self.weight_grad(
+            layer, "up", functools.partial(up_grad, p, p.rows_first(layer, "up")), (*acts, *d), [left] * 2 + [right] * 2, flops
+        )
+
+    def attend_grad(self, layer, acts, d):
+        p = self.plan
+        left = pl.BlockSpec(acts[0].shape, lambda i, ids: (0, 0))
+        right = pl.BlockSpec(d[0].shape, lambda i, ids: (0, 0))
+        flops = 4 * p.tok * p.width * PARTS * BLOCK
+        return self.weight_grad(
+            layer, "attend", functools.partial(attend_grad, p, p.rows_first(layer, "attend")), (*acts, *d), [left] * 2 + [right] * 2, flops
+        )
+
+    def feed_backward(self, layer, d_out, resid, slope, small, weights):
         p = self.plan
         t, d = p.tok, p.width
         return call(
             functools.partial(feed_backward, p, layer),
             f"feed_backward_{layer}",
-            (self.ids, d_out, resid, normed, slope, small, *weights),
-            [SMEM] + [VMEM] * 5 + [HBM] * len(weights),
-            (*self.grads("up"), shape((t, d), F32), shape((2, d), F32)),
-            (HBM, HBM, VMEM, VMEM),
-            [self.part, self.tall, self.part, self.sem, self.sem, self.sem],
-            2 * t * d * d * 12,
+            (self.ids, d_out, resid, slope, small, *weights),
+            [SMEM] + [VMEM] * 4 + [HBM] * len(weights),
+            (*(shape((t, PARTS * BLOCK), BF),) * 2, shape((t, d), F32), shape((2, d), F32)),
+            (VMEM,) * 4,
+            [self.part, self.tall, self.sem, self.sem],
+            2 * t * d * d * 8,
         )
 
-    def attend_backward(self, layer, x, d_resid, normed, qkv, probs, mixed, small, weights):
+    def attend_backward(self, layer, x, d_resid, qkv, probs, small, weights):
         p = self.plan
         t, d = p.tok, p.width
         return call(
             functools.partial(attend_backward, p, layer),
             f"attend_backward_{layer}",
-            (self.ids, x, d_resid, normed, qkv, probs, mixed, small, *self.tables, *weights),
-            [SMEM] + [VMEM] * 9 + [HBM] * len(weights),
-            (*self.grads("attend"), shape((t, d), BF), shape((2, d), F32)),
-            (HBM, HBM, VMEM, VMEM),
-            [self.part, self.part, pltpu.VMEM((t, d), BF), pltpu.VMEM((t, 3 * d), BF), self.sem, self.sem],
-            2 * t * d * d * 8 + 10 * self.heads * t * t * LANES,
+            (self.ids, x, d_resid, qkv, probs, small, *self.tables, *weights),
+            [SMEM] + [VMEM] * 7 + [HBM] * len(weights),
+            (*(shape((t, (PARTS + 1) * BLOCK), BF),) * 2, shape((t, d), BF), shape((2, d), F32)),
+            (VMEM,) * 4,
+            [self.part, pltpu.VMEM((t, d), BF), pltpu.VMEM((t, 3 * d), BF), self.sem],
+            2 * t * d * d * 4 + 10 * self.heads * t * t * LANES,
         )
-
 
     def pack(self, shards):
         p = self.plan
@@ -563,21 +625,25 @@
             name="pack",
         )(self.ids, *shards)
 
-    def final(self, kind, x):
+    def final(self, kind, sources):
         p = self.plan
         share, d = p.width // p.rows, p.width
         dims = {"attend": ((share, 3 * d), (share, d)), "up": ((share, PARTS * d),), "down": ((share * PARTS, d),)}
         outs = tuple(shape((1, *dim), F32) for dim in dims[kind])
-        return call(
+        specs = []
+        for x, at in sources:
+            specs.append(pl.BlockSpec((p.groups, PARTS, p.tall, BLOCK), lambda i, ids, at=at: (0, at, 0, 0)))
+        return pl.pallas_call(
             functools.partial(final_layout, p, kind),
-            f"final_{kind}",
-            (self.ids, x),
-            [SMEM, VMEM],
-            outs,
-            (VMEM,) * len(outs),
-            [],
-            0,
-        )
+            out_shape=outs,
+            grid_spec=pltpu.PrefetchScalarGridSpec(
+                num_scalar_prefetch=1,
+                grid=(1,),
+                in_specs=specs,
+                out_specs=tuple(pl.BlockSpec(o.shape, lambda i, ids: (0, 0, 0)) for o in outs),
+            ),
+            name=f"final_{kind}",
+        )(self.ids, *(x for x, _ in sources))
 
 
 def swap_cores(x):
@@ -653,19 +719,16 @@
     return jnp.stack(halves)
 
 
-def ordered_grads(plan, kind, core, group, row, keep, send):
+def ordered_grads(plan, kind, core, group, row, x):
     groups, rows, tall = plan.groups, plan.rows, plan.tall
     tables = jnp.array(masks_of(groups, False), jnp.int32)
-    outs = []
-    for x, half in ((keep, core), (send, 1 - core)):
-        if kind == "down":
-            x = x.reshape(rows, groups, PARTS, tall, BLOCK).transpose(1, 0, 2, 3, 4)
-        else:
-            x = x.reshape(PARTS, rows, groups, tall, BLOCK).transpose(2, 1, 0, 3, 4)
-        x = jnp.take(x, group ^ jnp.where(half == 0, tables[0], tables[1]), axis=0)
-        x = jnp.take(x, jnp.stack([row_to(plan, row, k) for k in range(rows)]), axis=1)
-        outs.append(x)
-    return outs
+    if kind == "down":
+        x = x.reshape(rows, groups, PARTS, tall, BLOCK).transpose(1, 0, 2, 3, 4)
+    else:
+        x = x.reshape(PARTS, rows, groups, tall, BLOCK).transpose(2, 1, 0, 3, 4)
+    x = jnp.take(x, group ^ jnp.where(core == 0, tables[0], tables[1]), axis=0)
+    x = jnp.take(x, jnp.stack([row_to(plan, row, k) for k in range(rows)]), axis=1)
+    return x[: groups // 2], x[groups // 2 :]
 
 
 def on_device(
@@ -733,10 +796,10 @@
         x = gate(xs[layer], after)
         out = kernels.attend_forward(layer, x, smalls[layer], weights_of(layer, "attend"))
         saved[layer, "attend"] = out
-        return out[4]
+        return out[3]
 
     def run_feed(layer, after):
-        resid = gate(saved[layer, "attend"][4], after)
+        resid = gate(saved[layer, "attend"][3], after)
         weights = weights_of(layer, "up") + weights_of(layer, "down")
         *out, y = kernels.feed_forward(layer, resid, smalls[layer], weights)
         saved[layer, "feed"] = out
@@ -748,7 +811,7 @@
     depth = hops + stages
     kernel_at = {depth + SHIFT: (run_attend, 0), depth + 2 + SHIFT: (run_feed, 0), depth + 3 + SHIFT: (run_attend, 1)}
     small_steps = row_bits + [0]
-    gotten = {}
+    gotten, to_swap, acts_too = {}, {}, {}
     for slot in range(n_chunks + depth + 1):
         after = history.get(slot - DEPTH, [])
         done = []
@@ -802,40 +865,73 @@
             kind = KINDS[slot - 1]
             theirs[kind] = tuple(swap_cores(gate(w, history[slot - 1])) for w in shards[kind])
             done += theirs[kind]
+        for (layer, kind), acts in list(to_swap.items()):
+            acts_too[layer, kind] = swap_cores(gate(acts, after))
+            done.append(acts_too[layer, kind])
+            del to_swap[layer, kind]
         if slot in kernel_at:
             run, layer = kernel_at[slot]
             done.append(run(layer, history[slot - 1]))
+            if run is run_attend:
+                to_swap[layer, "attend"] = saved[layer, "attend"][2]
+            else:
+                to_swap[layer, "feed"] = saved[layer, "feed"][0]
         history[slot] = done
     run_feed(1, [])
-
-    grads, backs, sums = {}, [None, None], {}
+    to_swap[1, "feed"] = saved[1, "feed"][0]
+    for (layer, kind), acts in to_swap.items():
+        acts_too[layer, kind] = swap_cores(acts)
+
+    backs, sums, d_cols = [None, None], {}, {}
     order = [(layer, kind) for layer in (1, 0) for kind in ("down", "up", "attend")]
-
-    def run_backward(flow, layer, kind, after):
-        normed, qkv, probs, mixed, resid = saved[layer, "attend"]
-        normed_two, active, slope = saved[layer, "feed"]
-        d_out, d_resid = flow
-        if kind == "down":
-            return kernels.down_grad(layer, active, gate(d_out, after)), flow
-        if kind == "up":
-            weights = weights_of(layer, "up") + weights_of(layer, "down")
-            *g, d_resid, sums[layer, kind] = kernels.feed_backward(
-                layer, gate(d_out, after), resid, normed_two, slope, smalls[layer], weights
-            )
-            return g, (d_out, d_resid)
-        *g, d_x, sums[layer, kind] = kernels.attend_backward(
+    halves = lax.dynamic_slice_in_dim(cotangent, core * BLOCK, BLOCK, 2)
+    d_cols[2, "attend"] = (
+        lax.dynamic_index_in_dim(halves, core, 0, False),
+        lax.dynamic_index_in_dim(halves, 1 - core, 0, False),
+    )
+    d_outs = {1: cot}
+    d_resids = {}
+
+    def chain_feed(layer, after):
+        weights = weights_of(layer, "up") + weights_of(layer, "down")
+        resid, slope = saved[layer, "attend"][3], saved[layer, "feed"][1]
+        own, send, d_resids[layer], sums[layer, "up"] = kernels.feed_backward(
+            layer, gate(d_outs[layer], after), resid, slope, smalls[layer], weights
+        )
+        d_cols[layer, "up"] = (own, swap_cores(send))
+        return send
+
+    def chain_attend(layer, after):
+        qkv, probs = saved[layer, "attend"][:2]
+        own, send, dx, sums[layer, "attend"] = kernels.attend_backward(
             layer,
             xs[layer],
-            gate(d_resid, after),
-            normed,
+            gate(d_resids[layer], after),
             qkv,
             probs,
-            mixed,
             smalls[layer],
             weights_of(layer, "attend"),
         )
-        backs[layer] = d_x
-        return g, (d_x, d_resid)
+        d_cols[layer, "attend"] = (own, swap_cores(send))
+        backs[layer] = d_outs[layer - 1] = dx
+        return send
+
+    def weight_grad(layer, kind, after):
+        if kind == "attend":
+            acts = (saved[layer, "attend"][2], acts_too[layer, "attend"])
+            own, other = d_cols[layer, "attend"]
+            outs = kernels.attend_grad(layer, acts, (gate(own, after), other))
+        else:
+            acts = (saved[layer, "feed"][0], acts_too[layer, "feed"])
+            own, other = d_cols[layer, "up"] if kind == "up" else d_cols[layer + 1, "attend"]
+            d = (gate(own, after), other)
+            if kind == "up":
+                outs = kernels.up_grad(layer, acts, d)
+            else:
+                outs = kernels.down_grad(layer, acts, d, 0 if layer == 1 else PARTS * BLOCK)
+        if not plan.direct:
+            return ordered_grads(plan, kind, core, group, row, outs[0])
+        return [x.reshape(*x.shape[:2], PARTS, plan.tall, BLOCK) for x in outs]
 
     def total_of(parts):
         total = parts[0].astype(F32)
@@ -843,25 +939,22 @@
             total = total + part.astype(F32)
         return total.astype(BF)
 
-    def ready(kind, keep, send):
-        if plan.direct:
-            dims = (groups, rows, PARTS, plan.tall, BLOCK)
-            return {"sum": [keep.reshape(dims), send.reshape(dims)]}
-        return {"sum": ordered_grads(plan, kind, core, group, row, keep, send)}
-
-    def way_of(kind):
+    def way_of(layer, kind):
         over_groups = [(0, i) for i in range(stages)]
         over_rows = [(1, bit) for bit in row_bits] if few else [(1, 0)]
-        return over_rows + over_groups if few and kind in ROWS_FIRST else over_groups + over_rows
-
-    last = 1 + stages + hops
-
-    def step(kind, parts, stage, after):
+        return over_rows + over_groups if plan.rows_first(layer, kind) else over_groups + over_rows
+
+    last = stages + hops
+
+    def step(layer, kind, parts, stage, after):
         if stage == 0:
-            parts["sum"] = [parts["sum"][0], swap_cores(gate(parts["sum"][1], after))]
-            parts["left"] = [groups, rows]
-            return parts["sum"][1]
-        axis, bit = way_of(kind)[stage - 1]
+            send = gate(parts["send"], after)
+            axis, bit = way_of(layer, kind)[0]
+            got = swap_rows(send, bit) if axis else swap_groups(send, groups, bit)
+            parts["sum"] = [parts["keep"], got]
+            parts["left"] = list(parts["keep"].shape[:2])
+            return got
+        axis, bit = way_of(layer, kind)[stage]
         if axis == 1 and not few:
             send = total_of([p[0] for p in parts["sum"]])
             held = jnp.argsort(jnp.stack([row_to(plan, row, k) for k in range(rows)]))
@@ -875,6 +968,7 @@
         send = total_of([p[low[0] : high[0], low[1] : high[1]] for p in parts["sum"]])
         parts["left"][axis] //= 2
         send = gate(send, after)
+        sends.append(send)
         got = swap_groups(send, groups, bit) if axis == 0 else swap_rows(send, bit)
         parts["sum"] = parts["sum"] + [got]
         return got
@@ -882,35 +976,83 @@
     def result_of(parts):
         return total_of([p[:1, 0] for p in parts["sum"]])
 
-    history = {}
-    flow = (cot, None)
-    g, flow = run_backward(flow, *order[0], [])
-    live = {0: ready(order[0][1], *g)}
-    final = {}
-    small_sum, small_stage = None, 0
+    def home(low, high):
+        got = swap_cores(jnp.where(first, high, low))
+        keep = jnp.where(first, low, high)
+        return jnp.where(first, jnp.stack([keep, got]), jnp.stack([got, keep]))
+
+    layer_out = home(xs[1], xs[2])
+    history, sends = {}, []
+    chain_feed(1, [])
+    keep, send = weight_grad(*order[0], [])
+    live = {0: {"keep": keep, "send": send}}
+    def outside(x):
+        return x.transpose(0, 3, 2, 1, 4).reshape(1, share, -1).astype(F32)
+
+    def result_for(kind):
+        sources = []
+        for source_layer in range(2):
+            for name, (layer, kinds) in gathers.items():
+                if layer == source_layer and kind in kinds:
+                    sources += [(x, kinds.index(kind)) for x in final[name]]
+        if plan.direct:
+            return kernels.final(kind, sources)
+        parts = [x[:, i * PARTS : (i + 1) * PARTS] for x, i in sources]
+        tables = jnp.array(masks_of(groups, False), jnp.int32)
+        low = jnp.take(jnp.where(first, parts[0], parts[3]), jnp.argsort(group ^ tables[0]), axis=0)
+        high = jnp.take(jnp.where(first, parts[1], parts[2]), jnp.argsort(group ^ tables[1]), axis=0)
+        x = jnp.stack([low, high], axis=1)
+        if kind == "attend":
+            return (outside(x[:, :, 0:3]), outside(x[:, :, 3:4]))
+        if kind == "up":
+            return (outside(x),)
+        return (x.transpose(0, 2, 3, 1, 4).reshape(1, -1, width).astype(F32),)
+
+    final, results = {}, {}
+    gathers = GATHERS
+    small_sum, small_stage, smalls_seen = None, 0, []
+    beside = [[(chain_attend, 1)], [(chain_feed, 0)], [(chain_attend, 0)], [], []]
     for slot in range(n_chunks + last + stages + 1):
         after = history.get(slot - DEPTH_BACK, [])
         done = []
+        sends.clear()
         for c in range(n_chunks):
             if 0 <= slot - c < last:
-                done.append(step(order[c][1], live[c], slot - c, after))
-        for i, kind in enumerate(("down", "up", "attend")):
-            stage = slot - (i + len(KINDS) + last)
+                held = smalls_seen[-LATE : len(smalls_seen) - LATE + 1] if LATE and c == n_chunks - 1 else []
+                done.append(step(*order[c], live[c], slot - c, after + held))
+        for name, (layer, kinds) in gathers.items():
+            stage = slot - last - max(order.index((layer, kind)) for kind in kinds)
             if stage == 0:
-                low, high = (result_of(live[order.index((layer, kind))]) for layer in range(2))
-                other = swap_cores(jnp.where(first, high, low))
-                final[kind] = jnp.stack([jnp.where(first, low, high), other], axis=1)
-                done.append(other)
-            elif 1 <= stage <= stages:
-                got = swap_groups(gate(final[kind], after), groups, stages - stage)
-                final[kind] = jnp.concatenate([final[kind], got], axis=0)
-                done.append(got)
+                final[name] = jnp.concatenate([result_of(live[order.index((layer, k))]) for k in kinds], axis=1)
+            if 0 <= stage < stages:
+                got = swap_groups(final[name], groups, stages - 1 - stage)
+                final[name] = jnp.concatenate([final[name], got], axis=0)
+            elif stage == stages:
+                held = final[name]
+                if name == "attend":
+                    held = gate(held, [layer_out, input_grad, *results[EARLY]] if EARLY else [layer_out, input_grad])
+                got = lax.ppermute(held, "section", [(1 - layer, layer)])
+                final[name] = (final[name], got)
+                if name == "feed":
+                    for kind in ("down", "up"):
+                        results[kind] = result_for(kind)
         if slot + 1 < n_chunks:
-            layer, kind = order[slot + 1]
-            g, flow = run_backward(flow, layer, kind, history.get(slot - 1, []))
-            live[slot + 1] = ready(kind, *g)
-            done.append(flow[0] if kind == "attend" else flow[1] if kind == "up" else g[0])
+            before = history.get(slot - 1, []) if OLD else list(sends)
+            now = done[-BESIDE:] if BESIDE else []
+            extra = []
+            for run, layer in beside[slot]:
+                if order[slot + 1][1] == "down":
+                    continue
+                extra.append(run(layer, before))
+            keep, send = weight_grad(*order[slot + 1], extra or before)
+            live[slot + 1] = {"keep": keep, "send": gate(send, now)}
+            if order[slot + 1][1] == "down":
+                for run, layer in beside[slot]:
+                    extra.append(run(layer, [send]))
+            if OLD:
+                done.append(send)
         if slot + 1 == n_chunks:
+            input_grad = home(*backs)
             small_sum = jnp.stack([jnp.concatenate([sums[i, "attend"], sums[i, "up"]]) for i in range(2)])
         if small_sum is not None and small_stage <= stages + len(row_bits):
             held = gate(small_sum, history.get(slot - 1, []))
@@ -922,33 +1064,12 @@
                 got = swap_rows(held, row_bits[small_stage - stages - 1])
             small_stage += 1
             small_sum = small_sum + got
+            smalls_seen.append(small_sum)
         history[slot] = done
 
-    def home(low, high):
-        got = swap_cores(jnp.where(first, high, low))
-        keep = jnp.where(first, low, high)
-        return jnp.where(first, jnp.stack([keep, got]), jnp.stack([got, keep]))
-
-    layer_out = home(xs[1], xs[2])
-    input_grad = home(*backs)
-
-    def outside(x):
-        return x.transpose(0, 3, 2, 1, 4).reshape(1, share, -1).astype(F32)
-
-    if plan.direct:
-        qkv_grad, out_grad = kernels.final("attend", final["attend"])
-        (up_grad,) = kernels.final("up", final["up"])
-        (down_grads,) = kernels.final("down", final["down"])
-    else:
-        tables = jnp.array(masks_of(groups, False), jnp.int32)
-        at = jnp.argsort(group ^ jnp.where(first, tables[0], tables[1]))
-        for kind in KINDS:
-            x = jnp.take(final[kind], at, axis=0)
-            final[kind] = jnp.take(x, jnp.arange(2) ^ core, axis=1)
-        qkv_grad = outside(final["attend"][:, :, 0:3])
-        out_grad = outside(final["attend"][:, :, 3:4])
-        up_grad = outside(final["up"])
-        down_grads = final["down"].transpose(0, 2, 3, 1, 4).reshape(1, -1, width).astype(F32)
+    qkv_grad, out_grad = result_for("attend")
+    (up_grad,) = results["up"]
+    (down_grads,) = results["down"]
 
     small_grads = small_sum
     own = lax.dynamic_index_in_dim(small_grads, core, 0, False)

time: 426 us -> 415 us (0.974)
  waiting for transfers between devices: 153 us -> 119 us
  starting transfers between devices: 71 us -> 93.2 us
  Pallas kernels: 118 us -> 135 us
  other arithmetic: 56.1 us -> 45.8 us
  local copies, waits for them, and re-layouts: 18.6 us -> 13.1 us
    pallas_call x0 -> x9, Pallas kernels: none -> 45.8 us  [the longest x6 34.1 us: weight_grad(): pl.pallas_call(body, out_shape=outs, grid_spec=pltpu.PrefetchScalarGridSp...]
    ppermute x32, waiting for transfers between devices: 83.1 us -> 48.6 us  [swap_groups(): return lax.ppermute(x, ('section', 'group'), pairs)]
    pallas_call x13 -> x8, Pallas kernels: 115 us -> 86 us  [call(): pl.pallas_call(body, out_shape=outs, in_specs=specs, out_specs=out_specs,...]
    ppermute x32, starting transfers between devices: 34.7 us -> 44.9 us  [swap_groups(): return lax.ppermute(x, ('section', 'group'), pairs)]
    convert_element_type x24, other arithmetic: 32.9 us -> 25.9 us  [total_of(): return total.astype(BF)]
    ppermute x0 -> x3, starting transfers between devices: none -> 5.51 us  [on_device(): got = lax.ppermute(held, 'section', [(1 - layer, layer)])]
  transfers between devices with their start and end apart: 90 -> 92, of which waited for: 35 -> 33; matrix products, arithmetic and copies ran while one was open for 16% -> 13% of each run, Pallas kernels for 23% -> 29%
where the time goes in v3:
time: 415 us; the launch traced here: 408 us
  Pallas kernels  135 us (33%)
  waiting for transfers between devices  119 us (29%)
  starting transfers between devices  93.2 us (22%)
  other arithmetic  45.8 us (11%)
  local copies, waits for them, and re-layouts  13.1 us (3%)
    pallas_call x8, Pallas kernels, call(): pl.pallas_call(body, out_shape=outs, in_specs=specs, out_specs=out_specs,...  86 us
    ppermute x28, waiting for transfers between devices, swap_rows(): return lax.ppermute(x, 'dp', [(i, i ^ bit) for i in range(rows)])  69.6 us
    ppermute x32, waiting for transfers between devices, swap_groups(): return lax.ppermute(x, ('section', 'group'), pairs)  48.6 us
    ppermute x32, starting transfers between devices, swap_groups(): return lax.ppermute(x, ('section', 'group'), pairs)  44.9 us
    ppermute x28, starting transfers between devices, swap_rows(): return lax.ppermute(x, 'dp', [(i, i ^ bit) for i in range(rows)])  35.2 us
    pallas_call x6, Pallas kernels, weight_grad(): pl.pallas_call(body, out_shape=outs, grid_spec=pltpu.PrefetchScalarGridSp...  34.1 us
    convert_element_type x24, other arithmetic, total_of(): return total.astype(BF)  25.9 us
    pallas_call x3, Pallas kernels, final(): pl.pallas_call(functools.partial(final_layout, p, kind), out_shape=outs,...  11.7 us
  transfers between devices with their start and end apart: 92, of which 33 were waited for; matrix products, arithmetic and copies ran while one was open for 13% of the time, Pallas kernels for 29%

profile of v3, /device:TPU:0, one launch (start us, length us, event | category | flops | bytes accessed | tf_op | source)
XLA Modules:
  0.0 407.9 jit_solution(6827661084457683134)
XLA Ops:
  12.3 7.4 %collective-permute-done.1 = bf16[1,1,4,48,384]{4,3,2,1,0:T(8,128)(2,1)S(1)} collective-permute-done((bf16[1,1,4,48,384]{4,3,2,1,0:T(8,128)(2,1)S(1)}, bf16[1,1,4,48,384]{4,3,2,1,0:T(8,128)(2,1)S(1)}, u32[]{:S(2)}, u32[]{:S(2)}) %collective-permute-start.1) | collective-permute-done | bytes 147488 | tf_op jit(solution)/shard_map/ppermute | solution.py:677
  25.9 6.6 %collective-permute-done.5 = bf16[1,1,4,48,384]{4,3,2,1,0:T(8,128)(2,1)S(1)} collective-permute-done((bf16[1,1,4,48,384]{4,3,2,1,0:T(8,128)(2,1)S(1)}, bf16[1,1,4,48,384]{4,3,2,1,0:T(8,128)(2,1)S(1)}, u32[]{:S(2)}, u32[]{:S(2)}) %collective-permute-start.5) | collective-permute-done | bytes 147488 | tf_op jit(solution)/shard_map/ppermute | solution.py:677
  52.9 7.0 %collective-permute-done.18 = bf16[1,2,4,48,384]{4,3,2,1,0:T(8,128)(2,1)S(1)} collective-permute-done((bf16[1,2,4,48,384]{4,3,2,1,0:T(8,128)(2,1)S(1)}, bf16[1,2,4,48,384]{4,3,2,1,0:T(8,128)(2,1)S(1)}, u32[]{:S(2)}, u32[]{:S(2)}) %collective-permute-start.18) | collective-permute-done | bytes 294944 | tf_op jit(solution)/shard_map/ppermute | solution.py:677
  91.5 6.5 %collective-permute-done.30 = bf16[1,2,4,48,384]{4,3,2,1,0:T(8,128)(2,1)S(1)} collective-permute-done((bf16[1,2,4,48,384]{4,3,2,1,0:T(8,128)(2,1)S(1)}, bf16[1,2,4,48,384]{4,3,2,1,0:T(8,128)(2,1)S(1)}, u32[]{:S(2)}, u32[]{:S(2)}) %collective-permute-start.30) | collective-permute-done | bytes 294944 | tf_op jit(solution)/shard_map/ppermute | solution.py:677
  106.8 10.1 %attend_forward_0.1 = (bf16[256,2304]{1,0:T(8,128)(2,1)}, f32[12,256,256]{2,1,0:T(8,128)}, bf16[256,1536]{1,0:T(8,128)(2,1)}, f32[256,768]{1,0:T(8,128)}) custom-call(s32[3]{0:T(128)} %pad_add_fusion.ids, s32[3]{0:T(128)} %get-tuple-element.211.lens, bf16[256,768]{1,0:T(8,128)(2,1)} %dynamic-slice_bitcast_fusion.1.x_ref, f32[4,768]{1,0:T(4,128)} %squeeze.25.small, ...), custom_call_target="tpu_custom_call" | custom-call | flops 1610612736 | bytes 12464152 | tf_op jit(solution)/shard_map/attend_forward_0/pallas_call | solution.py:469
  122.0 5.2 %collective-permute-done.40 = bf16[1,3,4,48,384]{4,3,2,1,0:T(8,128)(2,1)S(1)} collective-permute-done((bf16[1,3,4,48,384]{4,3,2,1,0:T(8,128)(2,1)S(1)}, bf16[1,3,4,48,384]{4,3,2,1,0:T(8,128)(2,1)S(1)}, u32[]{:S(2)}, u32[]{:S(2)}) %collective-permute-start.40) | collective-permute-done | bytes 442400 | tf_op jit(solution)/shard_map/ppermute | solution.py:663
  136.0 9.7 %feed_forward_0.1 = (bf16[256,3840]{1,0:T(8,128)(2,1)}, f32[256,3072]{1,0:T(8,128)}, bf16[256,768]{1,0:T(8,128)(2,1)}) custom-call(s32[3]{0:T(128)} %pad_add_fusion.ids, f32[256,768]{1,0:T(8,128)} %get-tuple-element.142.resid, f32[4,768]{1,0:T(4,128)} %squeeze.25.small, bf16[1,192,3072]{2,1,0:T(8,128)(2,1)} %refs_0_.14, bf16[1,192,3072]{2,1,0:T(8,128)(2,1)} %copy-done.6, ...), custom_call_target="tpu_custom_call" | custom-call | flops 2415919104 | bytes 18100236 | tf_op jit(solution)/shard_map/feed_forward_0/pallas_call | solution.py:469
  147.8 10.0 %attend_forward_1.1 = (bf16[256,2304]{1,0:T(8,128)(2,1)}, f32[12,256,256]{2,1,0:T(8,128)}, bf16[256,1536]{1,0:T(8,128)(2,1)}, f32[256,768]{1,0:T(8,128)}) custom-call(s32[3]{0:T(128)} %pad_add_fusion.ids, s32[3]{0:T(128)} %get-tuple-element.211.lens, bf16[256,768]{1,0:T(8,128)(2,1)} %get-tuple-element.148.x_ref, f32[4,768]{1,0:T(4,128)} %squeeze.26.small, ...), custom_call_target="tpu_custom_call" | custom-call | flops 1610612736 | bytes 12464152 | tf_op jit(solution)/shard_map/attend_forward_1/pallas_call | solution.py:469
  158.8 9.8 %feed_forward_1.1 = (bf16[256,3840]{1,0:T(8,128)(2,1)}, f32[256,3072]{1,0:T(8,128)}, bf16[256,768]{1,0:T(8,128)(2,1)}) custom-call(s32[3]{0:T(128)} %pad_add_fusion.ids, f32[256,768]{1,0:T(8,128)} %get-tuple-element.149.resid, f32[4,768]{1,0:T(4,128)} %squeeze.26.small, bf16[1,192,3072]{2,1,0:T(8,128)(2,1)} %refs_0_.14, bf16[1,192,3072]{2,1,0:T(8,128)(2,1)} %copy-done.6, ...), custom_call_target="tpu_custom_call" | custom-call | flops 2415919104 | bytes 18100236 | tf_op jit(solution)/shard_map/feed_forward_1/pallas_call | solution.py:469
  169.6 9.6 %feed_backward_1.1 = (bf16[256,1536]{1,0:T(8,128)(2,1)}, bf16[256,1536]{1,0:T(8,128)(2,1)}, f32[256,768]{1,0:T(8,128)}, f32[2,768]{1,0:T(2,128)}) custom-call(s32[3]{0:T(128)} %pad_add_fusion.ids, bf16[256,768]{1,0:T(8,128)(2,1)} %dynamic-slice_bitcast_fusion.d_out, f32[256,768]{1,0:T(8,128)} %get-tuple-element.149.resid, ...), custom_call_target="tpu_custom_call" | custom-call | flops 2415919104 | bytes 18499596 | tf_op jit(solution)/shard_map/feed_backward_1/pallas_call | solution.py:469
  182.0 5.8 %down_grad_1.1 = (bf16[4,2,192,384]{3,2,1,0:T(8,128)(2,1)}, bf16[4,2,192,384]{3,2,1,0:T(8,128)(2,1)}) custom-call(s32[3]{0:T(128)} %pad_add_fusion.ids, bf16[256,3840]{1,0:T(8,128)(2,1)} %get-tuple-element.159.active.normed, bf16[256,3840]{1,0:T(8,128)(2,1)} %copy-done.26, bf16[256,384]{1,0:T(8,128)(2,1)} %get-tuple-element.217.d, ...), custom_call_target="tpu_custom_call" | custom-call | flops 1207959552 | bytes 4194304 | tf_op jit(solution)/shard_map/down_grad_1/pallas_call | solution.py:542
  188.5 13.6 %attend_backward_1.1 = (bf16[256,1920]{1,0:T(8,128)(2,1)}, bf16[256,1920]{1,0:T(8,128)(2,1)}, bf16[256,768]{1,0:T(8,128)(2,1)}, f32[2,768]{1,0:T(2,128)}) custom-call(s32[3]{0:T(128)} %pad_add_fusion.ids, bf16[256,768]{1,0:T(8,128)(2,1)} %get-tuple-element.148.x_ref, f32[256,768]{1,0:T(8,128)} %get-tuple-element.155.d_resid, ...), custom_call_target="tpu_custom_call" | custom-call | flops 2214592512 | bytes 14043148 | tf_op jit(solution)/shard_map/attend_backward_1/pallas_call | solution.py:469
  202.2 5.4 %up_grad_1.1 = (bf16[2,4,4,48,384]{4,3,2,1,0:T(8,128)(2,1)}, bf16[2,4,4,48,384]{4,3,2,1,0:T(8,128)(2,1)}) custom-call(s32[3]{0:T(128)} %pad_add_fusion.ids, bf16[256,3840]{1,0:T(8,128)(2,1)} %get-tuple-element.159.active.normed, bf16[256,3840]{1,0:T(8,128)(2,1)} %copy-done.26, bf16[256,1536]{1,0:T(8,128)(2,1)} %get-tuple-element.170.d, ...), custom_call_target="tpu_custom_call" | custom-call | flops 1207959552 | bytes 4194304 | tf_op jit(solution)/shard_map/up_grad_1/pallas_call | solution.py:542
  210.0 6.3 %collective-permute-done.47 = bf16[4,2,4,48,384]{4,3,2,1,0:T(8,128)(2,1)} collective-permute-done((bf16[4,2,4,48,384]{4,3,2,1,0:T(8,128)(2,1)}, bf16[4,2,4,48,384]{4,3,2,1,0:T(8,128)(2,1)}, u32[]{:S(2)}, u32[]{:S(2)}) %collective-permute-start.47) | collective-permute-done | bytes 1179680 | tf_op jit(solution)/shard_map/ppermute | solution.py:677
  219.1 5.0 %collective-permute-done.51 = bf16[2,4,4,48,384]{4,3,2,1,0:T(8,128)(2,1)S(1)} collective-permute-done((bf16[2,4,4,48,384]{4,3,2,1,0:T(8,128)(2,1)}, bf16[2,4,4,48,384]{4,3,2,1,0:T(8,128)(2,1)S(1)}, u32[]{:S(2)}, u32[]{:S(2)}) %collective-permute-start.51) | collective-permute-done | bytes 1179680 | tf_op jit(solution)/shard_map/ppermute | solution.py:663
  226.9 9.6 %feed_backward_0.1 = (bf16[256,1536]{1,0:T(8,128)(2,1)}, bf16[256,1536]{1,0:T(8,128)(2,1)}, f32[256,768]{1,0:T(8,128)}, f32[2,768]{1,0:T(2,128)}) custom-call(s32[3]{0:T(128)} %pad_add_fusion.ids, bf16[256,768]{1,0:T(8,128)(2,1)} %get-tuple-element.162.d_out, f32[256,768]{1,0:T(8,128)} %get-tuple-element.142.resid, f32[256,3072]{1,0:T(8,128)} %get-tuple-element.163.slope, ...), custom_call_target="tpu_custom_call" | custom-call | flops 2415919104 | bytes 18499596 | tf_op jit(solution)/shard_map/feed_backward_0/pallas_call | solution.py:469
  236.7 5.7 %attend_grad_1.1 = (bf16[2,4,4,48,384]{4,3,2,1,0:T(8,128)(2,1)}, bf16[2,4,4,48,384]{4,3,2,1,0:T(8,128)(2,1)}) custom-call(s32[3]{0:T(128)} %pad_add_fusion.ids, bf16[256,1536]{1,0:T(8,128)(2,1)} %get-tuple-element.185.acts, bf16[256,1536]{1,0:T(8,128)(2,1)} %collective-permute-done.57.acts_too, bf16[256,1920]{1,0:T(8,128)(2,1)} %get-tuple-element.187.d, ...), custom_call_target="tpu_custom_call" | custom-call | flops 1207959552 | bytes 4194304 | tf_op jit(solution)/shard_map/attend_grad_1/pallas_call | solution.py:542
  249.5 6.3 %down_grad_0.1 = (bf16[2,4,192,384]{3,2,1,0:T(8,128)(2,1)}, bf16[2,4,192,384]{3,2,1,0:T(8,128)(2,1)}) custom-call(s32[3]{0:T(128)} %pad_add_fusion.ids, bf16[256,3840]{1,0:T(8,128)(2,1)} %get-tuple-element.166.active.normed, bf16[256,3840]{1,0:T(8,128)(2,1)} %collective-permute-done.48.active_too.normed_too, bf16[256,1920]{1,0:T(8,128)(2,1)} %get-tuple-element.187.d, ...), custom_call_target="tpu_custom_call" | custom-call | flops 1207959552 | bytes 4194304 | tf_op jit(solution)/shard_map/down_grad_0/pallas_call | solution.py:542
  258.4 13.5 %attend_backward_0.1 = (bf16[256,1920]{1,0:T(8,128)(2,1)}, bf16[256,1920]{1,0:T(8,128)(2,1)}, bf16[256,768]{1,0:T(8,128)(2,1)}, f32[2,768]{1,0:T(2,128)}) custom-call(s32[3]{0:T(128)} %pad_add_fusion.ids, bf16[256,768]{1,0:T(8,128)(2,1)} %dynamic-slice_bitcast_fusion.1.x_ref, f32[256,768]{1,0:T(8,128)} %get-tuple-element.176.d_resid, ...), custom_call_target="tpu_custom_call" | custom-call | flops 2214592512 | bytes 14043148 | tf_op jit(solution)/shard_map/attend_backward_0/pallas_call | solution.py:469
  281.7 5.1 %up_grad_0.1 = (bf16[2,4,4,48,384]{4,3,2,1,0:T(8,128)(2,1)}, bf16[2,4,4,48,384]{4,3,2,1,0:T(8,128)(2,1)}) custom-call(s32[3]{0:T(128)} %pad_add_fusion.ids, bf16[256,3840]{1,0:T(8,128)(2,1)} %get-tuple-element.166.active.normed, bf16[256,3840]{1,0:T(8,128)(2,1)} %collective-permute-done.48.active_too.normed_too, bf16[256,1536]{1,0:T(8,128)(2,1)} %get-tuple-element.192.d, ...), custom_call_target="tpu_custom_call" | custom-call | flops 1207959552 | bytes 4194304 | tf_op jit(solution)/shard_map/up_grad_0/pallas_call | solution.py:542
  296.7 5.8 %attend_grad_0.1 = (bf16[2,4,4,48,384]{4,3,2,1,0:T(8,128)(2,1)}, bf16[2,4,4,48,384]{4,3,2,1,0:T(8,128)(2,1)}) custom-call(s32[3]{0:T(128)} %pad_add_fusion.ids, bf16[256,1536]{1,0:T(8,128)(2,1)} %get-tuple-element.141.acts, bf16[256,1536]{1,0:T(8,128)(2,1)} %copy-done.50, bf16[256,1920]{1,0:T(8,128)(2,1)} %get-tuple-element.197.d, ...), custom_call_target="tpu_custom_call" | custom-call | flops 1207959552 | bytes 4194304 | tf_op jit(solution)/shard_map/attend_grad_0/pallas_call | solution.py:542
  328.7 5.6 %collective-permute-done.88 = bf16[1,12,48,384]{3,2,1,0:T(8,128)(2,1)S(1)} collective-permute-done((bf16[1,12,48,384]{3,2,1,0:T(8,128)(2,1)S(1)}, bf16[1,12,48,384]{3,2,1,0:T(8,128)(2,1)S(1)}, u32[]{:S(2)}, u32[]{:S(2)}) %collective-permute-start.88) | collective-permute-done | bytes 442400 | tf_op jit(solution)/shard_map/ppermute | solution.py:663
  339.3 7.0 %collective-permute-done.77 = bf16[1,1,4,48,384]{4,3,2,1,0:T(8,128)(2,1)S(1)} collective-permute-done((bf16[1,1,4,48,384]{4,3,2,1,0:T(8,128)(2,1)S(1)}, bf16[1,1,4,48,384]{4,3,2,1,0:T(8,128)(2,1)S(1)}, u32[]{:S(2)}, u32[]{:S(2)}) %collective-permute-start.77) | collective-permute-done | bytes 147488 | tf_op jit(solution)/shard_map/ppermute | solution.py:677
  380.7 4.5 %collective-permute-done.83 = bf16[2,4,48,384]{3,2,1,0:T(8,128)(2,1)} collective-permute-done((bf16[2,4,48,384]{3,2,1,0:T(8,128)(2,1)}, bf16[2,4,48,384]{3,2,1,0:T(8,128)(2,1)}, u32[]{:S(2)}, u32[]{:S(2)}) %collective-permute-start.83) | collective-permute-done | bytes 294944 | tf_op jit(solution)/shard_map/ppermute | solution.py:663
  (387 shorter events, 224.7 us)
Async XLA Ops:
  45.0 24.1 %collective-permute-start.23 = (bf16[2,3,4,48,384]{4,3,2,1,0:T(8,128)(2,1)S(1)}, bf16[2,3,4,48,384]{4,3,2,1,0:T(8,128)(2,1)S(1)}, u32[]{:S(2)}, u32[]{:S(2)}) collective-permute-start(bf16[2,3,4,48,384]{4,3,2,1,0:T(8,128)(2,1)S(1)} %pad_maximum_fusion.2.refs_4_), channel_id=1, source_target_pairs={{0,16},{16,0},{1,17},{17,1},{2,18},{18,2},{3,19},{19,3},{4,20},{20... | collective-permute-start | bytes 2654216 | tf_op jit(solution)/shard_map/ppermute | solution.py:650
  49.5 26.6 %collective-permute-start.24 = (bf16[1,768,768]{2,1,0:T(8,128)(2,1)S(1)}, bf16[1,768,768]{2,1,0:T(8,128)(2,1)S(1)}, u32[]{:S(2)}, u32[]{:S(2)}) collective-permute-start(bf16[1,768,768]{2,1,0:T(8,128)(2,1)S(1)} %copy-done.3), channel_id=1, source_target_pairs={{0,16},{16,0},{1,17},{17,1},{2,18},{18,2},{3,19},{19,3},{4,20},{20... | collective-permute-start | bytes 3538952 | tf_op jit(solution)/shard_map/ppermute | solution.py:650
  65.3 23.1 %collective-permute-start.16 = (bf16[2,3,4,48,384]{4,3,2,1,0:T(8,128)(2,1)}, bf16[2,3,4,48,384]{4,3,2,1,0:T(8,128)(2,1)}, u32[]{:S(2)}, u32[]{:S(2)}) collective-permute-start(bf16[2,3,4,48,384]{4,3,2,1,0:T(8,128)(2,1)} %pad_maximum_fusion.3.refs_2_), channel_id=1, source_target_pairs={{0,8},{4,12},{8,0},{12,4},{16,20},{20,16},{24,28},{28,24},{1,9},{5... | collective-permute-start | bytes 2654216 | tf_op jit(solution)/shard_map/ppermute | solution.py:663
  88.4 28.6 %collective-permute-start.36 = (bf16[2,3,4,48,384]{4,3,2,1,0:T(8,128)(2,1)S(1)}, bf16[2,3,4,48,384]{4,3,2,1,0:T(8,128)(2,1)}, u32[]{:S(2)}, u32[]{:S(2)}) collective-permute-start(bf16[2,3,4,48,384]{4,3,2,1,0:T(8,128)(2,1)S(1)} %pad_maximum_fusion.4), channel_id=1, source_target_pairs={{0,16},{16,0},{1,17},{17,1},{2,18},{18,2},{3,19},{19,3},{4,20},{20... | collective-permute-start | bytes 2654216 | tf_op jit(solution)/shard_map/ppermute | solution.py:650
  106.3 22.9 %collective-permute-start.29 = (bf16[2,3,4,48,384]{4,3,2,1,0:T(8,128)(2,1)S(1)}, bf16[2,3,4,48,384]{4,3,2,1,0:T(8,128)(2,1)S(1)}, u32[]{:S(2)}, u32[]{:S(2)}) collective-permute-start(bf16[2,3,4,48,384]{4,3,2,1,0:T(8,128)(2,1)S(1)} %pad_maximum_fusion.5.refs_4_), channel_id=1, source_target_pairs={{0,16},{16,0},{1,17},{17,1},{2,18},{18,2},{3,19},{19,3},{4,20},{20... | collective-permute-start | bytes 2654216 | tf_op jit(solution)/shard_map/ppermute | solution.py:650
  106.3 23.0 %collective-permute-start.26 = (bf16[2,3,4,48,384]{4,3,2,1,0:T(8,128)(2,1)}, bf16[2,3,4,48,384]{4,3,2,1,0:T(8,128)(2,1)S(1)}, u32[]{:S(2)}, u32[]{:S(2)}) collective-permute-start(bf16[2,3,4,48,384]{4,3,2,1,0:T(8,128)(2,1)} %collective-permute-done.25), channel_id=1, source_target_pairs={{0,16},{16,0},{1,17},{17,1},{2,18},{18,2},{3,19},{19,3},{4,20},{20... | collective-permute-start | bytes 2654216 | tf_op jit(solution)/shard_map/ppermute | solution.py:650
  133.4 24.5 %collective-permute-start.43 = (bf16[2,3,4,48,384]{4,3,2,1,0:T(8,128)(2,1)S(1)}, bf16[2,3,4,48,384]{4,3,2,1,0:T(8,128)(2,1)}, u32[]{:S(2)}, u32[]{:S(2)}) collective-permute-start(bf16[2,3,4,48,384]{4,3,2,1,0:T(8,128)(2,1)S(1)} %pad_maximum_fusion.7), channel_id=1, source_target_pairs={{0,16},{16,0},{1,17},{17,1},{2,18},{18,2},{3,19},{19,3},{4,20},{20... | collective-permute-start | bytes 2654216 | tf_op jit(solution)/shard_map/ppermute | solution.py:650
  179.3 22.9 %collective-permute-start.50 = (bf16[256,1536]{1,0:T(8,128)(2,1)}, bf16[256,1536]{1,0:T(8,128)(2,1)}, u32[]{:S(2)}, u32[]{:S(2)}) collective-permute-start(bf16[256,1536]{1,0:T(8,128)(2,1)} %get-tuple-element.171), channel_id=1, source_target_pairs={{0,16},{16,0},{1,17},{17,1},{2,18},{18,2},{3,19},{19,3},{4,20},{20... | collective-permute-start | bytes 2359304 | tf_op jit(solution)/shard_map/ppermute | solution.py:650
  187.8 28.4 %collective-permute-start.47 = (bf16[4,2,4,48,384]{4,3,2,1,0:T(8,128)(2,1)}, bf16[4,2,4,48,384]{4,3,2,1,0:T(8,128)(2,1)}, u32[]{:S(2)}, u32[]{:S(2)}) collective-permute-start(bf16[4,2,4,48,384]{4,3,2,1,0:T(8,128)(2,1)} %bitcast.107), channel_id=1, source_target_pairs={{0,1},{1,0},{2,3},{3,2},{4,5},{5,4},{6,7},{7,6},{8,9},{9,8},{10,11... | collective-permute-start | bytes 3538952 | tf_op jit(solution)/shard_map/ppermute | solution.py:677
  209.4 40.1 %collective-permute-start.48 = (bf16[256,3840]{1,0:T(8,128)(2,1)S(1)}, bf16[256,3840]{1,0:T(8,128)(2,1)}, u32[]{:S(2)}, u32[]{:S(2)}) collective-permute-start(bf16[256,3840]{1,0:T(8,128)(2,1)S(1)} %copy-done.14), channel_id=1, source_target_pairs={{0,16},{16,0},{1,17},{17,1},{2,18},{18,2},{3,19},{19,3},{4,20},{20... | collective-permute-start | bytes 5898248 | tf_op jit(solution)/shard_map/ppermute | solution.py:650
  209.4 27.3 %collective-permute-start.52 = (bf16[256,1920]{1,0:T(8,128)(2,1)}, bf16[256,1920]{1,0:T(8,128)(2,1)}, u32[]{:S(2)}, u32[]{:S(2)}) collective-permute-start(bf16[256,1920]{1,0:T(8,128)(2,1)} %get-tuple-element.169), channel_id=1, source_target_pairs={{0,16},{16,0},{1,17},{17,1},{2,18},{18,2},{3,19},{19,3},{4,20},{20... | collective-permute-start | bytes 2949128 | tf_op jit(solution)/shard_map/ppermute | solution.py:650
  209.9 26.7 %collective-permute-start.57 = (bf16[256,1536]{1,0:T(8,128)(2,1)}, bf16[256,1536]{1,0:T(8,128)(2,1)}, u32[]{:S(2)}, u32[]{:S(2)}) collective-permute-start(bf16[256,1536]{1,0:T(8,128)(2,1)} %get-tuple-element.185.acts), channel_id=1, source_target_pairs={{0,16},{16,0},{1,17},{17,1},{2,18},{18,2},{3,19},{19,3},{4,20},{20... | collective-permute-start | bytes 2359304 | tf_op jit(solution)/shard_map/ppermute | solution.py:650
  218.3 28.4 %collective-permute-start.49 = (bf16[4,1,4,48,384]{4,3,2,1,0:T(8,128)(2,1)}, bf16[4,1,4,48,384]{4,3,2,1,0:T(8,128)(2,1)}, u32[]{:S(2)}, u32[]{:S(2)}) collective-permute-start(bf16[4,1,4,48,384]{4,3,2,1,0:T(8,128)(2,1)} %add_convert_fusion.4), channel_id=1, source_target_pairs={{0,2},{1,3},{2,0},{3,1},{4,6},{5,7},{6,4},{7,5},{8,10},{9,11},{10,... | collective-permute-start | bytes 1769480 | tf_op jit(solution)/shard_map/ppermute | solution.py:677
  225.3 31.7 %collective-permute-start.54 = (bf16[1,4,4,48,384]{4,3,2,1,0:T(8,128)(2,1)}, bf16[1,4,4,48,384]{4,3,2,1,0:T(8,128)(2,1)}, u32[]{:S(2)}, u32[]{:S(2)}) collective-permute-start(bf16[1,4,4,48,384]{4,3,2,1,0:T(8,128)(2,1)} %add_convert_fusion.3), channel_id=1, source_target_pairs={{0,8},{4,12},{8,0},{12,4},{16,20},{20,16},{24,28},{28,24},{1,9},{5... | collective-permute-start | bytes 1769480 | tf_op jit(solution)/shard_map/ppermute | solution.py:663
  236.6 45.0 %collective-permute-start.64 = (bf16[256,1536]{1,0:T(8,128)(2,1)}, bf16[256,1536]{1,0:T(8,128)(2,1)}, u32[]{:S(2)}, u32[]{:S(2)}) collective-permute-start(bf16[256,1536]{1,0:T(8,128)(2,1)} %get-tuple-element.186), channel_id=1, source_target_pairs={{0,16},{16,0},{1,17},{17,1},{2,18},{18,2},{3,19},{19,3},{4,20},{20... | collective-permute-start | bytes 2359304 | tf_op jit(solution)/shard_map/ppermute | solution.py:650
  242.4 36.0 %collective-permute-start.58 = (bf16[2,4,4,48,384]{4,3,2,1,0:T(8,128)(2,1)}, bf16[2,4,4,48,384]{4,3,2,1,0:T(8,128)(2,1)}, u32[]{:S(2)}, u32[]{:S(2)}) collective-permute-start(bf16[2,4,4,48,384]{4,3,2,1,0:T(8,128)(2,1)} %get-tuple-element.189), channel_id=1, source_target_pairs={{0,4},{4,0},{8,12},{12,8},{16,24},{20,28},{24,16},{28,20},{1,5},{5... | collective-permute-start | bytes 3538952 | tf_op jit(solution)/shard_map/ppermute | solution.py:663
  248.6 25.4 %collective-permute-start.63 = (bf16[2,1,4,48,384]{4,3,2,1,0:T(8,128)(2,1)}, bf16[2,1,4,48,384]{4,3,2,1,0:T(8,128)(2,1)S(1)}, u32[]{:S(2)}, u32[]{:S(2)}) collective-permute-start(bf16[2,1,4,48,384]{4,3,2,1,0:T(8,128)(2,1)} %add_convert_fusion.10), channel_id=1, source_target_pairs={{0,4},{4,0},{8,12},{12,8},{16,24},{20,28},{24,16},{28,20},{1,5},{5... | collective-permute-start | bytes 884744 | tf_op jit(solution)/shard_map/ppermute | solution.py:663
  255.9 39.5 %collective-permute-start.61 = (bf16[2,4,4,48,384]{4,3,2,1,0:T(8,128)(2,1)}, bf16[2,4,4,48,384]{4,3,2,1,0:T(8,128)(2,1)}, u32[]{:S(2)}, u32[]{:S(2)}) collective-permute-start(bf16[2,4,4,48,384]{4,3,2,1,0:T(8,128)(2,1)} %bitcast.106), channel_id=1, source_target_pairs={{0,4},{4,0},{8,12},{12,8},{16,24},{20,28},{24,16},{28,20},{1,5},{5... | collective-permute-start | bytes 3538952 | tf_op jit(solution)/shard_map/ppermute | solution.py:663
  272.7 24.0 %collective-permute-start.70 = (bf16[256,1920]{1,0:T(8,128)(2,1)}, bf16[256,1920]{1,0:T(8,128)(2,1)}, u32[]{:S(2)}, u32[]{:S(2)}) collective-permute-start(bf16[256,1920]{1,0:T(8,128)(2,1)} %get-tuple-element.198), channel_id=1, source_target_pairs={{0,16},{16,0},{1,17},{17,1},{2,18},{18,2},{3,19},{19,3},{4,20},{20... | collective-permute-start | bytes 2949128 | tf_op jit(solution)/shard_map/ppermute | solution.py:650
  286.9 22.9 %collective-permute-start.65 = (bf16[2,4,4,48,384]{4,3,2,1,0:T(8,128)(2,1)}, bf16[2,4,4,48,384]{4,3,2,1,0:T(8,128)(2,1)}, u32[]{:S(2)}, u32[]{:S(2)}) collective-permute-start(bf16[2,4,4,48,384]{4,3,2,1,0:T(8,128)(2,1)} %get-tuple-element.193), channel_id=1, source_target_pairs={{0,4},{4,0},{8,12},{12,8},{16,24},{20,28},{24,16},{28,20},{1,5},{5... | collective-permute-start | bytes 3538952 | tf_op jit(solution)/shard_map/ppermute | solution.py:663
  302.5 36.1 %collective-permute-start.71 = (bf16[2,4,4,48,384]{4,3,2,1,0:T(8,128)(2,1)}, bf16[2,4,4,48,384]{4,3,2,1,0:T(8,128)(2,1)S(1)}, u32[]{:S(2)}, u32[]{:S(2)}) collective-permute-start(bf16[2,4,4,48,384]{4,3,2,1,0:T(8,128)(2,1)} %get-tuple-element.199), channel_id=1, source_target_pairs={{0,4},{4,0},{8,12},{12,8},{16,24},{20,28},{24,16},{28,20},{1,5},{5... | collective-permute-start | bytes 3538952 | tf_op jit(solution)/shard_map/ppermute | solution.py:663
  317.4 30.4 %collective-permute-start.66 = (f32[2,4,768]{2,1,0:T(4,128)S(1)}, f32[2,4,768]{2,1,0:T(4,128)S(1)}, u32[]{:S(2)}, u32[]{:S(2)}) collective-permute-start(f32[2,4,768]{2,1,0:T(4,128)S(1)} %pad_maximum_fusion.22), channel_id=1, source_target_pairs={{0,16},{16,0},{1,17},{17,1},{2,18},{18,2},{3,19},{19,3},{4,20},{20... | collective-permute-start | bytes 73736 | tf_op jit(solution)/shard_map/ppermute | solution.py:650
  334.4 23.3 %collective-permute-start.89 = (bf16[2,12,48,384]{3,2,1,0:T(8,128)(2,1)S(1)}, bf16[2,12,48,384]{3,2,1,0:T(8,128)(2,1)S(1)}, u32[]{:S(2)}, u32[]{:S(2)}) collective-permute-start(bf16[2,12,48,384]{3,2,1,0:T(8,128)(2,1)S(1)} %pad_maximum_fusion.8), channel_id=1, source_target_pairs={{0,4},{4,0},{8,12},{12,8},{16,24},{20,28},{24,16},{28,20},{1,5},{5... | collective-permute-start | bytes 2654216 | tf_op jit(solution)/shard_map/ppermute | solution.py:663
  358.0 28.3 %collective-permute-start.90 = (bf16[4,12,48,384]{3,2,1,0:T(8,128)(2,1)S(1)}, bf16[4,12,48,384]{3,2,1,0:T(8,128)(2,1)}, u32[]{:S(2)}, u32[]{:S(2)}) collective-permute-start(bf16[4,12,48,384]{3,2,1,0:T(8,128)(2,1)S(1)} %pad_maximum_fusion.high_own), channel_id=1, source_target_pairs={{0,16},{1,17},{2,18},{3,19},{4,20},{5,21},{6,22},{7,23},{8,24},{9,... | collective-permute-start | bytes 5308424 | tf_op jit(solution)/shard_map/ppermute | solution.py:1034
  (119 other events, 1319.4 us)

commit v4 on v3

--- a/solution.py
+++ b/solution.py
@@ -418,10 +418,13 @@
     width, tall = plan.width, plan.tall
     group = ids[1]
     first = ids[0] == 0
-    tables = masks_of(plan.groups, False)
-    for h, (a, b) in enumerate(((low_own, high_got), (low_got, high_own))):
-        for j in range(plan.groups):
-            peer = group ^ tables[h][j]
+    orders = masks_of(plan.groups, False)
+
+    def place(j, carry):
+        for h, (a, b) in enumerate(((low_own, high_got), (low_got, high_own))):
+            peer = group
+            for t in range(plan.groups.bit_length() - 1):
+                peer = peer ^ (((j >> t) & 1) * orders[h][1 << t])
             for p in range(PARTS):
                 value = jnp.where(first, a[j, p], b[j, p]).astype(jnp.float32)
                 if kind == "down":
@@ -433,6 +436,9 @@
                 c = 0 if kind == "attend" and p == PARTS - 1 else p
                 lanes = slice(c * width + h * BLOCK, c * width + (h + 1) * BLOCK)
                 out[0, pl.ds(at, tall), lanes] = value
+        return carry
+
+    lax.fori_loop(0, plan.groups, place, 0)
 
 
 SHARDS = {"attend": 2, "up": 1, "down": 1}
@@ -450,7 +456,7 @@
 
 
 DEPTH = 2
-DEPTH_BACK = 9
+DEPTH_BACK = 3
 EARLY = "down"
 LATE = 2
 GATHERS = {"upper": (1, ("down", "up", "attend")), "feed": (0, ("down", "up")), "attend": (0, ("attend",))}

time: 415 us -> 415 us (level)
  no operation moved by 1% of the time
where the time goes in v4:
time: 415 us; the launch traced here: 408 us
  Pallas kernels  135 us (33%)
  waiting for transfers between devices  119 us (29%)
  starting transfers between devices  93.1 us (22%)
  other arithmetic  45.9 us (11%)
  local copies, waits for them, and re-layouts  13.1 us (3%)
    pallas_call x8, Pallas kernels, call(): pl.pallas_call(body, out_shape=outs, in_specs=specs, out_specs=out_specs,...  85.9 us
    ppermute x28, waiting for transfers between devices, swap_rows(): return lax.ppermute(x, 'dp', [(i, i ^ bit) for i in range(rows)])  69.7 us
    ppermute x32, waiting for transfers between devices, swap_groups(): return lax.ppermute(x, ('section', 'group'), pairs)  48.7 us
    ppermute x32, starting transfers between devices, swap_groups(): return lax.ppermute(x, ('section', 'group'), pairs)  44.7 us
    ppermute x28, starting transfers between devices, swap_rows(): return lax.ppermute(x, 'dp', [(i, i ^ bit) for i in range(rows)])  35.4 us
    pallas_call x6, Pallas kernels, weight_grad(): pl.pallas_call(body, out_shape=outs, grid_spec=pltpu.PrefetchScalarGridSp...  34.1 us
    convert_element_type x24, other arithmetic, total_of(): return total.astype(BF)  25.9 us
    pallas_call x3, Pallas kernels, final(): pl.pallas_call(functools.partial(final_layout, p, kind), out_shape=outs,...  11.7 us
  transfers between devices with their start and end apart: 92, of which 33 were waited for; matrix products, arithmetic and copies ran while one was open for 13% of the time, Pallas kernels for 29%

profile of v4, /device:TPU:0, one launch (start us, length us, event | category | flops | bytes accessed | tf_op | source)
XLA Modules:
  0.0 408.0 jit_solution(8827715847875187506)
XLA Ops:
  12.3 7.4 %collective-permute-done.1 = bf16[1,1,4,48,384]{4,3,2,1,0:T(8,128)(2,1)S(1)} collective-permute-done((bf16[1,1,4,48,384]{4,3,2,1,0:T(8,128)(2,1)S(1)}, bf16[1,1,4,48,384]{4,3,2,1,0:T(8,128)(2,1)S(1)}, u32[]{:S(2)}, u32[]{:S(2)}) %collective-permute-start.1) | collective-permute-done | bytes 147488 | tf_op jit(solution)/shard_map/ppermute | solution.py:683
  25.9 6.6 %collective-permute-done.5 = bf16[1,1,4,48,384]{4,3,2,1,0:T(8,128)(2,1)S(1)} collective-permute-done((bf16[1,1,4,48,384]{4,3,2,1,0:T(8,128)(2,1)S(1)}, bf16[1,1,4,48,384]{4,3,2,1,0:T(8,128)(2,1)S(1)}, u32[]{:S(2)}, u32[]{:S(2)}) %collective-permute-start.5) | collective-permute-done | bytes 147488 | tf_op jit(solution)/shard_map/ppermute | solution.py:683
  52.9 7.0 %collective-permute-done.18 = bf16[1,2,4,48,384]{4,3,2,1,0:T(8,128)(2,1)S(1)} collective-permute-done((bf16[1,2,4,48,384]{4,3,2,1,0:T(8,128)(2,1)S(1)}, bf16[1,2,4,48,384]{4,3,2,1,0:T(8,128)(2,1)S(1)}, u32[]{:S(2)}, u32[]{:S(2)}) %collective-permute-start.18) | collective-permute-done | bytes 294944 | tf_op jit(solution)/shard_map/ppermute | solution.py:683
  91.5 6.5 %collective-permute-done.30 = bf16[1,2,4,48,384]{4,3,2,1,0:T(8,128)(2,1)S(1)} collective-permute-done((bf16[1,2,4,48,384]{4,3,2,1,0:T(8,128)(2,1)S(1)}, bf16[1,2,4,48,384]{4,3,2,1,0:T(8,128)(2,1)S(1)}, u32[]{:S(2)}, u32[]{:S(2)}) %collective-permute-start.30) | collective-permute-done | bytes 294944 | tf_op jit(solution)/shard_map/ppermute | solution.py:683
  106.8 10.1 %attend_forward_0.1 = (bf16[256,2304]{1,0:T(8,128)(2,1)}, f32[12,256,256]{2,1,0:T(8,128)}, bf16[256,1536]{1,0:T(8,128)(2,1)}, f32[256,768]{1,0:T(8,128)}) custom-call(s32[3]{0:T(128)} %pad_add_fusion.ids, s32[3]{0:T(128)} %get-tuple-element.243.lens, bf16[256,768]{1,0:T(8,128)(2,1)} %dynamic-slice_bitcast_fusion.1.x_ref, f32[4,768]{1,0:T(4,128)} %squeeze.25.small, ...), custom_call_target="tpu_custom_call" | custom-call | flops 1610612736 | bytes 12464152 | tf_op jit(solution)/shard_map/attend_forward_0/pallas_call | solution.py:475
  122.0 5.2 %collective-permute-done.40 = bf16[1,3,4,48,384]{4,3,2,1,0:T(8,128)(2,1)S(1)} collective-permute-done((bf16[1,3,4,48,384]{4,3,2,1,0:T(8,128)(2,1)S(1)}, bf16[1,3,4,48,384]{4,3,2,1,0:T(8,128)(2,1)S(1)}, u32[]{:S(2)}, u32[]{:S(2)}) %collective-permute-start.40) | collective-permute-done | bytes 442400 | tf_op jit(solution)/shard_map/ppermute | solution.py:669
  136.0 9.7 %feed_forward_0.1 = (bf16[256,3840]{1,0:T(8,128)(2,1)}, f32[256,3072]{1,0:T(8,128)}, bf16[256,768]{1,0:T(8,128)(2,1)}) custom-call(s32[3]{0:T(128)} %pad_add_fusion.ids, f32[256,768]{1,0:T(8,128)} %get-tuple-element.158.resid, f32[4,768]{1,0:T(4,128)} %squeeze.25.small, bf16[1,192,3072]{2,1,0:T(8,128)(2,1)} %refs_0_.14, bf16[1,192,3072]{2,1,0:T(8,128)(2,1)} %copy-done.6, ...), custom_call_target="tpu_custom_call" | custom-call | flops 2415919104 | bytes 18100236 | tf_op jit(solution)/shard_map/feed_forward_0/pallas_call | solution.py:475
  147.8 10.0 %attend_forward_1.1 = (bf16[256,2304]{1,0:T(8,128)(2,1)}, f32[12,256,256]{2,1,0:T(8,128)}, bf16[256,1536]{1,0:T(8,128)(2,1)}, f32[256,768]{1,0:T(8,128)}) custom-call(s32[3]{0:T(128)} %pad_add_fusion.ids, s32[3]{0:T(128)} %get-tuple-element.243.lens, bf16[256,768]{1,0:T(8,128)(2,1)} %get-tuple-element.164.x_ref, f32[4,768]{1,0:T(4,128)} %squeeze.26.small, ...), custom_call_target="tpu_custom_call" | custom-call | flops 1610612736 | bytes 12464152 | tf_op jit(solution)/shard_map/attend_forward_1/pallas_call | solution.py:475
  158.8 9.8 %feed_forward_1.1 = (bf16[256,3840]{1,0:T(8,128)(2,1)}, f32[256,3072]{1,0:T(8,128)}, bf16[256,768]{1,0:T(8,128)(2,1)}) custom-call(s32[3]{0:T(128)} %pad_add_fusion.ids, f32[256,768]{1,0:T(8,128)} %get-tuple-element.165.resid, f32[4,768]{1,0:T(4,128)} %squeeze.26.small, bf16[1,192,3072]{2,1,0:T(8,128)(2,1)} %refs_0_.14, bf16[1,192,3072]{2,1,0:T(8,128)(2,1)} %copy-done.6, ...), custom_call_target="tpu_custom_call" | custom-call | flops 2415919104 | bytes 18100236 | tf_op jit(solution)/shard_map/feed_forward_1/pallas_call | solution.py:475
  169.6 9.6 %feed_backward_1.1 = (bf16[256,1536]{1,0:T(8,128)(2,1)}, bf16[256,1536]{1,0:T(8,128)(2,1)}, f32[256,768]{1,0:T(8,128)}, f32[2,768]{1,0:T(2,128)}) custom-call(s32[3]{0:T(128)} %pad_add_fusion.ids, bf16[256,768]{1,0:T(8,128)(2,1)} %dynamic-slice_bitcast_fusion.d_out, f32[256,768]{1,0:T(8,128)} %get-tuple-element.165.resid, ...), custom_call_target="tpu_custom_call" | custom-call | flops 2415919104 | bytes 18499596 | tf_op jit(solution)/shard_map/feed_backward_1/pallas_call | solution.py:475
  182.0 5.8 %down_grad_1.1 = (bf16[4,2,192,384]{3,2,1,0:T(8,128)(2,1)}, bf16[4,2,192,384]{3,2,1,0:T(8,128)(2,1)}) custom-call(s32[3]{0:T(128)} %pad_add_fusion.ids, bf16[256,3840]{1,0:T(8,128)(2,1)} %get-tuple-element.175.active.normed, bf16[256,3840]{1,0:T(8,128)(2,1)} %copy-done.26, bf16[256,384]{1,0:T(8,128)(2,1)} %get-tuple-element.249.d, ...), custom_call_target="tpu_custom_call" | custom-call | flops 1207959552 | bytes 4194304 | tf_op jit(solution)/shard_map/down_grad_1/pallas_call | solution.py:548
  188.5 13.6 %attend_backward_1.1 = (bf16[256,1920]{1,0:T(8,128)(2,1)}, bf16[256,1920]{1,0:T(8,128)(2,1)}, bf16[256,768]{1,0:T(8,128)(2,1)}, f32[2,768]{1,0:T(2,128)}) custom-call(s32[3]{0:T(128)} %pad_add_fusion.ids, bf16[256,768]{1,0:T(8,128)(2,1)} %get-tuple-element.164.x_ref, f32[256,768]{1,0:T(8,128)} %get-tuple-element.171.d_resid, ...), custom_call_target="tpu_custom_call" | custom-call | flops 2214592512 | bytes 14043148 | tf_op jit(solution)/shard_map/attend_backward_1/pallas_call | solution.py:475
  202.2 5.4 %up_grad_1.1 = (bf16[2,4,4,48,384]{4,3,2,1,0:T(8,128)(2,1)}, bf16[2,4,4,48,384]{4,3,2,1,0:T(8,128)(2,1)}) custom-call(s32[3]{0:T(128)} %pad_add_fusion.ids, bf16[256,3840]{1,0:T(8,128)(2,1)} %get-tuple-element.175.active.normed, bf16[256,3840]{1,0:T(8,128)(2,1)} %copy-done.26, bf16[256,1536]{1,0:T(8,128)(2,1)} %get-tuple-element.186.d, ...), custom_call_target="tpu_custom_call" | custom-call | flops 1207959552 | bytes 4194304 | tf_op jit(solution)/shard_map/up_grad_1/pallas_call | solution.py:548
  210.0 6.3 %collective-permute-done.47 = bf16[4,2,4,48,384]{4,3,2,1,0:T(8,128)(2,1)} collective-permute-done((bf16[4,2,4,48,384]{4,3,2,1,0:T(8,128)(2,1)}, bf16[4,2,4,48,384]{4,3,2,1,0:T(8,128)(2,1)}, u32[]{:S(2)}, u32[]{:S(2)}) %collective-permute-start.47) | collective-permute-done | bytes 1179680 | tf_op jit(solution)/shard_map/ppermute | solution.py:683
  219.1 5.0 %collective-permute-done.51 = bf16[2,4,4,48,384]{4,3,2,1,0:T(8,128)(2,1)S(1)} collective-permute-done((bf16[2,4,4,48,384]{4,3,2,1,0:T(8,128)(2,1)}, bf16[2,4,4,48,384]{4,3,2,1,0:T(8,128)(2,1)S(1)}, u32[]{:S(2)}, u32[]{:S(2)}) %collective-permute-start.51) | collective-permute-done | bytes 1179680 | tf_op jit(solution)/shard_map/ppermute | solution.py:669
  226.9 9.6 %feed_backward_0.1 = (bf16[256,1536]{1,0:T(8,128)(2,1)}, bf16[256,1536]{1,0:T(8,128)(2,1)}, f32[256,768]{1,0:T(8,128)}, f32[2,768]{1,0:T(2,128)}) custom-call(s32[3]{0:T(128)} %pad_add_fusion.ids, bf16[256,768]{1,0:T(8,128)(2,1)} %get-tuple-element.178.d_out, f32[256,768]{1,0:T(8,128)} %get-tuple-element.158.resid, f32[256,3072]{1,0:T(8,128)} %get-tuple-element.179.slope, ...), custom_call_target="tpu_custom_call" | custom-call | flops 2415919104 | bytes 18499596 | tf_op jit(solution)/shard_map/feed_backward_0/pallas_call | solution.py:475
  236.7 5.7 %attend_grad_1.1 = (bf16[2,4,4,48,384]{4,3,2,1,0:T(8,128)(2,1)}, bf16[2,4,4,48,384]{4,3,2,1,0:T(8,128)(2,1)}) custom-call(s32[3]{0:T(128)} %pad_add_fusion.ids, bf16[256,1536]{1,0:T(8,128)(2,1)} %get-tuple-element.203.acts, bf16[256,1536]{1,0:T(8,128)(2,1)} %collective-permute-done.57.acts_too, bf16[256,1920]{1,0:T(8,128)(2,1)} %get-tuple-element.205.d, ...), custom_call_target="tpu_custom_call" | custom-call | flops 1207959552 | bytes 4194304 | tf_op jit(solution)/shard_map/attend_grad_1/pallas_call | solution.py:548
  249.5 6.3 %down_grad_0.1 = (bf16[2,4,192,384]{3,2,1,0:T(8,128)(2,1)}, bf16[2,4,192,384]{3,2,1,0:T(8,128)(2,1)}) custom-call(s32[3]{0:T(128)} %pad_add_fusion.ids, bf16[256,3840]{1,0:T(8,128)(2,1)} %get-tuple-element.182.active.normed, bf16[256,3840]{1,0:T(8,128)(2,1)} %collective-permute-done.48.active_too.normed_too, bf16[256,1920]{1,0:T(8,128)(2,1)} %get-tuple-element.205.d, ...), custom_call_target="tpu_custom_call" | custom-call | flops 1207959552 | bytes 4194304 | tf_op jit(solution)/shard_map/down_grad_0/pallas_call | solution.py:548
  258.6 13.4 %attend_backward_0.1 = (bf16[256,1920]{1,0:T(8,128)(2,1)}, bf16[256,1920]{1,0:T(8,128)(2,1)}, bf16[256,768]{1,0:T(8,128)(2,1)}, f32[2,768]{1,0:T(2,128)}) custom-call(s32[3]{0:T(128)} %pad_add_fusion.ids, bf16[256,768]{1,0:T(8,128)(2,1)} %dynamic-slice_bitcast_fusion.1.x_ref, f32[256,768]{1,0:T(8,128)} %get-tuple-element.192.d_resid, ...), custom_call_target="tpu_custom_call" | custom-call | flops 2214592512 | bytes 14043148 | tf_op jit(solution)/shard_map/attend_backward_0/pallas_call | solution.py:475
  281.7 5.1 %up_grad_0.1 = (bf16[2,4,4,48,384]{4,3,2,1,0:T(8,128)(2,1)}, bf16[2,4,4,48,384]{4,3,2,1,0:T(8,128)(2,1)}) custom-call(s32[3]{0:T(128)} %pad_add_fusion.ids, bf16[256,3840]{1,0:T(8,128)(2,1)} %get-tuple-element.182.active.normed, bf16[256,3840]{1,0:T(8,128)(2,1)} %collective-permute-done.48.active_too.normed_too, bf16[256,1536]{1,0:T(8,128)(2,1)} %get-tuple-element.215.d, ...), custom_call_target="tpu_custom_call" | custom-call | flops 1207959552 | bytes 4194304 | tf_op jit(solution)/shard_map/up_grad_0/pallas_call | solution.py:548
  296.7 5.8 %attend_grad_0.1 = (bf16[2,4,4,48,384]{4,3,2,1,0:T(8,128)(2,1)}, bf16[2,4,4,48,384]{4,3,2,1,0:T(8,128)(2,1)}) custom-call(s32[3]{0:T(128)} %pad_add_fusion.ids, bf16[256,1536]{1,0:T(8,128)(2,1)} %get-tuple-element.157.acts, bf16[256,1536]{1,0:T(8,128)(2,1)} %copy-done.50, bf16[256,1920]{1,0:T(8,128)(2,1)} %get-tuple-element.224.d, ...), custom_call_target="tpu_custom_call" | custom-call | flops 1207959552 | bytes 4194304 | tf_op jit(solution)/shard_map/attend_grad_0/pallas_call | solution.py:548
  328.6 5.6 %collective-permute-done.88 = bf16[1,12,48,384]{3,2,1,0:T(8,128)(2,1)S(1)} collective-permute-done((bf16[1,12,48,384]{3,2,1,0:T(8,128)(2,1)S(1)}, bf16[1,12,48,384]{3,2,1,0:T(8,128)(2,1)S(1)}, u32[]{:S(2)}, u32[]{:S(2)}) %collective-permute-start.88) | collective-permute-done | bytes 442400 | tf_op jit(solution)/shard_map/ppermute | solution.py:669
  339.3 7.2 %collective-permute-done.78 = bf16[1,1,4,48,384]{4,3,2,1,0:T(8,128)(2,1)S(1)} collective-permute-done((bf16[1,1,4,48,384]{4,3,2,1,0:T(8,128)(2,1)S(1)}, bf16[1,1,4,48,384]{4,3,2,1,0:T(8,128)(2,1)S(1)}, u32[]{:S(2)}, u32[]{:S(2)}) %collective-permute-start.78) | collective-permute-done | bytes 147488 | tf_op jit(solution)/shard_map/ppermute | solution.py:683
  380.8 4.5 %collective-permute-done.84 = bf16[2,4,48,384]{3,2,1,0:T(8,128)(2,1)} collective-permute-done((bf16[2,4,48,384]{3,2,1,0:T(8,128)(2,1)}, bf16[2,4,48,384]{3,2,1,0:T(8,128)(2,1)}, u32[]{:S(2)}, u32[]{:S(2)}) %collective-permute-start.84) | collective-permute-done | bytes 294944 | tf_op jit(solution)/shard_map/ppermute | solution.py:669
  (387 shorter events, 224.7 us)
Async XLA Ops:
  45.0 24.1 %collective-permute-start.23 = (bf16[2,3,4,48,384]{4,3,2,1,0:T(8,128)(2,1)S(1)}, bf16[2,3,4,48,384]{4,3,2,1,0:T(8,128)(2,1)S(1)}, u32[]{:S(2)}, u32[]{:S(2)}) collective-permute-start(bf16[2,3,4,48,384]{4,3,2,1,0:T(8,128)(2,1)S(1)} %pad_maximum_fusion.2.refs_4_), channel_id=1, source_target_pairs={{0,16},{16,0},{1,17},{17,1},{2,18},{18,2},{3,19},{19,3},{4,20},{20... | collective-permute-start | bytes 2654216 | tf_op jit(solution)/shard_map/ppermute | solution.py:656
  49.5 26.6 %collective-permute-start.24 = (bf16[1,768,768]{2,1,0:T(8,128)(2,1)S(1)}, bf16[1,768,768]{2,1,0:T(8,128)(2,1)S(1)}, u32[]{:S(2)}, u32[]{:S(2)}) collective-permute-start(bf16[1,768,768]{2,1,0:T(8,128)(2,1)S(1)} %copy-done.3), channel_id=1, source_target_pairs={{0,16},{16,0},{1,17},{17,1},{2,18},{18,2},{3,19},{19,3},{4,20},{20... | collective-permute-start | bytes 3538952 | tf_op jit(solution)/shard_map/ppermute | solution.py:656
  65.3 23.1 %collective-permute-start.16 = (bf16[2,3,4,48,384]{4,3,2,1,0:T(8,128)(2,1)}, bf16[2,3,4,48,384]{4,3,2,1,0:T(8,128)(2,1)}, u32[]{:S(2)}, u32[]{:S(2)}) collective-permute-start(bf16[2,3,4,48,384]{4,3,2,1,0:T(8,128)(2,1)} %pad_maximum_fusion.3.refs_2_), channel_id=1, source_target_pairs={{0,8},{4,12},{8,0},{12,4},{16,20},{20,16},{24,28},{28,24},{1,9},{5... | collective-permute-start | bytes 2654216 | tf_op jit(solution)/shard_map/ppermute | solution.py:669
  88.4 28.6 %collective-permute-start.36 = (bf16[2,3,4,48,384]{4,3,2,1,0:T(8,128)(2,1)S(1)}, bf16[2,3,4,48,384]{4,3,2,1,0:T(8,128)(2,1)}, u32[]{:S(2)}, u32[]{:S(2)}) collective-permute-start(bf16[2,3,4,48,384]{4,3,2,1,0:T(8,128)(2,1)S(1)} %pad_maximum_fusion.4), channel_id=1, source_target_pairs={{0,16},{16,0},{1,17},{17,1},{2,18},{18,2},{3,19},{19,3},{4,20},{20... | collective-permute-start | bytes 2654216 | tf_op jit(solution)/shard_map/ppermute | solution.py:656
  106.3 22.9 %collective-permute-start.29 = (bf16[2,3,4,48,384]{4,3,2,1,0:T(8,128)(2,1)S(1)}, bf16[2,3,4,48,384]{4,3,2,1,0:T(8,128)(2,1)S(1)}, u32[]{:S(2)}, u32[]{:S(2)}) collective-permute-start(bf16[2,3,4,48,384]{4,3,2,1,0:T(8,128)(2,1)S(1)} %pad_maximum_fusion.5.refs_4_), channel_id=1, source_target_pairs={{0,16},{16,0},{1,17},{17,1},{2,18},{18,2},{3,19},{19,3},{4,20},{20... | collective-permute-start | bytes 2654216 | tf_op jit(solution)/shard_map/ppermute | solution.py:656
  106.3 23.0 %collective-permute-start.26 = (bf16[2,3,4,48,384]{4,3,2,1,0:T(8,128)(2,1)}, bf16[2,3,4,48,384]{4,3,2,1,0:T(8,128)(2,1)S(1)}, u32[]{:S(2)}, u32[]{:S(2)}) collective-permute-start(bf16[2,3,4,48,384]{4,3,2,1,0:T(8,128)(2,1)} %collective-permute-done.25), channel_id=1, source_target_pairs={{0,16},{16,0},{1,17},{17,1},{2,18},{18,2},{3,19},{19,3},{4,20},{20... | collective-permute-start | bytes 2654216 | tf_op jit(solution)/shard_map/ppermute | solution.py:656
  133.4 24.5 %collective-permute-start.43 = (bf16[2,3,4,48,384]{4,3,2,1,0:T(8,128)(2,1)S(1)}, bf16[2,3,4,48,384]{4,3,2,1,0:T(8,128)(2,1)}, u32[]{:S(2)}, u32[]{:S(2)}) collective-permute-start(bf16[2,3,4,48,384]{4,3,2,1,0:T(8,128)(2,1)S(1)} %pad_maximum_fusion.7), channel_id=1, source_target_pairs={{0,16},{16,0},{1,17},{17,1},{2,18},{18,2},{3,19},{19,3},{4,20},{20... | collective-permute-start | bytes 2654216 | tf_op jit(solution)/shard_map/ppermute | solution.py:656
  179.3 22.9 %collective-permute-start.50 = (bf16[256,1536]{1,0:T(8,128)(2,1)}, bf16[256,1536]{1,0:T(8,128)(2,1)}, u32[]{:S(2)}, u32[]{:S(2)}) collective-permute-start(bf16[256,1536]{1,0:T(8,128)(2,1)} %get-tuple-element.187), channel_id=1, source_target_pairs={{0,16},{16,0},{1,17},{17,1},{2,18},{18,2},{3,19},{19,3},{4,20},{20... | collective-permute-start | bytes 2359304 | tf_op jit(solution)/shard_map/ppermute | solution.py:656
  187.8 28.4 %collective-permute-start.47 = (bf16[4,2,4,48,384]{4,3,2,1,0:T(8,128)(2,1)}, bf16[4,2,4,48,384]{4,3,2,1,0:T(8,128)(2,1)}, u32[]{:S(2)}, u32[]{:S(2)}) collective-permute-start(bf16[4,2,4,48,384]{4,3,2,1,0:T(8,128)(2,1)} %bitcast.106), channel_id=1, source_target_pairs={{0,1},{1,0},{2,3},{3,2},{4,5},{5,4},{6,7},{7,6},{8,9},{9,8},{10,11... | collective-permute-start | bytes 3538952 | tf_op jit(solution)/shard_map/ppermute | solution.py:683
  209.4 40.1 %collective-permute-start.48 = (bf16[256,3840]{1,0:T(8,128)(2,1)S(1)}, bf16[256,3840]{1,0:T(8,128)(2,1)}, u32[]{:S(2)}, u32[]{:S(2)}) collective-permute-start(bf16[256,3840]{1,0:T(8,128)(2,1)S(1)} %copy-done.14), channel_id=1, source_target_pairs={{0,16},{16,0},{1,17},{17,1},{2,18},{18,2},{3,19},{19,3},{4,20},{20... | collective-permute-start | bytes 5898248 | tf_op jit(solution)/shard_map/ppermute | solution.py:656
  209.4 27.3 %collective-permute-start.52 = (bf16[256,1920]{1,0:T(8,128)(2,1)}, bf16[256,1920]{1,0:T(8,128)(2,1)}, u32[]{:S(2)}, u32[]{:S(2)}) collective-permute-start(bf16[256,1920]{1,0:T(8,128)(2,1)} %get-tuple-element.185), channel_id=1, source_target_pairs={{0,16},{16,0},{1,17},{17,1},{2,18},{18,2},{3,19},{19,3},{4,20},{20... | collective-permute-start | bytes 2949128 | tf_op jit(solution)/shard_map/ppermute | solution.py:656
  209.9 26.7 %collective-permute-start.57 = (bf16[256,1536]{1,0:T(8,128)(2,1)}, bf16[256,1536]{1,0:T(8,128)(2,1)}, u32[]{:S(2)}, u32[]{:S(2)}) collective-permute-start(bf16[256,1536]{1,0:T(8,128)(2,1)} %get-tuple-element.203.acts), channel_id=1, source_target_pairs={{0,16},{16,0},{1,17},{17,1},{2,18},{18,2},{3,19},{19,3},{4,20},{20... | collective-permute-start | bytes 2359304 | tf_op jit(solution)/shard_map/ppermute | solution.py:656
  218.3 28.4 %collective-permute-start.49 = (bf16[4,1,4,48,384]{4,3,2,1,0:T(8,128)(2,1)}, bf16[4,1,4,48,384]{4,3,2,1,0:T(8,128)(2,1)}, u32[]{:S(2)}, u32[]{:S(2)}) collective-permute-start(bf16[4,1,4,48,384]{4,3,2,1,0:T(8,128)(2,1)} %add_convert_fusion.4), channel_id=1, source_target_pairs={{0,2},{1,3},{2,0},{3,1},{4,6},{5,7},{6,4},{7,5},{8,10},{9,11},{10,... | collective-permute-start | bytes 1769480 | tf_op jit(solution)/shard_map/ppermute | solution.py:683
  225.3 30.5 %collective-permute-start.54 = (bf16[1,4,4,48,384]{4,3,2,1,0:T(8,128)(2,1)}, bf16[1,4,4,48,384]{4,3,2,1,0:T(8,128)(2,1)}, u32[]{:S(2)}, u32[]{:S(2)}) collective-permute-start(bf16[1,4,4,48,384]{4,3,2,1,0:T(8,128)(2,1)} %add_convert_fusion.3), channel_id=1, source_target_pairs={{0,8},{4,12},{8,0},{12,4},{16,20},{20,16},{24,28},{28,24},{1,9},{5... | collective-permute-start | bytes 1769480 | tf_op jit(solution)/shard_map/ppermute | solution.py:669
  236.6 45.0 %collective-permute-start.64 = (bf16[256,1536]{1,0:T(8,128)(2,1)}, bf16[256,1536]{1,0:T(8,128)(2,1)}, u32[]{:S(2)}, u32[]{:S(2)}) collective-permute-start(bf16[256,1536]{1,0:T(8,128)(2,1)} %get-tuple-element.204), channel_id=1, source_target_pairs={{0,16},{16,0},{1,17},{17,1},{2,18},{18,2},{3,19},{19,3},{4,20},{20... | collective-permute-start | bytes 2359304 | tf_op jit(solution)/shard_map/ppermute | solution.py:656
  242.4 36.0 %collective-permute-start.58 = (bf16[2,4,4,48,384]{4,3,2,1,0:T(8,128)(2,1)}, bf16[2,4,4,48,384]{4,3,2,1,0:T(8,128)(2,1)}, u32[]{:S(2)}, u32[]{:S(2)}) collective-permute-start(bf16[2,4,4,48,384]{4,3,2,1,0:T(8,128)(2,1)} %get-tuple-element.207), channel_id=1, source_target_pairs={{0,4},{4,0},{8,12},{12,8},{16,24},{20,28},{24,16},{28,20},{1,5},{5... | collective-permute-start | bytes 3538952 | tf_op jit(solution)/shard_map/ppermute | solution.py:669
  248.6 25.5 %collective-permute-start.63 = (bf16[2,1,4,48,384]{4,3,2,1,0:T(8,128)(2,1)}, bf16[2,1,4,48,384]{4,3,2,1,0:T(8,128)(2,1)S(1)}, u32[]{:S(2)}, u32[]{:S(2)}) collective-permute-start(bf16[2,1,4,48,384]{4,3,2,1,0:T(8,128)(2,1)} %add_convert_fusion.10), channel_id=1, source_target_pairs={{0,4},{4,0},{8,12},{12,8},{16,24},{20,28},{24,16},{28,20},{1,5},{5... | collective-permute-start | bytes 884744 | tf_op jit(solution)/shard_map/ppermute | solution.py:669
  257.6 37.8 %collective-permute-start.61 = (bf16[2,4,4,48,384]{4,3,2,1,0:T(8,128)(2,1)}, bf16[2,4,4,48,384]{4,3,2,1,0:T(8,128)(2,1)}, u32[]{:S(2)}, u32[]{:S(2)}) collective-permute-start(bf16[2,4,4,48,384]{4,3,2,1,0:T(8,128)(2,1)} %bitcast.35), channel_id=1, source_target_pairs={{0,4},{4,0},{8,12},{12,8},{16,24},{20,28},{24,16},{28,20},{1,5},{5... | collective-permute-start | bytes 3538952 | tf_op jit(solution)/shard_map/ppermute | solution.py:669
  272.9 23.8 %collective-permute-start.70 = (bf16[256,1920]{1,0:T(8,128)(2,1)}, bf16[256,1920]{1,0:T(8,128)(2,1)}, u32[]{:S(2)}, u32[]{:S(2)}) collective-permute-start(bf16[256,1920]{1,0:T(8,128)(2,1)} %get-tuple-element.225), channel_id=1, source_target_pairs={{0,16},{16,0},{1,17},{17,1},{2,18},{18,2},{3,19},{19,3},{4,20},{20... | collective-permute-start | bytes 2949128 | tf_op jit(solution)/shard_map/ppermute | solution.py:656
  286.9 22.9 %collective-permute-start.65 = (bf16[2,4,4,48,384]{4,3,2,1,0:T(8,128)(2,1)}, bf16[2,4,4,48,384]{4,3,2,1,0:T(8,128)(2,1)}, u32[]{:S(2)}, u32[]{:S(2)}) collective-permute-start(bf16[2,4,4,48,384]{4,3,2,1,0:T(8,128)(2,1)} %get-tuple-element.217), channel_id=1, source_target_pairs={{0,4},{4,0},{8,12},{12,8},{16,24},{20,28},{24,16},{28,20},{1,5},{5... | collective-permute-start | bytes 3538952 | tf_op jit(solution)/shard_map/ppermute | solution.py:669
  302.5 36.1 %collective-permute-start.71 = (bf16[2,4,4,48,384]{4,3,2,1,0:T(8,128)(2,1)}, bf16[2,4,4,48,384]{4,3,2,1,0:T(8,128)(2,1)S(1)}, u32[]{:S(2)}, u32[]{:S(2)}) collective-permute-start(bf16[2,4,4,48,384]{4,3,2,1,0:T(8,128)(2,1)} %get-tuple-element.227), channel_id=1, source_target_pairs={{0,4},{4,0},{8,12},{12,8},{16,24},{20,28},{24,16},{28,20},{1,5},{5... | collective-permute-start | bytes 3538952 | tf_op jit(solution)/shard_map/ppermute | solution.py:669
  317.3 30.7 %collective-permute-start.66 = (f32[2,4,768]{2,1,0:T(4,128)S(1)}, f32[2,4,768]{2,1,0:T(4,128)S(1)}, u32[]{:S(2)}, u32[]{:S(2)}) collective-permute-start(f32[2,4,768]{2,1,0:T(4,128)S(1)} %pad_maximum_fusion.22), channel_id=1, source_target_pairs={{0,16},{16,0},{1,17},{17,1},{2,18},{18,2},{3,19},{19,3},{4,20},{20... | collective-permute-start | bytes 73736 | tf_op jit(solution)/shard_map/ppermute | solution.py:656
  334.4 23.3 %collective-permute-start.89 = (bf16[2,12,48,384]{3,2,1,0:T(8,128)(2,1)S(1)}, bf16[2,12,48,384]{3,2,1,0:T(8,128)(2,1)S(1)}, u32[]{:S(2)}, u32[]{:S(2)}) collective-permute-start(bf16[2,12,48,384]{3,2,1,0:T(8,128)(2,1)S(1)} %pad_maximum_fusion.8), channel_id=1, source_target_pairs={{0,4},{4,0},{8,12},{12,8},{16,24},{20,28},{24,16},{28,20},{1,5},{5... | collective-permute-start | bytes 2654216 | tf_op jit(solution)/shard_map/ppermute | solution.py:669
  358.0 28.3 %collective-permute-start.90 = (bf16[4,12,48,384]{3,2,1,0:T(8,128)(2,1)S(1)}, bf16[4,12,48,384]{3,2,1,0:T(8,128)(2,1)}, u32[]{:S(2)}, u32[]{:S(2)}) collective-permute-start(bf16[4,12,48,384]{3,2,1,0:T(8,128)(2,1)S(1)} %pad_maximum_fusion.high_own), channel_id=1, source_target_pairs={{0,16},{1,17},{2,18},{3,19},{4,20},{5,21},{6,22},{7,23},{8,24},{9,... | collective-permute-start | bytes 5308424 | tf_op jit(solution)/shard_map/ppermute | solution.py:1040
  (119 other events, 1308.7 us)
